TPU v7x, 128 devices: a whole 4x4x4 slice. The times are simulated.
128 devices in a mesh: day: 16 (over z, x), blk: 8 (over y, core).
Axes of the slice: x: 4, y: 4, z: 4, core: 2. Of those that a mesh axis runs over, the one named last changes fastest.
Arguments:
- diag_blocks: float32 [32, 2560, 2560], P('day', 'blk'), may hold values from -1 to 3, as said below
- off_blocks: float32 [32, 2560, 2560], P('day', 'blk'), may hold values from -1 to 1
- leakage: float32 [32, 2560], P('day', 'blk'), may hold values from 0.001 to 0.3
- obs_count: int32 [32], P('day'), may hold values from 1 to 1024, 16384 in all
- obs_triangle: int32 [32, 1024], P('day', 'blk'), may hold values from 0 to 5115
- obs_bary: float32 [3, 32, 1024], P(None, 'day', 'blk'), may hold values from 0.05 to 1
- obs_prec: float32 [32, 1024], P('day', 'blk'), may hold values from 0.3 to 3
- obs_value: float32 [32, 1024], P('day', 'blk'), may hold values from -6 to 6
- covariates: float32 [64, 32, 1024], P(None, 'day', 'blk'), may hold values from -0.0625 to 0.0625
- triangles: int32 [3, 5116], replicated, may hold values from 0 to 2559
- prior_prec: float32 [64], replicated, may hold values from 0.5 to 2
- probes: float32 [15, 32, 2560], P(None, 'day', 'blk'), may hold values from -6 to 6
- probes_cov: float32 [15, 64], replicated, may hold values from -6 to 6
Outputs:
- step_field: float32 [16, 32, 2560], P(None, 'day', 'blk')
- step_cov: float32 [16, 64], replicated
Inputs may be any that keep to these rules, and one draw needn't show every extreme that they name: Every block diag_blocks[t] is symmetric, and the whole precision made of diag_blocks and off_blocks is positive definite. Slots 0 to obs_count[t] - 1 of day t hold observations, the others are empty; the counts sum to 16384.
All inputs are finite; a program needn't handle non-finite values. No bound on the sum of `obs_count` on one device may be relied on, other than what follows from the above.
Results may differ from a plain program's by a relative error of at most 0.0002.
Values sent between devices are 32-bit elements; how exact they have to be, the bound alone decides.
No kernel may reach another device: no remote copies, remote signals or barrier semaphores. Data moves between devices by JAX's collectives and lax.ppermute only.
A program may use at most 192 MiB of HBM per device.

v0:
```python
import jax
import jax.numpy as jnp
from jax import lax
from jax.experimental import pallas as pl
from jax.experimental.pallas import tpu as pltpu
from jax.sharding import Mesh
from jax.sharding import PartitionSpec as P

DAY = ("day_0", "day_1")
BLK = ("blk_0", "blk_1")
F32 = jnp.float32
BF16 = jnp.bfloat16
NT = (((1,), (1,)), ((), ()))
NN = (((1,), (0,)), ((), ()))


def shift(value, axis, distance):
    size = lax.axis_size(axis)
    return lax.ppermute(value, axis, [(i, (i + distance) % size) for i in range(size)])


def swapped(value):
    return lax.ppermute(value, "blk_1", [(0, 1), (1, 0)])


def ring_gather(value, axis):
    return [value] + [shift(value, axis, k) for k in (1, 2, 3)]


def ring_sum(relative):
    return (relative[0] + relative[2]) + (relative[1] + relative[3])


def scattered_pieces(kept, sent):
    row = lax.axis_index("blk_0")
    half = kept + swapped(sent)
    pieces = [lax.dynamic_index_in_dim(half, (row + k) % 4, 0, False) for k in range(4)]
    return [pieces[0]] + [shift(pieces[k], "blk_0", k) for k in (1, 2, 3)]


def gather_nodes(message):
    column = jnp.stack(ring_gather(message, "blk_0"))
    return column, swapped(column)


def chain_coefficients(decay, dominant):
    group, place = lax.axis_index("day_0"), lax.axis_index("day_1")
    me = 4 * group + place
    decays = decay.reshape(32, 320)
    dominants = dominant.reshape(32, 320)
    gain = [None] * 33
    gain[32] = jnp.zeros_like(decays[0])
    follow = jnp.concatenate([decays[1:], jnp.zeros((1, 320), jnp.float32)])
    for day in range(31, -1, -1):
        gain[day] = 1.0 / dominants[day] + follow[day] * follow[day] * gain[day + 1]
    gains = jnp.stack(gain)
    follows = jnp.concatenate([decays, jnp.zeros((1, 320), jnp.float32)])
    days = lax.dynamic_slice_in_dim(gains, 2 * me, 3, 0)
    decs = lax.dynamic_slice_in_dim(follows, 2 * me, 3, 0)
    step = (follows[1::2] * follows[2::2]).reshape(4, 4, 320)
    mine = lax.dynamic_index_in_dim(step, group, 0, False)
    one, zero = jnp.ones((320,), jnp.float32), jnp.zeros((320,), jnp.float32)
    index = jnp.arange(4)[:, None]

    def product(factors, low, high):
        kept = jnp.where((index >= low) & (index < high), factors, 1.0)
        return kept[0] * kept[1] * kept[2] * kept[3]

    whole = jnp.prod(step, axis=1)
    local_f, local_b, total_f, total_b, far = [], [], [], [], []
    for k in range(4):
        source = (place - k) % 4
        total_f.append(product(mine, source + 1, 4))
        total_b.append(product(mine, 0, source))
        if k:
            local_f.append(jnp.where(source < place, product(mine, source + 1, place), zero))
            local_b.append(jnp.where(source > place, product(mine, place + 1, source), zero))
            origin = (group - k) % 4
            low, high = jnp.minimum(origin, group) + 1, jnp.maximum(origin, group)
            far.append(product(whole, low, high))
    rows = [days[0], days[1], days[2], decs[0], decs[1], decs[2]]
    rows += local_f + local_b + total_f + total_b + far
    rows += [product(mine, 0, place), product(mine, place + 1, 4)]
    return jnp.stack(rows)


def ring_message(w, co):
    g0, g1, gg, d1, dg = co[0:1], co[1:2], co[2:3], co[4:5], co[5:6]
    ahead = dg * (w[1] + d1 * w[0]) + w[2]
    behind = g0 * w[0] + d1 * (g1 * w[1] + dg * gg * w[2])
    return ahead, behind


def weighted(co, first, values):
    return sum(co[first + k : first + k + 1] * value for k, value in enumerate(values))


def middle_kernel(m0, m1, m2, m3, co, out1, out2, out3, local):
    messages = (m0, m1, m2, m3)
    fs = [m[:, :320] for m in messages]
    bs = [m[:, 320:640] for m in messages]
    pack = ring_sum([m[:, 640:] for m in messages])
    local[0] = weighted(co, 6, fs[1:])
    local[1] = weighted(co, 9, bs[1:])
    local[2] = jnp.zeros((16, 320), F32)
    local[2, :, :128] = pack
    total_f = weighted(co, 12, fs)
    total_b = weighted(co, 16, bs)
    group = lax.axis_index("day_0")
    for k, out in ((1, out1), (2, out2), (3, out3)):
        out[:, :320] = jnp.where(group + k < 4, total_f, total_b)
        out[:, 320:] = pack


def last_kernel(r1, r2, r3, local, w, co, v, message):
    group = lax.axis_index("day_0")
    g0, g1, gg, d1, dg = co[0:1], co[1:2], co[2:3], co[4:5], co[5:6]
    far_f, far_b = jnp.zeros((16, 320), F32), jnp.zeros((16, 320), F32)
    packs = [local[2, :, :128]]
    for k, r in ((1, r1), (2, r2), (3, r3)):
        packs.append(r[:, 320:])
        value = co[19 + k : 20 + k] * r[:, :320]
        far_f = far_f + jnp.where(group >= k, value, 0.0)
        far_b = far_b + jnp.where(group >= k, 0.0, value)
    come_f = local[0] + co[23:24] * far_f
    come_b = local[1] + co[24:25] * far_b
    l0 = w[0] + come_f
    l1 = w[1] + d1 * l0
    u1 = dg * (come_b + gg * w[2])
    u0 = d1 * (g1 * w[1] + u1)
    days = (g0 * l0 + u0, g1 * l1 + u1, gg * (dg * l1 + w[2]) + come_b)
    for day, value in enumerate(days):
        v[day] = value
        message[:, day * 320 : day * 320 + 320] = value
    message[:, 960:] = ring_sum(packs)


def precondition(w, message, co):
    pieces = ring_gather(message, "day_1")
    one = shaped(16, 448)
    *out, local = call(
        middle_kernel, "middle", (one, one, one, shaped(3, 16, 320)), [VMEM_BLOCK] * 5, *pieces, co
    )
    got = [shift(out[k - 1], "day_0", k) for k in (1, 2, 3)]
    return call(
        last_kernel, "last", (shaped(3, 16, 320), shaped(16, 1088)), [VMEM_BLOCK] * 6, *got, local, w, co
    )


def halves(value):
    high = value.astype(BF16)
    return high, (value - high.astype(F32)).astype(BF16)


def stacked_halves(value):
    return jnp.concatenate(halves(value), axis=0)


def matmul(first, second, dims):
    return lax.dot_general(first, second, dims, preferred_element_type=F32)


def times_rows(value, pair):
    n = pair.shape[0] // 2
    out = matmul(stacked_halves(value), pair, NT)
    return (out[:16, :n] + out[16:, :n]) + (out[:16, n:] + out[16:, n:])


def times_matrix(value, pair):
    high, low = halves(value)
    both = jnp.concatenate(
        [jnp.concatenate([high, high], axis=1), jnp.concatenate([low, low], axis=1)], axis=0
    )
    out = matmul(both, pair, NN)
    return out[:16] + out[16:]


VMEM_BLOCK = pl.BlockSpec(memory_space=pltpu.VMEM)
SMEM_BLOCK = pl.BlockSpec(memory_space=pltpu.SMEM)
HBM_BLOCK = pl.BlockSpec(memory_space=pltpu.HBM)


def shaped(*shape):
    return jax.ShapeDtypeStruct(shape, F32)


def call(kernel, name, outs, in_specs, *operands, scratch=(), limit=16):
    return pl.pallas_call(
        kernel,
        out_shape=outs,
        in_specs=in_specs,
        out_specs=jax.tree.map(lambda _: VMEM_BLOCK, outs),
        scratch_shapes=scratch,
        compiler_params=pltpu.CompilerParams(vmem_limit_bytes=limit << 20),
        name=name,
    )(*operands)


CHUNK = 80


def split_kernel(diag, off, diag_pair, off_pair, buffer, sem):
    jobs = [
        (source, target, day, row)
        for source, target in ((off, off_pair), (diag, diag_pair))
        for day in range(2)
        for row in range(0, 320, CHUNK)
    ]

    def fetch(index):
        source, _, day, row = jobs[index]
        slot = index % 3
        return pltpu.make_async_copy(source.at[day, pl.ds(row, CHUNK)], buffer.at[slot], sem.at[slot])

    fetch(0).start()
    fetch(1).start()
    for index, (_, target, day, row) in enumerate(jobs):
        if index + 2 < len(jobs):
            fetch(index + 2).start()
        fetch(index).wait()
        high, low = halves(buffer[index % 3])
        target[day, pl.ds(row, CHUNK)] = high
        target[day, pl.ds(320 + row, CHUNK)] = low


def split_blocks(diag, off):
    pair = pltpu.VMEM((2, 640, 2560), BF16)
    return call(
        split_kernel,
        "split_blocks",
        (pair, pair),
        [HBM_BLOCK, HBM_BLOCK],
        diag,
        off,
        scratch=[pltpu.VMEM((3, CHUNK, 2560), F32), pltpu.SemaphoreType.DMA((3,))],
    )


def behind_kernel(off_pair, own, out):
    for day in range(2):
        out[day] = times_matrix(own[day], off_pair[day])


def behind_terms(off_pair, own):
    return call(behind_kernel, "behind_terms", shaped(2, 16, 2560), [VMEM_BLOCK] * 2, off_pair, own)


def rows_into(diag_pair, off_pair, whole, out):
    for day in range(2):
        out[day] = times_rows(whole[day], diag_pair[day]) + times_rows(whole[day + 1], off_pair[day])


def lanes(*values):
    lane = lax.broadcasted_iota(jnp.int32, (16, 64), 1)
    out = jnp.zeros((16, 64), F32)
    for index, value in enumerate(values):
        out = jnp.where(lane == index, value, out)
    return out


def first_rows_kernel(diag_pair, off_pair, whole, bx, v1, out, dots):
    rows_into(diag_pair, off_pair, whole, out)
    dots[...] = lanes(sum(row_sum(bx[day] * v1[day]) for day in range(2)))


def first_rows(*operands):
    return call(
        first_rows_kernel, "first_rows", (shaped(2, 16, 320), shaped(16, 64)), [VMEM_BLOCK] * 5, *operands
    )


def second_rows_kernel(diag_pair, off_pair, whole, bx, v1, v2, w1, scalars, out, dots, r1, z1):
    rows_into(diag_pair, off_pair, whole, out)
    step0 = scalars[:, 0:1]
    norm = cross = jnp.zeros((16, 1), F32)
    for day in range(3):
        z = v1[day] - step0 * v2[day]
        r = (bx[day] if day < 2 else 0.0) - step0 * w1[day]
        z1[day] = z
        r1[day] = r
        norm = norm + row_sum(r * z)
        cross = cross + row_sum(z * w1[day])
    dots[...] = lanes(norm, 0.0, cross)


def second_rows(*operands):
    own = shaped(3, 16, 320)
    return call(
        second_rows_kernel,
        "second_rows",
        (shaped(2, 16, 320), shaped(16, 64), own, own),
        [VMEM_BLOCK] * 8,
        *operands,
    )


def start_kernel(p0, p1, p2, p3, probes, grad_cov, co, bx, w, message):
    grad = ring_sum([p0[...], p1[...], p2[...], p3[...]])
    for day in range(2):
        bx[day, 0:1] = grad[day : day + 1]
        bx[day, 1:16] = probes[:, day, :]
        w[day] = bx[day]
    w[2] = jnp.zeros((16, 320), F32)
    ahead, behind = ring_message(w, co)
    message[:, :320] = ahead
    message[:, 320:640] = behind
    message[:, 640:] = jnp.zeros((16, 128), F32)
    message[0:1, 640:704] = grad_cov[...]


def start_stage(*operands):
    return call(
        start_kernel,
        "start_stage",
        (shaped(2, 16, 320), shaped(3, 16, 320), shaped(16, 768)),
        [VMEM_BLOCK] * 7,
        *operands,
    )


def image_kernel(p0, p1, p2, p3, rows, vector, cov_terms, dots, co, w, message):
    pieces = (p0, p1, p2, p3)
    total = jnp.zeros((16, 1), F32)
    for day in range(3):
        value = ring_sum([p[day] for p in pieces])
        if day < 2:
            value = value + rows[day]
        w[day] = value
        total = total + row_sum(vector[day] * value)
    ahead, behind = ring_message(w, co)
    message[:, :320] = ahead
    message[:, 320:640] = behind
    message[:, 640:704] = cov_terms[...]
    message[:, 704:] = dots[...] + lanes(0.0, total)


def image_stage(*operands):
    return call(
        image_kernel,
        "image_stage",
        (shaped(3, 16, 320), shaped(16, 768)),
        [VMEM_BLOCK] * 9,
        *operands,
    )


def assemble(mine, other, whole):
    row, core = lax.axis_index("blk_0"), lax.axis_index("blk_1")
    packs = []
    for k in range(4):
        at = pl.multiple_of(lax.rem(row + (4 - k), 4) * 640, 128)
        for day in range(3):
            a = mine[k, :, day * 320 : day * 320 + 320]
            b = other[k, :, day * 320 : day * 320 + 320]
            first = jnp.where(core == 0, a, b)
            second = jnp.where(core == 0, b, a)
            whole[day, :, pl.ds(at, 640)] = jnp.concatenate([first, second], axis=1)
        packs.append(mine[k, :, 960:1088] + other[k, :, 960:1088])
    return (packs[0] + packs[2]) + (packs[1] + packs[3])


def scatter_parts(obs0, obs1, behind0, behind1, kept, sent):
    core = lax.axis_index("blk_1")
    last = lax.axis_index("day_0") * 4 + lax.axis_index("day_1") == 15
    days = (obs0, obs1 + behind0, jnp.where(last, 0.0, behind1))
    for day, part in enumerate(days):
        for row in range(4):
            first = part[:, row * 640 : row * 640 + 320]
            second = part[:, row * 640 + 320 : row * 640 + 640]
            kept[row, day] = jnp.where(core == 0, first, second)
            sent[row, day] = jnp.where(core == 0, second, first)


def observe(whole, cov, spread, covariates, weight):
    result = []
    for day in range(2):
        out = matmul(stacked_halves(whole[day]), spread[day], NN)
        out = (out[:16, :128] + out[16:, :128]) + (out[:16, 128:] + out[16:, 128:])
        predictor = out + times_matrix(cov, stacked_halves(covariates[day]))
        result.append((predictor, weight[day : day + 1] * predictor))
    return result


def spread_out(value, pair):
    high, low = halves(value)
    both = jnp.concatenate(
        [jnp.concatenate([high, high], axis=1), jnp.concatenate([low, low], axis=1)], axis=0
    )
    out = matmul(both, pair, NT)
    return out[:16] + out[16:]


def observe_back(observed, behind, spread, covariates, kept, sent, cov_terms):
    weights = [pair[1] for pair in observed]
    obs = [spread_out(weights[day], spread[day]) for day in range(2)]
    scatter_parts(obs[0], obs[1], behind[0], behind[1], kept, sent)
    cov_terms[...] = sum(times_rows(weights[day], stacked_halves(covariates[day])) for day in range(2))


def row_sum(value):
    return jnp.sum(value, axis=1, keepdims=True)


PARTS = (shaped(4, 3, 16, 320), shaped(4, 3, 16, 320), shaped(16, 64))


def first_kernel(mine, other, probes_cov, spread, covariates, weight, behind, kept, sent, cov_terms, whole, cov):
    pack = assemble(mine, other, whole)
    cov[...] = jnp.where(
        lax.broadcasted_iota(jnp.int32, (16, 64), 0) == 0, pack[:, :64], probes_cov[...]
    )
    observed = observe(whole, cov[...], spread, covariates, weight)
    observe_back(observed, behind, spread, covariates, kept, sent, cov_terms)


def first_stage(mine, other, probes_cov, spread, covariates, weight, behind):
    return call(
        first_kernel,
        "first_stage",
        PARTS + (shaped(3, 16, 2560), shaped(16, 64)),
        [VMEM_BLOCK] * 7,
        mine, other, probes_cov, spread, covariates, weight, behind,
    )


def second_kernel(
    mine, other, whole1, c0, prior, spread, covariates, weight, behind1, behind2,
    kept, sent, cov_terms, whole2, whole, cov, hcov, scalars, behind,
):
    pack = assemble(mine, other, whole2)
    hcov1 = pack[:, :64] + prior[...] * c0[...]
    norm0 = pack[:, 64:65] + row_sum(c0[...] * c0[...])
    curve0 = pack[:, 65:66] + row_sum(c0[...] * hcov1)
    step0 = norm0 / curve0
    for day in range(3):
        whole[day] = whole1[day] - step0 * whole2[day]
    for day in range(2):
        behind[day] = behind1[day] - step0 * behind2[day]
    cov[...] = c0[...] - step0 * hcov1
    hcov[...] = hcov1
    lane = lax.broadcasted_iota(jnp.int32, (16, 128), 1)
    scalars[...] = jnp.where(lane == 0, step0, jnp.where(lane == 1, norm0, curve0))
    observed = observe(whole, cov[...], spread, covariates, weight)
    observe_back(observed, behind, spread, covariates, kept, sent, cov_terms)


def second_stage(mine, other, whole1, c0, prior, spread, covariates, weight, behind1, behind2):
    whole = shaped(3, 16, 2560)
    return call(
        second_kernel,
        "second_stage",
        PARTS + (whole, whole, shaped(16, 64), shaped(16, 64), shaped(16, 128)),
        [VMEM_BLOCK] * 10,
        mine, other, whole1, c0, prior, spread, covariates, weight, behind1, behind2,
        scratch=[pltpu.VMEM((2, 16, 2560), F32)],
    )


def third_kernel(
    mine, other, whole2, z1whole, scalars, c0, z1cov, hcov1, prior, spread, covariates, weight,
    diag_pair, off_pair, r1, z1, w1, w2, v1, v2, v3,
    sums, z2, p1, scalars_out, covs, whole,
):
    pack = assemble(mine, other, whole)
    norm0, curve0 = scalars[:, 1:2], scalars[:, 2:3]
    hcov2 = pack[:, :64] + prior[...] * z1cov[...]
    norm1 = pack[:, 64:65] + row_sum(z1cov[...] * z1cov[...])
    beta1 = norm1 / norm0
    curve1 = (
        pack[:, 65:66]
        + row_sum(z1cov[...] * hcov2)
        + 2.0 * beta1 * (pack[:, 66:67] + row_sum(z1cov[...] * hcov1[...]))
        + beta1 * beta1 * curve0
    )
    step1 = norm1 / curve1
    hp1cov = hcov2 + beta1 * hcov1[...]
    r2cov = z1cov[...] - step1 * hp1cov
    covs[0] = r2cov
    covs[1] = z1cov[...] + beta1 * c0[...]
    own_norm = jnp.zeros((16, 1), F32)
    cross = jnp.zeros((16, 1), F32)
    for day in range(3):
        hp1 = w2[day] + beta1 * w1[day]
        r2 = r1[day] - step1 * hp1
        z2day = z1[day] - step1 * (v3[day] + beta1 * v2[day])
        own_norm = own_norm + row_sum(r2 * z2day)
        cross = cross + row_sum(z2day * hp1)
        if day < 2:
            z2[day] = z2day
            p1[day] = z1[day] + beta1 * v1[day]
        whole[day] = z1whole[day] - step1 * (whole[day] + beta1 * whole2[day])
    observed = observe(whole, r2cov, spread, covariates, weight)
    quadratic = sum(row_sum(predictor * weighted) for predictor, weighted in observed)
    for day in range(2):
        rows = times_rows(whole[day], diag_pair[day]) + 2.0 * times_rows(whole[day + 1], off_pair[day])
        quadratic = quadratic + row_sum(z2[day] * rows)
    lane = lax.broadcasted_iota(jnp.int32, (16, 128), 1)
    sub = lax.broadcasted_iota(jnp.int32, (16, 128), 0)
    line = jnp.zeros((16, 128), F32)
    for index, value in enumerate((own_norm, quadratic, cross)):
        line = jnp.where(lane == sub + 16 * index, value, line)
    sums[...] = jnp.broadcast_to(jnp.sum(line, axis=0, keepdims=True), (128, 128))
    norm2cov = row_sum(r2cov * r2cov)
    quadcov = row_sum(r2cov * prior[...] * r2cov)
    crosscov = row_sum(r2cov * hp1cov)
    values = (scalars[:, 0:1], step1, norm1, curve1, norm2cov, quadcov, crosscov)
    out = jnp.zeros((16, 128), F32)
    for index, value in enumerate(values):
        out = jnp.where(lane == index, value, out)
    scalars_out[...] = out


def third_stage(*operands):
    own = shaped(2, 16, 320)
    return call(
        third_kernel,
        "third_stage",
        (shaped(128, 128), own, own, shaped(16, 128), shaped(2, 16, 64)),
        [VMEM_BLOCK] * len(operands),
        *operands,
        scratch=[pltpu.VMEM((3, 16, 2560), F32)],
    )


def final_kernel(sums, scalars, v1, p1, z2, c0, covs, field, cov):
    step0, step1, norm1, curve1, norm2cov, quadcov, crosscov = (
        scalars[:, i : i + 1] for i in range(7)
    )
    lane = lax.broadcasted_iota(jnp.int32, (16, 128), 1)
    sub = lax.broadcasted_iota(jnp.int32, (16, 128), 0)
    line = jnp.sum(sums[...], axis=0, keepdims=True)
    own_norm, quadratic, cross = (
        row_sum(jnp.where(lane == sub + 16 * index, line, 0.0)) for index in range(3)
    )
    norm2 = own_norm + norm2cov
    beta2 = norm2 / norm1
    curve2 = (
        quadratic + quadcov + 2.0 * beta2 * (cross + crosscov) + beta2 * beta2 * curve1
    )
    step2 = norm2 / curve2
    middle = step1 + step2 * beta2
    for day in range(2):
        field[:, day, :] = step0 * v1[day] + middle * p1[day] + step2 * z2[day]
    cov[...] = step0 * c0[...] + middle * covs[1] + step2 * covs[0]


def final_stage(*operands):
    return call(
        final_kernel,
        "final_stage",
        (shaped(16, 2, 320), shaped(16, 64)),
        [VMEM_BLOCK] * len(operands),
        *operands,
    )


def setup_kernel(count, vertices, bary, prec, value, covariates, spread, weight, kept, sent, grad_cov):
    core = lax.axis_index("blk_1")
    slot_start = (lax.axis_index("blk_0") * 2 + core) * 128
    cov_sum = jnp.zeros((1, 64), F32)
    for day in range(2):
        shares = [bary[k, day : day + 1, :] for k in range(3)]
        total = shares[0] + shares[1] + shares[2]
        nodes = lax.broadcasted_iota(jnp.int32, (2560, 128), 0)
        dense = jnp.zeros((2560, 128), F32)
        for k in range(3):
            dense = dense + jnp.where(nodes == vertices[k, day : day + 1, :], shares[k] / total, 0.0)
        high, low = halves(dense)
        spread[day, :, :128] = high
        spread[day, :, 128:] = low
        slot = lax.broadcasted_iota(jnp.int32, (1, 128), 1) + slot_start
        slot_weight = jnp.where(slot < count[day], prec[day : day + 1], 0.0)
        weight[day : day + 1] = slot_weight
        weighted_value = jnp.broadcast_to(slot_weight * value[day : day + 1], (16, 128))
        grad = spread_out(weighted_value, spread[day])[:1]
        for row in range(4):
            first = grad[:, row * 640 : row * 640 + 320]
            second = grad[:, row * 640 + 320 : row * 640 + 640]
            kept[row, day : day + 1] = jnp.where(core == 0, first, second)
            sent[row, day : day + 1] = jnp.where(core == 0, second, first)
        cov_sum = cov_sum + times_rows(weighted_value, stacked_halves(covariates[day]))[:1]
    grad_cov[...] = cov_sum


def setup_stage(*operands):
    return call(
        setup_kernel,
        "setup_stage",
        (
            pltpu.VMEM((2, 2560, 256), BF16), shaped(2, 128), shaped(4, 2, 320), shaped(4, 2, 320),
            shaped(1, 64),
        ),
        [SMEM_BLOCK] + [VMEM_BLOCK] * (len(operands) - 1),
        *operands,
    )


def on_device(
    diag_blocks,
    off_blocks,
    leakage,
    obs_count,
    obs_triangle,
    obs_bary,
    obs_prec,
    obs_value,
    covariates,
    triangles,
    prior_prec,
    probes,
    probes_cov,
):
    row_start = lax.axis_index(BLK) * 320
    square = lax.dynamic_slice_in_dim(diag_blocks, row_start, 320, 2)
    rows = lax.broadcasted_iota(jnp.int32, (2, 320, 320), 1)
    columns = lax.broadcasted_iota(jnp.int32, (2, 320, 320), 2)
    dominant = jnp.sum(jnp.where(rows == columns, square, 0.0), axis=1)
    both = jnp.concatenate([1.0 - leakage, dominant])
    every = lax.all_to_all(jnp.broadcast_to(both, (16, 4, 320)), DAY, 0, 0, tiled=True)
    co = chain_coefficients(every[:, :2], every[:, 2:])

    vertices = triangles[:, obs_triangle]
    covs = jnp.moveaxis(covariates, 1, 0)
    spread, weight, kept, sent, grad_cov = setup_stage(
        obs_count, vertices, obs_bary, obs_prec, obs_value, covs
    )
    diag_pair, off_pair = split_blocks(diag_blocks, off_blocks)
    bx, w0, message = start_stage(*scattered_pieces(kept, sent), probes, grad_cov, co)
    prior = prior_prec[None]
    padded_cov = jnp.pad(probes_cov, ((1, 0), (0, 0)))

    v1, message = precondition(w0, message, co)
    behind1 = behind_terms(off_pair, v1)
    kept, sent, cov1, whole1, c0 = first_stage(
        *gather_nodes(message), padded_cov, spread, covs, weight, behind1
    )
    image, dots = first_rows(diag_pair, off_pair, whole1, bx, v1)
    w1, message = image_stage(*scattered_pieces(kept, sent), image, v1, cov1, dots, co)

    v2, message = precondition(w1, message, co)
    behind2 = behind_terms(off_pair, v2)
    kept, sent, cov2, whole2, z1whole, z1cov, hcov1, scalars = second_stage(
        *gather_nodes(message), whole1, c0, prior, spread, covs, weight, behind1, behind2
    )
    image, dots, r1, z1 = second_rows(diag_pair, off_pair, z1whole, bx, v1, v2, w1, scalars)
    w2, message = image_stage(*scattered_pieces(kept, sent), image, z1, cov2, dots, co)

    v3, message = precondition(w2, message, co)
    sums, z2, p1, scalars, covs2 = third_stage(
        *gather_nodes(message), whole2, z1whole, scalars, c0, z1cov, hcov1, prior, spread, covs, weight,
        diag_pair, off_pair, r1, z1, w1, w2, v1, v2, v3,
    )
    sums = lax.all_to_all(sums, DAY + BLK, 0, 0, tiled=True)
    return final_stage(sums, scalars, v1, p1, z2, c0, covs2)


def solution(mesh):
    split = Mesh(mesh.devices.reshape(4, 4, 4, 2), ("day_0", "day_1", "blk_0", "blk_1"))
    in_specs = (
        P(DAY, BLK, None),
        P(DAY, BLK, None),
        P(DAY, BLK),
        P(DAY),
        P(DAY, BLK),
        P(None, DAY, BLK),
        P(DAY, BLK),
        P(DAY, BLK),
        P(None, DAY, BLK),
        P(),
        P(),
        P(None, DAY, BLK),
        P(),
    )
    out_specs = (P(None, DAY, BLK), P())
    return jax.shard_map(
        on_device, mesh=split, in_specs=in_specs, out_specs=out_specs, check_vma=False
    )
```

profile of v0, /device:TPU:1, one launch (start us, length us, event | category | flops | bytes accessed | tf_op | source)
XLA Modules:
  0.0 163.5 jit_solution(13292790883785162655)
XLA Ops:
  3.5 8.4 %all-to-all-start = ((f32[16,4,320]{2,1,0:T(4,128)}), f32[16,4,320]{2,1,0:T(4,128)S(1)}, u32[]{:S(2)}, u32[]{:S(2)}) async-start(f32[16,4,320]{2,1,0:T(4,128)} %broadcast_in_dim.137), calls=%async_computation | async-start | bytes 196608 | tf_op jit(solution)/shard_map/all_to_all | solution.py:619
  13.5 1.7 %copy.18 = s32[3,5116]{0,1:T(8,128)S(1)} copy(s32[3,5116]{1,0:T(4,128)} %param.22) | data formatting | bytes 122784 | tf_op args[9]
  18.6 2.4 %setup_stage.1 = (bf16[2,2560,256]{2,1,0:T(8,128)(2,1)S(1)}, f32[2,128]{1,0:T(2,128)S(1)}, f32[4,2,320]{2,1,0:T(2,128)S(1)}, f32[4,2,320]{2,1,0:T(2,128)S(1)}, f32[1,64]{1,0:T(1,128)S(1)}) custom-call(s32[2]{0:T(128)S(1)} %copy-done.7, s32[3,2,128]{2,1,0:T(2,128)S(1)} %bitcast.74, f32[3,2,128]{2,1,0:T(2,128)S(1)} %copy-done.3, f32[2,128]{1,0:T(2,128)S(1)} %copy-done.5, ...), custom_call_target="tpu_custom_call" | custom-call | tf_op jit(solution)/shard_map/setup_stage/pallas_call | solution.py:188
  22.9 2.8 %collective-permute-start.3 = (f32[2,320]{1,0:T(2,128)S(1)}, f32[2,320]{1,0:T(2,128)S(1)}, u32[]{:S(2)}, u32[]{:S(2)}) collective-permute-start(f32[2,320]{1,0:T(2,128)S(1)} %get-tuple-element.172), channel_id=1, source_target_pairs={{0,6},{2,0},{4,2},{6,4},{1,7},{3,1},{5,3},{7,5},{8,14},{10,8},{12,... | collective-permute-start | bytes 7688 | tf_op jit(solution)/shard_map/ppermute | solution.py:19
  27.9 1.7 %collective-permute-done.2.p2 = f32[2,320]{1,0:T(2,128)S(1)} collective-permute-done((f32[2,320]{1,0:T(2,128)S(1)}, f32[2,320]{1,0:T(2,128)S(1)}, u32[]{:S(2)}, u32[]{:S(2)}) %collective-permute-start.2) | collective-permute-done | bytes 2592 | tf_op jit(solution)/shard_map/ppermute | solution.py:19
  30.6 2.9 %collective-permute-start.6 = (f32[16,768]{1,0:T(8,128)S(1)}, f32[16,768]{1,0:T(8,128)S(1)}, u32[]{:S(2)}, u32[]{:S(2)}) collective-permute-start(f32[16,768]{1,0:T(8,128)S(1)} %get-tuple-element.61.m0), channel_id=1, source_target_pairs={{0,24},{8,0},{16,8},{24,16},{1,25},{9,1},{17,9},{25,17},{2,26},{10... | collective-permute-start | bytes 147464 | tf_op jit(solution)/shard_map/ppermute | solution.py:19
  34.7 3.3 %collective-permute-done.5.m2 = f32[16,768]{1,0:T(8,128)S(1)} collective-permute-done((f32[16,768]{1,0:T(8,128)S(1)}, f32[16,768]{1,0:T(8,128)S(1)}, u32[]{:S(2)}, u32[]{:S(2)}) %collective-permute-start.5) | collective-permute-done | bytes 49184 | tf_op jit(solution)/shard_map/ppermute | solution.py:19
  39.8 2.4 %collective-permute-start.8 = (f32[16,448]{1,0:T(8,128)S(1)}, f32[16,448]{1,0:T(8,128)S(1)}, u32[]{:S(2)}, u32[]{:S(2)}) collective-permute-start(f32[16,448]{1,0:T(8,128)S(1)} %get-tuple-element.63), channel_id=1, source_target_pairs={{0,64},{32,96},{64,0},{96,32},{1,65},{33,97},{65,1},{97,33},{2,66}... | collective-permute-start | bytes 86024 | tf_op jit(solution)/shard_map/ppermute | solution.py:19
  48.7 1.8 %collective-permute-done.11 = f32[16,1088]{1,0:T(8,128)S(1)} collective-permute-done((f32[16,1088]{1,0:T(8,128)S(1)}, f32[16,1088]{1,0:T(8,128)S(1)}, u32[]{:S(2)}, u32[]{:S(2)}) %collective-permute-start.11) | collective-permute-done | bytes 69664 | tf_op jit(solution)/shard_map/ppermute | solution.py:19
  51.4 6.7 %collective-permute-start.13 = (f32[4,16,1088]{2,1,0:T(8,128)S(1)}, f32[4,16,1088]{2,1,0:T(8,128)S(1)}, u32[]{:S(2)}, u32[]{:S(2)}) collective-permute-start(f32[4,16,1088]{2,1,0:T(8,128)S(1)} %pad_maximum_fusion.mine), channel_id=1, source_target_pairs={{0,1},{1,0},{2,3},{3,2},{4,5},{5,4},{6,7},{7,6},{8,9},{9,8},{10,11... | collective-permute-start | bytes 835592 | tf_op jit(solution)/shard_map/ppermute | solution.py:23
  58.1 2.9 %copy-done = f32[2,320,2560]{2,1,0:T(8,128)S(1)} copy-done((f32[2,320,2560]{2,1,0:T(8,128)S(1)}, f32[2,320,2560]{2,1,0:T(8,128)}, u32[]{:S(2)}) %copy-start) | copy-done | bytes 6553624
  61.0 2.9 %copy-done.1 = f32[2,320,2560]{2,1,0:T(8,128)S(1)} copy-done((f32[2,320,2560]{2,1,0:T(8,128)S(1)}, f32[2,320,2560]{2,1,0:T(8,128)}, u32[]{:S(2)}) %copy-start.1) | copy-done | bytes 6553624
  63.8 3.4 %split_blocks.1 = (bf16[2,640,2560]{2,1,0:T(8,128)(2,1)S(1)}, bf16[2,640,2560]{2,1,0:T(8,128)(2,1)S(1)}) custom-call(f32[2,320,2560]{2,1,0:T(8,128)S(1)} %copy-done, f32[2,320,2560]{2,1,0:T(8,128)S(1)} %copy-done.1), custom_call_target="tpu_custom_call" | custom-call | tf_op jit(solution)/shard_map/split_blocks/pallas_call | solution.py:188
  68.4 1.6 %first_stage.1 = (f32[4,3,16,320]{3,2,1,0:T(8,128)S(1)}, f32[4,3,16,320]{3,2,1,0:T(8,128)S(1)}, f32[16,64]{1,0:T(8,128)S(1)}, f32[3,16,2560]{2,1,0:T(8,128)S(1)}, f32[16,64]{1,0:T(8,128)S(1)}) custom-call(f32[4,16,1088]{2,1,0:T(8,128)S(1)} %pad_maximum_fusion.mine, f32[4,16,1088]{2,1,0:T(8,128)S(1)} %collective-permute-done.13.other, ...), custom_call_target="tpu_custom_call" | custom-call | tf_op jit(solution)/shard_map/first_stage/pallas_call | solution.py:188
  70.1 1.6 collective-permute-done.14
  73.9 3.9 %first_rows.1 = (f32[2,16,320]{2,1,0:T(8,128)S(1)}, f32[16,64]{1,0:T(8,128)S(1)}) custom-call(bf16[2,640,2560]{2,1,0:T(8,128)(2,1)S(1)} %get-tuple-element.74.diag_pair, bf16[2,640,2560]{2,1,0:T(8,128)(2,1)S(1)} %get-tuple-element.70.off_pair, f32[3,16,2560]{2,1,0:T(8,128)S(1)} %get-tuple-element.75.whole.whole1, f32[2,16,320]{2,1,0:T(8,128)S(1)} %get-tuple-element.76.bx, ...), custom_call_target="tpu_custom_call" | custom-call | tf_op jit(solution)/shard_map/first_rows/pallas_call | solution.py:188
  78.0 2.2 %collective-permute-done.15.p1 = f32[3,16,320]{2,1,0:T(8,128)S(1)} collective-permute-done((f32[3,16,320]{2,1,0:T(8,128)S(1)}, f32[3,16,320]{2,1,0:T(8,128)S(1)}, u32[]{:S(2)}, u32[]{:S(2)}) %collective-permute-start.15) | collective-permute-done | bytes 61472 | tf_op jit(solution)/shard_map/ppermute | solution.py:19
  83.3 1.7 %collective-permute-done.19.m2 = f32[16,768]{1,0:T(8,128)S(1)} collective-permute-done((f32[16,768]{1,0:T(8,128)S(1)}, f32[16,768]{1,0:T(8,128)S(1)}, u32[]{:S(2)}, u32[]{:S(2)}) %collective-permute-start.19) | collective-permute-done | bytes 49184 | tf_op jit(solution)/shard_map/ppermute | solution.py:19
  86.0 3.5 %collective-permute-start.22 = (f32[16,448]{1,0:T(8,128)S(1)}, f32[16,448]{1,0:T(8,128)S(1)}, u32[]{:S(2)}, u32[]{:S(2)}) collective-permute-start(f32[16,448]{1,0:T(8,128)S(1)} %get-tuple-element.82), channel_id=1, source_target_pairs={{0,64},{32,96},{64,0},{96,32},{1,65},{33,97},{65,1},{97,33},{2,66}... | collective-permute-start | bytes 86024 | tf_op jit(solution)/shard_map/ppermute | solution.py:19
  94.2 1.8 %collective-permute-done.26 = f32[16,1088]{1,0:T(8,128)S(1)} collective-permute-done((f32[16,1088]{1,0:T(8,128)S(1)}, f32[16,1088]{1,0:T(8,128)S(1)}, u32[]{:S(2)}, u32[]{:S(2)}) %collective-permute-start.26) | collective-permute-done | bytes 69664 | tf_op jit(solution)/shard_map/ppermute | solution.py:19
  96.0 1.6 collective-permute-done.25
  98.4 6.3 %collective-permute-start.27 = (f32[4,16,1088]{2,1,0:T(8,128)S(1)}, f32[4,16,1088]{2,1,0:T(8,128)S(1)}, u32[]{:S(2)}, u32[]{:S(2)}) collective-permute-start(f32[4,16,1088]{2,1,0:T(8,128)S(1)} %pad_maximum_fusion.1.mine), channel_id=1, source_target_pairs={{0,1},{1,0},{2,3},{3,2},{4,5},{5,4},{6,7},{7,6},{8,9},{9,8},{10,11... | collective-permute-start | bytes 835592 | tf_op jit(solution)/shard_map/ppermute | solution.py:23
  105.9 1.9 %second_stage.1 = (f32[4,3,16,320]{3,2,1,0:T(8,128)S(1)}, f32[4,3,16,320]{3,2,1,0:T(8,128)S(1)}, f32[16,64]{1,0:T(8,128)S(1)}, f32[3,16,2560]{2,1,0:T(8,128)S(1)...) custom-call(f32[4,16,1088]{2,1,0:T(8,128)S(1)} %pad_maximum_fusion.1.mine, ...), custom_call_target="tpu_custom_call" | custom-call | tf_op jit(solution)/shard_map/second_stage/pallas_call | solution.py:188
  111.3 3.9 %second_rows.1 = (f32[2,16,320]{2,1,0:T(8,128)S(1)}, f32[16,64]{1,0:T(8,128)S(1)}, f32[3,16,320]{2,1,0:T(8,128)S(1)}, f32[3,16,320]{2,1,0:T(8,128)S(1)}) custom-call(bf16[2,640,2560]{2,1,0:T(8,128)(2,1)S(1)} %get-tuple-element.74.diag_pair, bf16[2,640,2560]{2,1,0:T(8,128)(2,1)S(1)} %get-tuple-element.70.off_pair, ...), custom_call_target="tpu_custom_call" | custom-call | tf_op jit(solution)/shard_map/second_rows/pallas_call | solution.py:188
  115.4 1.7 %collective-permute-done.29.p1 = f32[3,16,320]{2,1,0:T(8,128)S(1)} collective-permute-done((f32[3,16,320]{2,1,0:T(8,128)S(1)}, f32[3,16,320]{2,1,0:T(8,128)S(1)}, u32[]{:S(2)}, u32[]{:S(2)}) %collective-permute-start.29) | collective-permute-done | bytes 61472 | tf_op jit(solution)/shard_map/ppermute | solution.py:19
  117.3 1.5 collective-permute-start.34
  120.2 3.0 %collective-permute-done.33.m2 = f32[16,768]{1,0:T(8,128)S(1)} collective-permute-done((f32[16,768]{1,0:T(8,128)S(1)}, f32[16,768]{1,0:T(8,128)S(1)}, u32[]{:S(2)}, u32[]{:S(2)}) %collective-permute-start.33) | collective-permute-done | bytes 49184 | tf_op jit(solution)/shard_map/ppermute | solution.py:19
  123.9 2.1 %collective-permute-start.36 = (f32[16,448]{1,0:T(8,128)S(1)}, f32[16,448]{1,0:T(8,128)S(1)}, u32[]{:S(2)}, u32[]{:S(2)}) collective-permute-start(f32[16,448]{1,0:T(8,128)S(1)} %get-tuple-element.99), channel_id=1, source_target_pairs={{0,64},{32,96},{64,0},{96,32},{1,65},{33,97},{65,1},{97,33},{2,66}... | collective-permute-start | bytes 86024 | tf_op jit(solution)/shard_map/ppermute | solution.py:19
  132.2 2.3 %collective-permute-done.39 = f32[16,1088]{1,0:T(8,128)S(1)} collective-permute-done((f32[16,1088]{1,0:T(8,128)S(1)}, f32[16,1088]{1,0:T(8,128)S(1)}, u32[]{:S(2)}, u32[]{:S(2)}) %collective-permute-start.39) | collective-permute-done | bytes 69664 | tf_op jit(solution)/shard_map/ppermute | solution.py:19
  135.4 6.2 %collective-permute-start.41 = (f32[4,16,1088]{2,1,0:T(8,128)S(1)}, f32[4,16,1088]{2,1,0:T(8,128)S(1)}, u32[]{:S(2)}, u32[]{:S(2)}) collective-permute-start(f32[4,16,1088]{2,1,0:T(8,128)S(1)} %pad_maximum_fusion.2.mine), channel_id=1, source_target_pairs={{0,1},{1,0},{2,3},{3,2},{4,5},{5,4},{6,7},{7,6},{8,9},{9,8},{10,11... | collective-permute-start | bytes 835592 | tf_op jit(solution)/shard_map/ppermute | solution.py:23
  142.8 4.9 %third_stage.1 = (f32[128,128]{1,0:T(8,128)S(1)}, f32[2,16,320]{2,1,0:T(8,128)S(1)}, f32[2,16,320]{2,1,0:T(8,128)S(1)}, f32[16,128]{1,0:T(8,128)S(1)}, f32[2,16,64]{2,1,0:T(8,128)S(1)}) custom-call(f32[4,16,1088]{2,1,0:T(8,128)S(1)} %pad_maximum_fusion.2.mine, f32[4,16,1088]{2,1,0:T(8,128)S(1)} %collective-permute-done.41.other, ...), custom_call_target="tpu_custom_call" | custom-call | tf_op jit(solution)/shard_map/third_stage/pallas_call | solution.py:188
  147.6 14.7 %all_to_all.16 = f32[128,1,128]{2,1,0:T(1,128)S(1)} all-to-all(f32[128,1,128]{2,1,0:T(1,128)S(1)} %bitcast.73), channel_id=1, replica_groups=mesh['day_0'=4,'day_1'=4,'blk_0'=4,'blk_1'=2] {'day_0','day_1','blk_0','..., dimensions={0} | all-to-all | bytes 131072 | tf_op jit(solution)/shard_map/all_to_all | solution.py:653
  (157 shorter events, 52.8 us)
Async XLA Ops:
  3.5 23.2 %all-to-all-start = ((f32[16,4,320]{2,1,0:T(4,128)}), f32[16,4,320]{2,1,0:T(4,128)S(1)}, u32[]{:S(2)}, u32[]{:S(2)}) async-start(f32[16,4,320]{2,1,0:T(4,128)} %broadcast_in_dim.137), calls=%async_computation | async-start | bytes 196608 | tf_op jit(solution)/shard_map/all_to_all | solution.py:619
  22.9 5.0 %collective-permute-start.3 = (f32[2,320]{1,0:T(2,128)S(1)}, f32[2,320]{1,0:T(2,128)S(1)}, u32[]{:S(2)}, u32[]{:S(2)}) collective-permute-start(f32[2,320]{1,0:T(2,128)S(1)} %get-tuple-element.172), channel_id=1, source_target_pairs={{0,6},{2,0},{4,2},{6,4},{1,7},{3,1},{5,3},{7,5},{8,14},{10,8},{12,... | collective-permute-start | bytes 7688 | tf_op jit(solution)/shard_map/ppermute | solution.py:19
  25.7 4.0 %collective-permute-start.2 = (f32[2,320]{1,0:T(2,128)S(1)}, f32[2,320]{1,0:T(2,128)S(1)}, u32[]{:S(2)}, u32[]{:S(2)}) collective-permute-start(f32[2,320]{1,0:T(2,128)S(1)} %get-tuple-element.173), channel_id=1, source_target_pairs={{0,4},{2,6},{4,0},{6,2},{1,5},{3,7},{5,1},{7,3},{8,12},{10,14},{12... | collective-permute-start | bytes 7688 | tf_op jit(solution)/shard_map/ppermute | solution.py:19
  26.0 3.7 %collective-permute-start.1 = (f32[2,320]{1,0:T(2,128)S(1)}, f32[2,320]{1,0:T(2,128)S(1)}, u32[]{:S(2)}, u32[]{:S(2)}) collective-permute-start(f32[2,320]{1,0:T(2,128)S(1)} %get-tuple-element.174), channel_id=1, source_target_pairs={{0,2},{2,4},{4,6},{6,0},{1,3},{3,5},{5,7},{7,1},{8,10},{10,12},{12... | collective-permute-start | bytes 7688 | tf_op jit(solution)/shard_map/ppermute | solution.py:19
  30.6 4.1 %collective-permute-start.6 = (f32[16,768]{1,0:T(8,128)S(1)}, f32[16,768]{1,0:T(8,128)S(1)}, u32[]{:S(2)}, u32[]{:S(2)}) collective-permute-start(f32[16,768]{1,0:T(8,128)S(1)} %get-tuple-element.61.m0), channel_id=1, source_target_pairs={{0,24},{8,0},{16,8},{24,16},{1,25},{9,1},{17,9},{25,17},{2,26},{10... | collective-permute-start | bytes 147464 | tf_op jit(solution)/shard_map/ppermute | solution.py:19
  33.5 4.5 %collective-permute-start.5 = (f32[16,768]{1,0:T(8,128)S(1)}, f32[16,768]{1,0:T(8,128)S(1)}, u32[]{:S(2)}, u32[]{:S(2)}) collective-permute-start(f32[16,768]{1,0:T(8,128)S(1)} %get-tuple-element.61.m0), channel_id=1, source_target_pairs={{0,16},{8,24},{16,0},{24,8},{1,17},{9,25},{17,1},{25,9},{2,18},{10... | collective-permute-start | bytes 147464 | tf_op jit(solution)/shard_map/ppermute | solution.py:19
  34.1 4.4 %collective-permute-start.4 = (f32[16,768]{1,0:T(8,128)S(1)}, f32[16,768]{1,0:T(8,128)S(1)}, u32[]{:S(2)}, u32[]{:S(2)}) collective-permute-start(f32[16,768]{1,0:T(8,128)S(1)} %get-tuple-element.61.m0), channel_id=1, source_target_pairs={{0,8},{8,16},{16,24},{24,0},{1,9},{9,17},{17,25},{25,1},{2,10},{10... | collective-permute-start | bytes 147464 | tf_op jit(solution)/shard_map/ppermute | solution.py:19
  38.6 4.8 %collective-permute-start.7 = (f32[16,448]{1,0:T(8,128)S(1)}, f32[16,448]{1,0:T(8,128)S(1)}, u32[]{:S(2)}, u32[]{:S(2)}) collective-permute-start(f32[16,448]{1,0:T(8,128)S(1)} %get-tuple-element.62), channel_id=1, source_target_pairs={{0,32},{32,64},{64,96},{96,0},{1,33},{33,65},{65,97},{97,1},{2,34}... | collective-permute-start | bytes 86024 | tf_op jit(solution)/shard_map/ppermute | solution.py:19
  39.8 4.3 %collective-permute-start.8 = (f32[16,448]{1,0:T(8,128)S(1)}, f32[16,448]{1,0:T(8,128)S(1)}, u32[]{:S(2)}, u32[]{:S(2)}) collective-permute-start(f32[16,448]{1,0:T(8,128)S(1)} %get-tuple-element.63), channel_id=1, source_target_pairs={{0,64},{32,96},{64,0},{96,32},{1,65},{33,97},{65,1},{97,33},{2,66}... | collective-permute-start | bytes 86024 | tf_op jit(solution)/shard_map/ppermute | solution.py:19
  45.7 4.7 %collective-permute-start.11 = (f32[16,1088]{1,0:T(8,128)S(1)}, f32[16,1088]{1,0:T(8,128)S(1)}, u32[]{:S(2)}, u32[]{:S(2)}) collective-permute-start(f32[16,1088]{1,0:T(8,128)S(1)} %get-tuple-element.67), channel_id=1, source_target_pairs={{0,4},{2,6},{4,0},{6,2},{1,5},{3,7},{5,1},{7,3},{8,12},{10,14},{12... | collective-permute-start | bytes 208904 | tf_op jit(solution)/shard_map/ppermute | solution.py:19
  46.9 4.4 %collective-permute-start.10 = (f32[16,1088]{1,0:T(8,128)S(1)}, f32[16,1088]{1,0:T(8,128)S(1)}, u32[]{:S(2)}, u32[]{:S(2)}) collective-permute-start(f32[16,1088]{1,0:T(8,128)S(1)} %get-tuple-element.67), channel_id=1, source_target_pairs={{0,2},{2,4},{4,6},{6,0},{1,3},{3,5},{5,7},{7,1},{8,10},{10,12},{12... | collective-permute-start | bytes 208904 | tf_op jit(solution)/shard_map/ppermute | solution.py:19
  51.4 17.0 %collective-permute-start.13 = (f32[4,16,1088]{2,1,0:T(8,128)S(1)}, f32[4,16,1088]{2,1,0:T(8,128)S(1)}, u32[]{:S(2)}, u32[]{:S(2)}) collective-permute-start(f32[4,16,1088]{2,1,0:T(8,128)S(1)} %pad_maximum_fusion.mine), channel_id=1, source_target_pairs={{0,1},{1,0},{2,3},{3,2},{4,5},{5,4},{6,7},{7,6},{8,9},{9,8},{10,11... | collective-permute-start | bytes 835592 | tf_op jit(solution)/shard_map/ppermute | solution.py:23
  71.7 6.0 %collective-permute-start.17 = (f32[3,16,320]{2,1,0:T(8,128)S(1)}, f32[3,16,320]{2,1,0:T(8,128)S(1)}, u32[]{:S(2)}, u32[]{:S(2)}) collective-permute-start(f32[3,16,320]{2,1,0:T(8,128)S(1)} %get-tuple-element.150), channel_id=1, source_target_pairs={{0,6},{2,0},{4,2},{6,4},{1,7},{3,1},{5,3},{7,5},{8,14},{10,8},{12,... | collective-permute-start | bytes 184328 | tf_op jit(solution)/shard_map/ppermute | solution.py:19
  73.2 4.8 %collective-permute-start.16 = (f32[3,16,320]{2,1,0:T(8,128)S(1)}, f32[3,16,320]{2,1,0:T(8,128)S(1)}, u32[]{:S(2)}, u32[]{:S(2)}) collective-permute-start(f32[3,16,320]{2,1,0:T(8,128)S(1)} %get-tuple-element.151), channel_id=1, source_target_pairs={{0,4},{2,6},{4,0},{6,2},{1,5},{3,7},{5,1},{7,3},{8,12},{10,14},{12... | collective-permute-start | bytes 184328 | tf_op jit(solution)/shard_map/ppermute | solution.py:19
  73.8 6.3 %collective-permute-start.15 = (f32[3,16,320]{2,1,0:T(8,128)S(1)}, f32[3,16,320]{2,1,0:T(8,128)S(1)}, u32[]{:S(2)}, u32[]{:S(2)}) collective-permute-start(f32[3,16,320]{2,1,0:T(8,128)S(1)} %get-tuple-element.152), channel_id=1, source_target_pairs={{0,2},{2,4},{4,6},{6,0},{1,3},{3,5},{5,7},{7,1},{8,10},{10,12},{12... | collective-permute-start | bytes 184328 | tf_op jit(solution)/shard_map/ppermute | solution.py:19
  80.6 4.4 %collective-permute-start.19 = (f32[16,768]{1,0:T(8,128)S(1)}, f32[16,768]{1,0:T(8,128)S(1)}, u32[]{:S(2)}, u32[]{:S(2)}) collective-permute-start(f32[16,768]{1,0:T(8,128)S(1)} %get-tuple-element.80.m0), channel_id=1, source_target_pairs={{0,16},{8,24},{16,0},{24,8},{1,17},{9,25},{17,1},{25,9},{2,18},{10... | collective-permute-start | bytes 147464 | tf_op jit(solution)/shard_map/ppermute | solution.py:19
  81.6 4.2 %collective-permute-start.18 = (f32[16,768]{1,0:T(8,128)S(1)}, f32[16,768]{1,0:T(8,128)S(1)}, u32[]{:S(2)}, u32[]{:S(2)}) collective-permute-start(f32[16,768]{1,0:T(8,128)S(1)} %get-tuple-element.80.m0), channel_id=1, source_target_pairs={{0,8},{8,16},{16,24},{24,0},{1,9},{9,17},{17,25},{25,1},{2,10},{10... | collective-permute-start | bytes 147464 | tf_op jit(solution)/shard_map/ppermute | solution.py:19
  85.9 4.0 %collective-permute-start.21 = (f32[16,448]{1,0:T(8,128)S(1)}, f32[16,448]{1,0:T(8,128)S(1)}, u32[]{:S(2)}, u32[]{:S(2)}) collective-permute-start(f32[16,448]{1,0:T(8,128)S(1)} %get-tuple-element.81), channel_id=1, source_target_pairs={{0,32},{32,64},{64,96},{96,0},{1,33},{33,65},{65,97},{97,1},{2,34}... | collective-permute-start | bytes 86024 | tf_op jit(solution)/shard_map/ppermute | solution.py:19
  86.0 5.2 %collective-permute-start.22 = (f32[16,448]{1,0:T(8,128)S(1)}, f32[16,448]{1,0:T(8,128)S(1)}, u32[]{:S(2)}, u32[]{:S(2)}) collective-permute-start(f32[16,448]{1,0:T(8,128)S(1)} %get-tuple-element.82), channel_id=1, source_target_pairs={{0,64},{32,96},{64,0},{96,32},{1,65},{33,97},{65,1},{97,33},{2,66}... | collective-permute-start | bytes 86024 | tf_op jit(solution)/shard_map/ppermute | solution.py:19
  92.8 4.8 %collective-permute-start.25 = (f32[16,1088]{1,0:T(8,128)S(1)}, f32[16,1088]{1,0:T(8,128)S(1)}, u32[]{:S(2)}, u32[]{:S(2)}) collective-permute-start(f32[16,1088]{1,0:T(8,128)S(1)} %get-tuple-element.86), channel_id=1, source_target_pairs={{0,4},{2,6},{4,0},{6,2},{1,5},{3,7},{5,1},{7,3},{8,12},{10,14},{12... | collective-permute-start | bytes 208904 | tf_op jit(solution)/shard_map/ppermute | solution.py:19
  93.9 4.5 %collective-permute-start.24 = (f32[16,1088]{1,0:T(8,128)S(1)}, f32[16,1088]{1,0:T(8,128)S(1)}, u32[]{:S(2)}, u32[]{:S(2)}) collective-permute-start(f32[16,1088]{1,0:T(8,128)S(1)} %get-tuple-element.86), channel_id=1, source_target_pairs={{0,2},{2,4},{4,6},{6,0},{1,3},{3,5},{5,7},{7,1},{8,10},{10,12},{12... | collective-permute-start | bytes 208904 | tf_op jit(solution)/shard_map/ppermute | solution.py:19
  98.4 7.5 %collective-permute-start.27 = (f32[4,16,1088]{2,1,0:T(8,128)S(1)}, f32[4,16,1088]{2,1,0:T(8,128)S(1)}, u32[]{:S(2)}, u32[]{:S(2)}) collective-permute-start(f32[4,16,1088]{2,1,0:T(8,128)S(1)} %pad_maximum_fusion.1.mine), channel_id=1, source_target_pairs={{0,1},{1,0},{2,3},{3,2},{4,5},{5,4},{6,7},{7,6},{8,9},{9,8},{10,11... | collective-permute-start | bytes 835592 | tf_op jit(solution)/shard_map/ppermute | solution.py:23
  109.6 5.6 %collective-permute-start.31 = (f32[3,16,320]{2,1,0:T(8,128)S(1)}, f32[3,16,320]{2,1,0:T(8,128)S(1)}, u32[]{:S(2)}, u32[]{:S(2)}) collective-permute-start(f32[3,16,320]{2,1,0:T(8,128)S(1)} %get-tuple-element.146), channel_id=1, source_target_pairs={{0,6},{2,0},{4,2},{6,4},{1,7},{3,1},{5,3},{7,5},{8,14},{10,8},{12,... | collective-permute-start | bytes 184328 | tf_op jit(solution)/shard_map/ppermute | solution.py:19
  110.6 4.8 %collective-permute-start.30 = (f32[3,16,320]{2,1,0:T(8,128)S(1)}, f32[3,16,320]{2,1,0:T(8,128)S(1)}, u32[]{:S(2)}, u32[]{:S(2)}) collective-permute-start(f32[3,16,320]{2,1,0:T(8,128)S(1)} %get-tuple-element.147), channel_id=1, source_target_pairs={{0,4},{2,6},{4,0},{6,2},{1,5},{3,7},{5,1},{7,3},{8,12},{10,14},{12... | collective-permute-start | bytes 184328 | tf_op jit(solution)/shard_map/ppermute | solution.py:19
  111.3 5.8 %collective-permute-start.29 = (f32[3,16,320]{2,1,0:T(8,128)S(1)}, f32[3,16,320]{2,1,0:T(8,128)S(1)}, u32[]{:S(2)}, u32[]{:S(2)}) collective-permute-start(f32[3,16,320]{2,1,0:T(8,128)S(1)} %get-tuple-element.148), channel_id=1, source_target_pairs={{0,2},{2,4},{4,6},{6,0},{1,3},{3,5},{5,7},{7,1},{8,10},{10,12},{12... | collective-permute-start | bytes 184328 | tf_op jit(solution)/shard_map/ppermute | solution.py:19
  118.8 4.5 %collective-permute-start.33 = (f32[16,768]{1,0:T(8,128)S(1)}, f32[16,768]{1,0:T(8,128)S(1)}, u32[]{:S(2)}, u32[]{:S(2)}) collective-permute-start(f32[16,768]{1,0:T(8,128)S(1)} %get-tuple-element.97.m0), channel_id=1, source_target_pairs={{0,16},{8,24},{16,0},{24,8},{1,17},{9,25},{17,1},{25,9},{2,18},{10... | collective-permute-start | bytes 147464 | tf_op jit(solution)/shard_map/ppermute | solution.py:19
  119.4 4.3 %collective-permute-start.32 = (f32[16,768]{1,0:T(8,128)S(1)}, f32[16,768]{1,0:T(8,128)S(1)}, u32[]{:S(2)}, u32[]{:S(2)}) collective-permute-start(f32[16,768]{1,0:T(8,128)S(1)} %get-tuple-element.97.m0), channel_id=1, source_target_pairs={{0,8},{8,16},{16,24},{24,0},{1,9},{9,17},{17,25},{25,1},{2,10},{10... | collective-permute-start | bytes 147464 | tf_op jit(solution)/shard_map/ppermute | solution.py:19
  123.9 4.0 %collective-permute-start.35 = (f32[16,448]{1,0:T(8,128)S(1)}, f32[16,448]{1,0:T(8,128)S(1)}, u32[]{:S(2)}, u32[]{:S(2)}) collective-permute-start(f32[16,448]{1,0:T(8,128)S(1)} %get-tuple-element.98), channel_id=1, source_target_pairs={{0,32},{32,64},{64,96},{96,0},{1,33},{33,65},{65,97},{97,1},{2,34}... | collective-permute-start | bytes 86024 | tf_op jit(solution)/shard_map/ppermute | solution.py:19
  123.9 4.3 %collective-permute-start.36 = (f32[16,448]{1,0:T(8,128)S(1)}, f32[16,448]{1,0:T(8,128)S(1)}, u32[]{:S(2)}, u32[]{:S(2)}) collective-permute-start(f32[16,448]{1,0:T(8,128)S(1)} %get-tuple-element.99), channel_id=1, source_target_pairs={{0,64},{32,96},{64,0},{96,32},{1,65},{33,97},{65,1},{97,33},{2,66}... | collective-permute-start | bytes 86024 | tf_op jit(solution)/shard_map/ppermute | solution.py:19
  129.8 4.7 %collective-permute-start.39 = (f32[16,1088]{1,0:T(8,128)S(1)}, f32[16,1088]{1,0:T(8,128)S(1)}, u32[]{:S(2)}, u32[]{:S(2)}) collective-permute-start(f32[16,1088]{1,0:T(8,128)S(1)} %get-tuple-element.103), channel_id=1, source_target_pairs={{0,4},{2,6},{4,0},{6,2},{1,5},{3,7},{5,1},{7,3},{8,12},{10,14},{12... | collective-permute-start | bytes 208904 | tf_op jit(solution)/shard_map/ppermute | solution.py:19
  130.9 4.4 %collective-permute-start.38 = (f32[16,1088]{1,0:T(8,128)S(1)}, f32[16,1088]{1,0:T(8,128)S(1)}, u32[]{:S(2)}, u32[]{:S(2)}) collective-permute-start(f32[16,1088]{1,0:T(8,128)S(1)} %get-tuple-element.103), channel_id=1, source_target_pairs={{0,2},{2,4},{4,6},{6,0},{1,3},{3,5},{5,7},{7,1},{8,10},{10,12},{12... | collective-permute-start | bytes 208904 | tf_op jit(solution)/shard_map/ppermute | solution.py:19
  135.4 7.4 %collective-permute-start.41 = (f32[4,16,1088]{2,1,0:T(8,128)S(1)}, f32[4,16,1088]{2,1,0:T(8,128)S(1)}, u32[]{:S(2)}, u32[]{:S(2)}) collective-permute-start(f32[4,16,1088]{2,1,0:T(8,128)S(1)} %pad_maximum_fusion.2.mine), channel_id=1, source_target_pairs={{0,1},{1,0},{2,3},{3,2},{4,5},{5,4},{6,7},{7,6},{8,9},{9,8},{10,11... | collective-permute-start | bytes 835592 | tf_op jit(solution)/shard_map/ppermute | solution.py:23
  (20 other events, 124.5 us)
where the time goes:
time: 164 us; the launch traced here: 163 us
  starting transfers between devices  63.4 us (39%)
  waiting for transfers between devices  40.2 us (25%)
  Pallas kernels  26.6 us (16%)
  blocking collectives  14.7 us (9%)
  local copies, waits for them, and re-layouts  13.7 us (8%)
  other arithmetic  3.63 us (2%)
    ppermute x36, waiting for transfers between devices, shift(): lax.ppermute(value, axis, [(i, (i + distance) % size) for i in range(size)])  35.6 us
    ppermute x36, starting transfers between devices, shift(): lax.ppermute(value, axis, [(i, (i + distance) % size) for i in range(size)])  34.2 us
    pallas_call x19, Pallas kernels, call(): pl.pallas_call(kernel, out_shape=outs, in_specs=in_specs, out_specs=jax.t...  26.6 us
    ppermute x6, starting transfers between devices, swapped(): return lax.ppermute(value, 'blk_1', [(0, 1), (1, 0)])  20.8 us
    all_to_all x1, blocking collectives, on_device(): sums = lax.all_to_all(sums, DAY + BLK, 0, 0, tiled=True)  14.7 us
    unnamed x20, local copies, waits for them, and re-layouts  11.7 us
    all_to_all x1, starting transfers between devices, on_device(): lax.all_to_all(jnp.broadcast_to(both, (16, 4, 320)), DAY, 0, 0, tiled=True)  8.43 us
    ppermute x6, waiting for transfers between devices, swapped(): return lax.ppermute(value, 'blk_1', [(0, 1), (1, 0)])  4.59 us
  transfers between devices with their start and end apart: 43, of which 35 were waited for; matrix products, arithmetic and copies ran while one was open for 3% of the time, Pallas kernels for 10%

commit v1 on v0

--- a/solution.py
+++ b/solution.py
@@ -1,3 +1,5 @@
+import functools
+
 import jax
 import jax.numpy as jnp
 from jax import lax
@@ -38,50 +40,9 @@
     return [pieces[0]] + [shift(pieces[k], "blk_0", k) for k in (1, 2, 3)]
 
 
-def gather_nodes(message):
-    column = jnp.stack(ring_gather(message, "blk_0"))
-    return column, swapped(column)
-
-
-def chain_coefficients(decay, dominant):
-    group, place = lax.axis_index("day_0"), lax.axis_index("day_1")
-    me = 4 * group + place
-    decays = decay.reshape(32, 320)
-    dominants = dominant.reshape(32, 320)
-    gain = [None] * 33
-    gain[32] = jnp.zeros_like(decays[0])
-    follow = jnp.concatenate([decays[1:], jnp.zeros((1, 320), jnp.float32)])
-    for day in range(31, -1, -1):
-        gain[day] = 1.0 / dominants[day] + follow[day] * follow[day] * gain[day + 1]
-    gains = jnp.stack(gain)
-    follows = jnp.concatenate([decays, jnp.zeros((1, 320), jnp.float32)])
-    days = lax.dynamic_slice_in_dim(gains, 2 * me, 3, 0)
-    decs = lax.dynamic_slice_in_dim(follows, 2 * me, 3, 0)
-    step = (follows[1::2] * follows[2::2]).reshape(4, 4, 320)
-    mine = lax.dynamic_index_in_dim(step, group, 0, False)
-    one, zero = jnp.ones((320,), jnp.float32), jnp.zeros((320,), jnp.float32)
-    index = jnp.arange(4)[:, None]
-
-    def product(factors, low, high):
-        kept = jnp.where((index >= low) & (index < high), factors, 1.0)
-        return kept[0] * kept[1] * kept[2] * kept[3]
-
-    whole = jnp.prod(step, axis=1)
-    local_f, local_b, total_f, total_b, far = [], [], [], [], []
-    for k in range(4):
-        source = (place - k) % 4
-        total_f.append(product(mine, source + 1, 4))
-        total_b.append(product(mine, 0, source))
-        if k:
-            local_f.append(jnp.where(source < place, product(mine, source + 1, place), zero))
-            local_b.append(jnp.where(source > place, product(mine, place + 1, source), zero))
-            origin = (group - k) % 4
-            low, high = jnp.minimum(origin, group) + 1, jnp.maximum(origin, group)
-            far.append(product(whole, low, high))
-    rows = [days[0], days[1], days[2], decs[0], decs[1], decs[2]]
-    rows += local_f + local_b + total_f + total_b + far
-    rows += [product(mine, 0, place), product(mine, place + 1, 4)]
-    return jnp.stack(rows)
+def gather_nodes(message, ready):
+    column, ready = lax.optimization_barrier((jnp.stack(ring_gather(message, "blk_0")), ready))
+    return (column, swapped(column)), ready
 
 
 def ring_message(w, co):
@@ -95,7 +56,12 @@
     return sum(co[first + k : first + k + 1] * value for k, value in enumerate(values))
 
 
-def middle_kernel(m0, m1, m2, m3, co, out1, out2, out3, local):
+def middle_kernel(m0, m1, m2, m3, co, *refs):
+    out1, out2, out3, local = refs[-4:]
+    middle_body(m0, m1, m2, m3, co, out1, out2, out3, local)
+
+
+def middle_body(m0, m1, m2, m3, co, out1, out2, out3, local):
     messages = (m0, m1, m2, m3)
     fs = [m[:, :320] for m in messages]
     bs = [m[:, 320:640] for m in messages]
@@ -112,7 +78,11 @@
         out[:, 320:] = pack
 
 
-def last_kernel(r1, r2, r3, local, w, co, v, message):
+def last_kernel(r1, r2, r3, local, w, co, *refs):
+    last_body(r1, r2, r3, local, w, co, *refs[-2:])
+
+
+def last_body(r1, r2, r3, local, w, co, v, message):
     group = lax.axis_index("day_0")
     g0, g1, gg, d1, dg = co[0:1], co[1:2], co[2:3], co[4:5], co[5:6]
     far_f, far_b = jnp.zeros((16, 320), F32), jnp.zeros((16, 320), F32)
@@ -135,15 +105,17 @@
     message[:, 960:] = ring_sum(packs)
 
 
-def precondition(w, message, co):
+def precondition(w, message, co, early=(), late=()):
     pieces = ring_gather(message, "day_1")
     one = shaped(16, 448)
     *out, local = call(
-        middle_kernel, "middle", (one, one, one, shaped(3, 16, 320)), [VMEM_BLOCK] * 5, *pieces, co
+        middle_kernel, "middle", (one, one, one, shaped(3, 16, 320)),
+        [VMEM_BLOCK] * 5 + [ANY_BLOCK] * len(early), *pieces, co, *early,
     )
     got = [shift(out[k - 1], "day_0", k) for k in (1, 2, 3)]
     return call(
-        last_kernel, "last", (shaped(3, 16, 320), shaped(16, 1088)), [VMEM_BLOCK] * 6, *got, local, w, co
+        last_kernel, "last", (shaped(3, 16, 320), shaped(16, 1088)),
+        [VMEM_BLOCK] * 6 + [ANY_BLOCK] * len(late), *got, local, w, co, *late,
     )
 
 
@@ -177,6 +149,7 @@
 
 VMEM_BLOCK = pl.BlockSpec(memory_space=pltpu.VMEM)
 SMEM_BLOCK = pl.BlockSpec(memory_space=pltpu.SMEM)
+ANY_BLOCK = pl.BlockSpec(memory_space=pl.ANY)
 HBM_BLOCK = pl.BlockSpec(memory_space=pltpu.HBM)
 
 
@@ -184,9 +157,14 @@
     return jax.ShapeDtypeStruct(shape, F32)
 
 
-def call(kernel, name, outs, in_specs, *operands, scratch=(), limit=16):
+def whole_block(operand):
+    return pl.BlockSpec(operand.shape, lambda i: (0,) * operand.ndim)
+
+
+def call(kernel, name, outs, in_specs, *operands, scratch=(), limit=16, grid=()):
     return pl.pallas_call(
         kernel,
+        grid=grid,
         out_shape=outs,
         in_specs=in_specs,
         out_specs=jax.tree.map(lambda _: VMEM_BLOCK, outs),
@@ -199,55 +177,105 @@
 CHUNK = 80
 
 
-def split_kernel(diag, off, diag_pair, off_pair, buffer, sem):
-    jobs = [
-        (source, target, day, row)
-        for source, target in ((off, off_pair), (diag, diag_pair))
-        for day in range(2)
-        for row in range(0, 320, CHUNK)
-    ]
+def split_kernel(day, source, target, buffer, sem):
+    jobs = [(day, row) for row in range(0, 320, CHUNK)]
 
     def fetch(index):
-        source, _, day, row = jobs[index]
+        day, row = jobs[index]
         slot = index % 3
         return pltpu.make_async_copy(source.at[day, pl.ds(row, CHUNK)], buffer.at[slot], sem.at[slot])
 
     fetch(0).start()
     fetch(1).start()
-    for index, (_, target, day, row) in enumerate(jobs):
+    for index, (day, row) in enumerate(jobs):
         if index + 2 < len(jobs):
             fetch(index + 2).start()
         fetch(index).wait()
         high, low = halves(buffer[index % 3])
-        target[day, pl.ds(row, CHUNK)] = high
-        target[day, pl.ds(320 + row, CHUNK)] = low
-
-
-def split_blocks(diag, off):
-    pair = pltpu.VMEM((2, 640, 2560), BF16)
-    return call(
-        split_kernel,
-        "split_blocks",
-        (pair, pair),
-        [HBM_BLOCK, HBM_BLOCK],
-        diag,
-        off,
+        target[pl.ds(row, CHUNK)] = high
+        target[pl.ds(320 + row, CHUNK)] = low
+
+
+def split_blocks(blocks, name, day):
+    return call(
+        functools.partial(split_kernel, day),
+        name + str(day),
+        pltpu.VMEM((640, 2560), BF16),
+        [HBM_BLOCK],
+        pltpu.with_memory_space_constraint(blocks, pltpu.HBM),
         scratch=[pltpu.VMEM((3, CHUNK, 2560), F32), pltpu.SemaphoreType.DMA((3,))],
     )
 
 
-def behind_kernel(off_pair, own, out):
+def chain_kernel(every, co, gains, decs, steps):
+    group, place = lax.axis_index("day_0"), lax.axis_index("day_1")
+    me = 4 * group + place
+    zero, one = jnp.zeros((1, 320), F32), jnp.ones((1, 320), F32)
+    follow = [every[day // 2, day % 2 : day % 2 + 1, :] for day in range(32)] + [zero]
+    gain = zero
+    for day in range(32, -1, -1):
+        if day < 32:
+            inverse = 1.0 / every[day // 2, 2 + day % 2 : 3 + day % 2, :]
+            gain = inverse + follow[day + 1] * follow[day + 1] * gain
+        gains[day : day + 1] = gain
+        decs[day : day + 1] = follow[day]
+    for device in range(16):
+        steps[device : device + 1] = follow[2 * device + 1] * follow[2 * device + 2]
+    mine = [steps[pl.ds(4 * group + device, 1), :] for device in range(4)]
+    whole = []
+    for other in range(4):
+        rows = [steps[4 * other + device : 4 * other + device + 1] for device in range(4)]
+        whole.append(rows[0] * rows[1] * rows[2] * rows[3])
+
+    def product(factors, low, high):
+        kept = [
+            jnp.where((low <= index) & (index < high), factor, one)
+            for index, factor in enumerate(factors)
+        ]
+        return kept[0] * kept[1] * kept[2] * kept[3]
+
+    rows = [gains[pl.ds(2 * me + day, 1), :] for day in range(3)]
+    rows += [decs[pl.ds(2 * me + day, 1), :] for day in range(3)]
+    local_f, local_b, total_f, total_b, far = [], [], [], [], []
+    for k in range(4):
+        source = lax.rem(place + (4 - k), 4)
+        total_f.append(product(mine, source + 1, 4))
+        total_b.append(product(mine, 0, source))
+        if k:
+            local_f.append(jnp.where(source < place, product(mine, source + 1, place), zero))
+            local_b.append(jnp.where(source > place, product(mine, place + 1, source), zero))
+            origin = lax.rem(group + (4 - k), 4)
+            far.append(product(whole, jnp.minimum(origin, group) + 1, jnp.maximum(origin, group)))
+    rows += local_f + local_b + total_f + total_b + far
+    rows += [product(mine, 0, place), product(mine, place + 1, 4)]
+    for index, row in enumerate(rows):
+        co[index : index + 1] = row
+
+
+def chain_coefficients(every):
+    return call(
+        chain_kernel,
+        "chain",
+        shaped(25, 320),
+        [VMEM_BLOCK],
+        every,
+        scratch=[pltpu.VMEM((40, 320), F32), pltpu.VMEM((40, 320), F32), pltpu.VMEM((16, 320), F32)],
+    )
+
+
+def own_terms_kernel(a0, a1, o0, o1, own, out):
+    out[0] = times_matrix(own[0], a0[...])
+    out[1] = times_matrix(own[1], a1[...]) + times_matrix(own[0], o0[...])
+    out[2] = times_matrix(own[1], o1[...])
+
+
+def own_terms(pairs, own):
+    return call(own_terms_kernel, "own_terms", shaped(3, 16, 2560), [VMEM_BLOCK] * 5, *pairs, own)
+
+
+def rows_into(pairs, whole, out):
     for day in range(2):
-        out[day] = times_matrix(own[day], off_pair[day])
-
-
-def behind_terms(off_pair, own):
-    return call(behind_kernel, "behind_terms", shaped(2, 16, 2560), [VMEM_BLOCK] * 2, off_pair, own)
-
-
-def rows_into(diag_pair, off_pair, whole, out):
-    for day in range(2):
-        out[day] = times_rows(whole[day], diag_pair[day]) + times_rows(whole[day + 1], off_pair[day])
+        out[day] = times_rows(whole[day + 1], pairs[day][...])
 
 
 def lanes(*values):
@@ -258,8 +286,8 @@
     return out
 
 
-def first_rows_kernel(diag_pair, off_pair, whole, bx, v1, out, dots):
-    rows_into(diag_pair, off_pair, whole, out)
+def first_rows_kernel(o0, o1, whole, bx, v1, out, dots):
+    rows_into((o0, o1), whole, out)
     dots[...] = lanes(sum(row_sum(bx[day] * v1[day]) for day in range(2)))
 
 
@@ -269,8 +297,8 @@
     )
 
 
-def second_rows_kernel(diag_pair, off_pair, whole, bx, v1, v2, w1, scalars, out, dots, r1, z1):
-    rows_into(diag_pair, off_pair, whole, out)
+def second_rows_kernel(o0, o1, whole, bx, v1, v2, w1, scalars, out, dots, r1, z1):
+    rows_into((o0, o1), whole, out)
     step0 = scalars[:, 0:1]
     norm = cross = jnp.zeros((16, 1), F32)
     for day in range(3):
@@ -294,7 +322,8 @@
     )
 
 
-def start_kernel(p0, p1, p2, p3, probes, grad_cov, co, bx, w, message):
+def start_kernel(p0, p1, p2, p3, probes, grad_cov, co, *refs):
+    bx, w, message = refs[-3:]
     grad = ring_sum([p0[...], p1[...], p2[...], p3[...]])
     for day in range(2):
         bx[day, 0:1] = grad[day : day + 1]
@@ -313,7 +342,7 @@
         start_kernel,
         "start_stage",
         (shaped(2, 16, 320), shaped(3, 16, 320), shaped(16, 768)),
-        [VMEM_BLOCK] * 7,
+        [VMEM_BLOCK] * 7 + [ANY_BLOCK] * (len(operands) - 7),
         *operands,
     )
 
@@ -359,10 +388,10 @@
     return (packs[0] + packs[2]) + (packs[1] + packs[3])
 
 
-def scatter_parts(obs0, obs1, behind0, behind1, kept, sent):
+def scatter_parts(obs, terms, kept, sent):
     core = lax.axis_index("blk_1")
     last = lax.axis_index("day_0") * 4 + lax.axis_index("day_1") == 15
-    days = (obs0, obs1 + behind0, jnp.where(last, 0.0, behind1))
+    days = (obs[0] + terms[0], obs[1] + terms[1], jnp.where(last, 0.0, terms[2]))
     for day, part in enumerate(days):
         for row in range(4):
             first = part[:, row * 640 : row * 640 + 320]
@@ -376,7 +405,7 @@
     for day in range(2):
         out = matmul(stacked_halves(whole[day]), spread[day], NN)
         out = (out[:16, :128] + out[16:, :128]) + (out[:16, 128:] + out[16:, 128:])
-        predictor = out + times_matrix(cov, stacked_halves(covariates[day]))
+        predictor = out + times_matrix(cov, covariates[day])
         result.append((predictor, weight[day : day + 1] * predictor))
     return result
 
@@ -393,8 +422,8 @@
 def observe_back(observed, behind, spread, covariates, kept, sent, cov_terms):
     weights = [pair[1] for pair in observed]
     obs = [spread_out(weights[day], spread[day]) for day in range(2)]
-    scatter_parts(obs[0], obs[1], behind[0], behind[1], kept, sent)
-    cov_terms[...] = sum(times_rows(weights[day], stacked_halves(covariates[day])) for day in range(2))
+    scatter_parts(obs, behind, kept, sent)
+    cov_terms[...] = sum(times_rows(weights[day], covariates[day]) for day in range(2))
 
 
 def row_sum(value):
@@ -434,7 +463,7 @@
     step0 = norm0 / curve0
     for day in range(3):
         whole[day] = whole1[day] - step0 * whole2[day]
-    for day in range(2):
+    for day in range(3):
         behind[day] = behind1[day] - step0 * behind2[day]
     cov[...] = c0[...] - step0 * hcov1
     hcov[...] = hcov1
@@ -452,13 +481,13 @@
         PARTS + (whole, whole, shaped(16, 64), shaped(16, 64), shaped(16, 128)),
         [VMEM_BLOCK] * 10,
         mine, other, whole1, c0, prior, spread, covariates, weight, behind1, behind2,
-        scratch=[pltpu.VMEM((2, 16, 2560), F32)],
+        scratch=[pltpu.VMEM((3, 16, 2560), F32)],
     )
 
 
 def third_kernel(
     mine, other, whole2, z1whole, scalars, c0, z1cov, hcov1, prior, spread, covariates, weight,
-    diag_pair, off_pair, r1, z1, w1, w2, v1, v2, v3,
+    a0, a1, o0, o1, r1, z1, w1, w2, v1, v2, v3,
     sums, z2, p1, scalars_out, covs, whole,
 ):
     pack = assemble(mine, other, whole)
@@ -492,8 +521,10 @@
     observed = observe(whole, r2cov, spread, covariates, weight)
     quadratic = sum(row_sum(predictor * weighted) for predictor, weighted in observed)
     for day in range(2):
-        rows = times_rows(whole[day], diag_pair[day]) + 2.0 * times_rows(whole[day + 1], off_pair[day])
-        quadratic = quadratic + row_sum(z2[day] * rows)
+        quadratic = quadratic + row_sum(times_matrix(z2[day], (a0, a1)[day][...]) * whole[day])
+        quadratic = quadratic + 2.0 * row_sum(
+            times_matrix(z2[day], (o0, o1)[day][...]) * whole[day + 1]
+        )
     lane = lax.broadcasted_iota(jnp.int32, (16, 128), 1)
     sub = lax.broadcasted_iota(jnp.int32, (16, 128), 0)
     line = jnp.zeros((16, 128), F32)
@@ -554,7 +585,7 @@
     )
 
 
-def setup_kernel(count, vertices, bary, prec, value, covariates, spread, weight, kept, sent, grad_cov):
+def setup_kernel(count, vertices, bary, prec, value, covs, after, spread, weight, kept, sent, grad_cov, covariates):
     core = lax.axis_index("blk_1")
     slot_start = (lax.axis_index("blk_0") * 2 + core) * 128
     cov_sum = jnp.zeros((1, 64), F32)
@@ -568,6 +599,7 @@
         high, low = halves(dense)
         spread[day, :, :128] = high
         spread[day, :, 128:] = low
+        covariates[day] = stacked_halves(covs[:, day, :])
         slot = lax.broadcasted_iota(jnp.int32, (1, 128), 1) + slot_start
         slot_weight = jnp.where(slot < count[day], prec[day : day + 1], 0.0)
         weight[day : day + 1] = slot_weight
@@ -578,7 +610,7 @@
             second = grad[:, row * 640 + 320 : row * 640 + 640]
             kept[row, day : day + 1] = jnp.where(core == 0, first, second)
             sent[row, day : day + 1] = jnp.where(core == 0, second, first)
-        cov_sum = cov_sum + times_rows(weighted_value, stacked_halves(covariates[day]))[:1]
+        cov_sum = cov_sum + times_rows(weighted_value, covariates[day])[:1]
     grad_cov[...] = cov_sum
 
 
@@ -588,10 +620,13 @@
         "setup_stage",
         (
             pltpu.VMEM((2, 2560, 256), BF16), shaped(2, 128), shaped(4, 2, 320), shaped(4, 2, 320),
-            shaped(1, 64),
+            shaped(1, 64), pltpu.VMEM((2, 128, 128), BF16),
         ),
-        [SMEM_BLOCK] + [VMEM_BLOCK] * (len(operands) - 1),
-        *operands,
+        [SMEM_BLOCK] + [whole_block(o) for o in operands[1:-1]] + [ANY_BLOCK],
+        operands[0],
+        *(pltpu.with_memory_space_constraint(o, pltpu.HBM) for o in operands[1:-1]),
+        operands[-1],
+        grid=(1,),
     )
 
 
@@ -617,38 +652,39 @@
     dominant = jnp.sum(jnp.where(rows == columns, square, 0.0), axis=1)
     both = jnp.concatenate([1.0 - leakage, dominant])
     every = lax.all_to_all(jnp.broadcast_to(both, (16, 4, 320)), DAY, 0, 0, tiled=True)
-    co = chain_coefficients(every[:, :2], every[:, 2:])
+    co = chain_coefficients(every)
 
     vertices = triangles[:, obs_triangle]
-    covs = jnp.moveaxis(covariates, 1, 0)
-    spread, weight, kept, sent, grad_cov = setup_stage(
-        obs_count, vertices, obs_bary, obs_prec, obs_value, covs
-    )
-    diag_pair, off_pair = split_blocks(diag_blocks, off_blocks)
-    bx, w0, message = start_stage(*scattered_pieces(kept, sent), probes, grad_cov, co)
+    spread, weight, kept, sent, grad_cov, covs = setup_stage(
+        obs_count, vertices, obs_bary, obs_prec, obs_value, covariates, co
+    )
+    off_pair = [split_blocks(off_blocks, "split_off", day) for day in range(2)]
+    diag_pair = [split_blocks(diag_blocks, "split_diag", day) for day in range(2)]
+    bx, w0, message = start_stage(*scattered_pieces(kept, sent), probes, grad_cov, co, off_pair[0])
     prior = prior_prec[None]
     padded_cov = jnp.pad(probes_cov, ((1, 0), (0, 0)))
 
-    v1, message = precondition(w0, message, co)
-    behind1 = behind_terms(off_pair, v1)
+    pairs = (*diag_pair, *off_pair)
+    v1, message = precondition(w0, message, co, (off_pair[1],), (diag_pair[0],))
+    nodes, behind1 = gather_nodes(message, own_terms(pairs, v1))
     kept, sent, cov1, whole1, c0 = first_stage(
-        *gather_nodes(message), padded_cov, spread, covs, weight, behind1
-    )
-    image, dots = first_rows(diag_pair, off_pair, whole1, bx, v1)
+        *nodes, padded_cov, spread, covs, weight, behind1
+    )
+    image, dots = first_rows(*off_pair, whole1, bx, v1)
     w1, message = image_stage(*scattered_pieces(kept, sent), image, v1, cov1, dots, co)
 
     v2, message = precondition(w1, message, co)
-    behind2 = behind_terms(off_pair, v2)
+    nodes, behind2 = gather_nodes(message, own_terms(pairs, v2))
     kept, sent, cov2, whole2, z1whole, z1cov, hcov1, scalars = second_stage(
-        *gather_nodes(message), whole1, c0, prior, spread, covs, weight, behind1, behind2
-    )
-    image, dots, r1, z1 = second_rows(diag_pair, off_pair, z1whole, bx, v1, v2, w1, scalars)
+        *nodes, whole1, c0, prior, spread, covs, weight, behind1, behind2
+    )
+    image, dots, r1, z1 = second_rows(*off_pair, z1whole, bx, v1, v2, w1, scalars)
     w2, message = image_stage(*scattered_pieces(kept, sent), image, z1, cov2, dots, co)
 
     v3, message = precondition(w2, message, co)
     sums, z2, p1, scalars, covs2 = third_stage(
-        *gather_nodes(message), whole2, z1whole, scalars, c0, z1cov, hcov1, prior, spread, covs, weight,
-        diag_pair, off_pair, r1, z1, w1, w2, v1, v2, v3,
+        *gather_nodes(message, behind2)[0], whole2, z1whole, scalars, c0, z1cov, hcov1, prior, spread, covs, weight,
+        *pairs, r1, z1, w1, w2, v1, v2, v3,
     )
     sums = lax.all_to_all(sums, DAY + BLK, 0, 0, tiled=True)
     return final_stage(sums, scalars, v1, p1, z2, c0, covs2)

time: 164 us -> 153 us (0.933)
  local copies, waits for them, and re-layouts: 13.7 us -> 3.81 us
  Pallas kernels: 26.6 us -> 31.1 us
  starting transfers between devices: 63.4 us -> 60.8 us
  waiting for transfers between devices: 40.2 us -> 38.2 us
    unnamed x20 -> x9, local copies, waits for them, and re-layouts: 11.7 us -> 1.67 us
    ppermute x36, waiting for transfers between devices: 35.6 us -> 28.4 us  [shift(): lax.ppermute(value, axis, [(i, (i + distance) % size) for i in range(size)])]
    pallas_call x19 -> x23, Pallas kernels: 26.6 us -> 31.1 us  [call(): pl.pallas_call(kernel, grid=grid, out_shape=outs, in_specs=in_specs, out_...]
    all_to_all x1, waiting for transfers between devices: 0.01 us -> 2.97 us  [on_device(): lax.all_to_all(jnp.broadcast_to(both, (16, 4, 320)), DAY, 0, 0, tiled=True)]
    ppermute x6, waiting for transfers between devices: 4.59 us -> 6.87 us  [swapped(): return lax.ppermute(value, 'blk_1', [(0, 1), (1, 0)])]
    ppermute x36, starting transfers between devices: 34.2 us -> 32.2 us  [shift(): lax.ppermute(value, axis, [(i, (i + distance) % size) for i in range(size)])]
  transfers between devices with their start and end apart: 43 -> 43, of which waited for: 35 -> 31; matrix products, arithmetic and copies ran while one was open for 3% -> 2% of each run, Pallas kernels for 10% -> 12%
where the time goes in v1:
time: 153 us; the launch traced here: 152 us
  starting transfers between devices  60.8 us (40%)
  waiting for transfers between devices  38.2 us (25%)
  Pallas kernels  31.1 us (20%)
  blocking collectives  14.5 us (9%)
  local copies, waits for them, and re-layouts  3.81 us (2%)
  other arithmetic  3.01 us (2%)
    ppermute x36, starting transfers between devices, shift(): lax.ppermute(value, axis, [(i, (i + distance) % size) for i in range(size)])  32.2 us
    pallas_call x23, Pallas kernels, call(): pl.pallas_call(kernel, grid=grid, out_shape=outs, in_specs=in_specs, out_...  31.1 us
    ppermute x36, waiting for transfers between devices, shift(): lax.ppermute(value, axis, [(i, (i + distance) % size) for i in range(size)])  28.4 us
    ppermute x6, starting transfers between devices, swapped(): return lax.ppermute(value, 'blk_1', [(0, 1), (1, 0)])  20.2 us
    all_to_all x1, blocking collectives, on_device(): sums = lax.all_to_all(sums, DAY + BLK, 0, 0, tiled=True)  14.5 us
    all_to_all x1, starting transfers between devices, on_device(): lax.all_to_all(jnp.broadcast_to(both, (16, 4, 320)), DAY, 0, 0, tiled=True)  8.43 us
    ppermute x6, waiting for transfers between devices, swapped(): return lax.ppermute(value, 'blk_1', [(0, 1), (1, 0)])  6.87 us
  transfers between devices with their start and end apart: 43, of which 31 were waited for; matrix products, arithmetic and copies ran while one was open for 2% of the time, Pallas kernels for 12%

profile of v1, /device:TPU:1, one launch (start us, length us, event | category | flops | bytes accessed | tf_op | source)
XLA Modules:
  0.0 152.4 jit_solution(16932148308487651430)
XLA Ops:
  3.5 8.4 %all-to-all-start = ((f32[16,4,320]{2,1,0:T(4,128)}), f32[16,4,320]{2,1,0:T(4,128)S(1)}, u32[]{:S(2)}, u32[]{:S(2)}) async-start(f32[16,4,320]{2,1,0:T(4,128)} %broadcast_in_dim.15), calls=%async_computation | async-start | bytes 196608 | tf_op jit(solution)/shard_map/all_to_all | solution.py:654
  15.7 3.0 %all-to-all-done.every = f32[16,4,320]{2,1,0:T(4,128)S(1)} async-done(((f32[16,4,320]{2,1,0:T(4,128)}), f32[16,4,320]{2,1,0:T(4,128)S(1)}, u32[]{:S(2)}, u32[]{:S(2)}) %all-to-all-start) | async-done | bytes 81952 | tf_op jit(solution)/shard_map/all_to_all | solution.py:654
  18.8 2.9 %setup_stage.1 = (bf16[2,2560,256]{2,1,0:T(8,128)(2,1)S(1)}, f32[2,128]{1,0:T(2,128)S(1)}, f32[4,2,320]{2,1,0:T(2,128)S(1)}, f32[4,2,320]{2,1,0:T(2,128)S(1)}, f...) custom-call(s32[2]{0:T(128)S(1)} %copy-done.2, s32[3,2,128]{2,1,0:T(2,128)} %bitcast.62, f32[3,2,128]{2,1,0:T(2,128)} %bary.1, ...), custom_call_target="tpu_custom_call" | custom-call | tf_op jit(solution)/shard_map/setup_stage/pallas_call | solution.py:165
  21.7 2.1 %collective-permute-start = (f32[4,2,320]{2,1,0:T(2,128)S(1)}, f32[4,2,320]{2,1,0:T(2,128)S(1)}, u32[]{:S(2)}, u32[]{:S(2)}) collective-permute-start(f32[4,2,320]{2,1,0:T(2,128)S(1)} %get-tuple-element.63), channel_id=1, source_target_pairs={{0,1},{1,0},{2,3},{3,2},{4,5},{5,4},{6,7},{7,6},{8,9},{9,8},{10,11... | collective-permute-start | bytes 30728 | tf_op jit(solution)/shard_map/ppermute | solution.py:25
  24.7 2.8 %collective-permute-start.3 = (f32[2,320]{1,0:T(2,128)S(1)}, f32[2,320]{1,0:T(2,128)S(1)}, u32[]{:S(2)}, u32[]{:S(2)}) collective-permute-start(f32[2,320]{1,0:T(2,128)S(1)} %get-tuple-element.130), channel_id=1, source_target_pairs={{0,6},{2,0},{4,2},{6,4},{1,7},{3,1},{5,3},{7,5},{8,14},{10,8},{12,... | collective-permute-start | bytes 7688 | tf_op jit(solution)/shard_map/ppermute | solution.py:21
  28.6 2.6 %split_off0.1.refs_0_.o0 = bf16[640,2560]{1,0:T(8,128)(2,1)S(1)} custom-call(f32[2,320,2560]{2,1,0:T(8,128)} %source.5), custom_call_target="tpu_custom_call" | custom-call | tf_op jit(solution)/shard_map/split_off0/pallas_call | solution.py:165
  33.7 2.6 %split_off1.1.refs_0_.o1 = bf16[640,2560]{1,0:T(8,128)(2,1)S(1)} custom-call(f32[2,320,2560]{2,1,0:T(8,128)} %source.5), custom_call_target="tpu_custom_call" | custom-call | tf_op jit(solution)/shard_map/split_off1/pallas_call | solution.py:165
  38.2 1.8 %collective-permute-start.8 = (f32[16,448]{1,0:T(8,128)S(1)}, f32[16,448]{1,0:T(8,128)S(1)}, u32[]{:S(2)}, u32[]{:S(2)}) collective-permute-start(f32[16,448]{1,0:T(8,128)S(1)} %get-tuple-element.67), channel_id=1, source_target_pairs={{0,64},{32,96},{64,0},{96,32},{1,65},{33,97},{65,1},{97,33},{2,66}... | collective-permute-start | bytes 86024 | tf_op jit(solution)/shard_map/ppermute | solution.py:21
  40.9 2.6 %split_diag0.1.refs_0_.a0 = bf16[640,2560]{1,0:T(8,128)(2,1)S(1)} custom-call(f32[2,320,2560]{2,1,0:T(8,128)} %source.7), custom_call_target="tpu_custom_call" | custom-call | tf_op jit(solution)/shard_map/split_diag0/pallas_call | solution.py:165
  43.7 1.7 %collective-permute-start.12 = (f32[16,1088]{1,0:T(8,128)S(1)}, f32[16,1088]{1,0:T(8,128)S(1)}, u32[]{:S(2)}, u32[]{:S(2)}) collective-permute-start(f32[16,1088]{1,0:T(8,128)S(1)} %get-tuple-element.71), channel_id=1, source_target_pairs={{0,6},{2,0},{4,2},{6,4},{1,7},{3,1},{5,3},{7,5},{8,14},{10,8},{12,... | collective-permute-start | bytes 208904 | tf_op jit(solution)/shard_map/ppermute | solution.py:21
  46.8 2.6 %split_diag1.1.a1 = bf16[640,2560]{1,0:T(8,128)(2,1)S(1)} custom-call(f32[2,320,2560]{2,1,0:T(8,128)} %source.7), custom_call_target="tpu_custom_call" | custom-call | tf_op jit(solution)/shard_map/split_diag1/pallas_call | solution.py:165
  49.4 2.3 %own_terms.2.behind.behind1 = f32[3,16,2560]{2,1,0:T(8,128)S(1)} custom-call(bf16[640,2560]{1,0:T(8,128)(2,1)S(1)} %split_diag0.1.refs_0_.a0, bf16[640,2560]{1,0:T(8,128)(2,1)S(1)} %split_diag1.1.a1, bf16[640,2560]{1,0:T(8,128)(2,1)S(1)} %split_off0.1.refs_0_.o0, bf16[640,2560]{1,0:T(8,128)(2,1)S(1)} %split_off1.1.refs_0_.o1, ...), custom_call_target="tpu_custom_call" | custom-call | tf_op jit(solution)/shard_map/own_terms/pallas_call | solution.py:165
  51.8 5.2 %collective-permute-start.13 = (f32[4,16,1088]{2,1,0:T(8,128)S(1)}, f32[4,16,1088]{2,1,0:T(8,128)S(1)}, u32[]{:S(2)}, u32[]{:S(2)}) collective-permute-start(f32[4,16,1088]{2,1,0:T(8,128)S(1)} %pad_maximum_fusion.mine), channel_id=1, source_target_pairs={{0,1},{1,0},{2,3},{3,2},{4,5},{5,4},{6,7},{7,6},{8,9},{9,8},{10,11... | collective-permute-start | bytes 835592 | tf_op jit(solution)/shard_map/ppermute | solution.py:25
  61.6 2.4 %collective-permute-start.17 = (f32[3,16,320]{2,1,0:T(8,128)S(1)}, f32[3,16,320]{2,1,0:T(8,128)S(1)}, u32[]{:S(2)}, u32[]{:S(2)}) collective-permute-start(f32[3,16,320]{2,1,0:T(8,128)S(1)} %get-tuple-element.126), channel_id=1, source_target_pairs={{0,6},{2,0},{4,2},{6,4},{1,7},{3,1},{5,3},{7,5},{8,14},{10,8},{12,... | collective-permute-start | bytes 184328 | tf_op jit(solution)/shard_map/ppermute | solution.py:21
  65.0 2.0 %first_rows.1 = (f32[2,16,320]{2,1,0:T(8,128)S(1)}, f32[16,64]{1,0:T(8,128)S(1)}) custom-call(bf16[640,2560]{1,0:T(8,128)(2,1)S(1)} %split_off0.1.refs_0_.o0, bf16[640,2560]{1,0:T(8,128)(2,1)S(1)} %split_off1.1.refs_0_.o1, f32[3,16,2560]{2,1,0:T(8,128)S(1)} %get-tuple-element.80.whole.whole1, f32[2,16,320]{2,1,0:T(8,128)S(1)} %get-tuple-element.81.bx, ...), custom_call_target="tpu_custom_call" | custom-call | tf_op jit(solution)/shard_map/first_rows/pallas_call | solution.py:165
  67.0 1.7 %collective-permute-done.16.p2 = f32[3,16,320]{2,1,0:T(8,128)S(1)} collective-permute-done((f32[3,16,320]{2,1,0:T(8,128)S(1)}, f32[3,16,320]{2,1,0:T(8,128)S(1)}, u32[]{:S(2)}, u32[]{:S(2)}) %collective-permute-start.16) | collective-permute-done | bytes 61472 | tf_op jit(solution)/shard_map/ppermute | solution.py:21
  68.7 2.0 %collective-permute-done.15.p1 = f32[3,16,320]{2,1,0:T(8,128)S(1)} collective-permute-done((f32[3,16,320]{2,1,0:T(8,128)S(1)}, f32[3,16,320]{2,1,0:T(8,128)S(1)}, u32[]{:S(2)}, u32[]{:S(2)}) %collective-permute-start.15) | collective-permute-done | bytes 61472 | tf_op jit(solution)/shard_map/ppermute | solution.py:21
  73.9 2.1 %collective-permute-done.19.m2 = f32[16,768]{1,0:T(8,128)S(1)} collective-permute-done((f32[16,768]{1,0:T(8,128)S(1)}, f32[16,768]{1,0:T(8,128)S(1)}, u32[]{:S(2)}, u32[]{:S(2)}) %collective-permute-start.19) | collective-permute-done | bytes 49184 | tf_op jit(solution)/shard_map/ppermute | solution.py:21
  78.0 2.2 %collective-permute-start.22 = (f32[16,448]{1,0:T(8,128)S(1)}, f32[16,448]{1,0:T(8,128)S(1)}, u32[]{:S(2)}, u32[]{:S(2)}) collective-permute-start(f32[16,448]{1,0:T(8,128)S(1)} %get-tuple-element.87), channel_id=1, source_target_pairs={{0,64},{32,96},{64,0},{96,32},{1,65},{33,97},{65,1},{97,33},{2,66}... | collective-permute-start | bytes 86024 | tf_op jit(solution)/shard_map/ppermute | solution.py:21
  84.6 2.3 %own_terms.3.behind2 = f32[3,16,2560]{2,1,0:T(8,128)S(1)} custom-call(bf16[640,2560]{1,0:T(8,128)(2,1)S(1)} %split_diag0.1.refs_0_.a0, bf16[640,2560]{1,0:T(8,128)(2,1)S(1)} %split_diag1.1.a1, bf16[640,2560]{1,0:T(8,128)(2,1)S(1)} %split_off0.1.refs_0_.o0, bf16[640,2560]{1,0:T(8,128)(2,1)S(1)} %split_off1.1.refs_0_.o1, ...), custom_call_target="tpu_custom_call" | custom-call | tf_op jit(solution)/shard_map/own_terms/pallas_call | solution.py:165
  88.8 5.9 %collective-permute-start.27 = (f32[4,16,1088]{2,1,0:T(8,128)S(1)}, f32[4,16,1088]{2,1,0:T(8,128)S(1)}, u32[]{:S(2)}, u32[]{:S(2)}) collective-permute-start(f32[4,16,1088]{2,1,0:T(8,128)S(1)} %pad_maximum_fusion.1.mine), channel_id=1, source_target_pairs={{0,1},{1,0},{2,3},{3,2},{4,5},{5,4},{6,7},{7,6},{8,9},{9,8},{10,11... | collective-permute-start | bytes 835592 | tf_op jit(solution)/shard_map/ppermute | solution.py:25
  95.9 2.0 %second_stage.1 = (f32[4,3,16,320]{3,2,1,0:T(8,128)S(1)}, f32[4,3,16,320]{3,2,1,0:T(8,128)S(1)}, f32[16,64]{1,0:T(8,128)S(1)}, f32[3,16,2560]{2,1,0:T(8,128)S(1)...) custom-call(f32[4,16,1088]{2,1,0:T(8,128)S(1)} %pad_maximum_fusion.1.mine, ...), custom_call_target="tpu_custom_call" | custom-call | tf_op jit(solution)/shard_map/second_stage/pallas_call | solution.py:165
  99.6 1.8 %collective-permute-start.31 = (f32[3,16,320]{2,1,0:T(8,128)S(1)}, f32[3,16,320]{2,1,0:T(8,128)S(1)}, u32[]{:S(2)}, u32[]{:S(2)}) collective-permute-start(f32[3,16,320]{2,1,0:T(8,128)S(1)} %get-tuple-element.122), channel_id=1, source_target_pairs={{0,6},{2,0},{4,2},{6,4},{1,7},{3,1},{5,3},{7,5},{8,14},{10,8},{12,... | collective-permute-start | bytes 184328 | tf_op jit(solution)/shard_map/ppermute | solution.py:21
  102.1 2.0 %second_rows.1 = (f32[2,16,320]{2,1,0:T(8,128)S(1)}, f32[16,64]{1,0:T(8,128)S(1)}, f32[3,16,320]{2,1,0:T(8,128)S(1)}, f32[3,16,320]{2,1,0:T(8,128)S(1)}) custom-call(bf16[640,2560]{1,0:T(8,128)(2,1)S(1)} %split_off0.1.refs_0_.o0, bf16[640,2560]{1,0:T(8,128)(2,1)S(1)} %split_off1.1.refs_0_.o1, f32[3,16,2560]{2,1,0:T(8,128)S(1)} %get-tuple-element.98.whole.z1whole, ...), custom_call_target="tpu_custom_call" | custom-call | tf_op jit(solution)/shard_map/second_rows/pallas_call | solution.py:165
  104.2 2.0 %collective-permute-done.30.p2 = f32[3,16,320]{2,1,0:T(8,128)S(1)} collective-permute-done((f32[3,16,320]{2,1,0:T(8,128)S(1)}, f32[3,16,320]{2,1,0:T(8,128)S(1)}, u32[]{:S(2)}, u32[]{:S(2)}) %collective-permute-start.30) | collective-permute-done | bytes 61472 | tf_op jit(solution)/shard_map/ppermute | solution.py:21
  106.2 1.9 %collective-permute-done.29.p1 = f32[3,16,320]{2,1,0:T(8,128)S(1)} collective-permute-done((f32[3,16,320]{2,1,0:T(8,128)S(1)}, f32[3,16,320]{2,1,0:T(8,128)S(1)}, u32[]{:S(2)}, u32[]{:S(2)}) %collective-permute-start.29) | collective-permute-done | bytes 61472 | tf_op jit(solution)/shard_map/ppermute | solution.py:21
  111.2 2.7 %collective-permute-done.33.m2 = f32[16,768]{1,0:T(8,128)S(1)} collective-permute-done((f32[16,768]{1,0:T(8,128)S(1)}, f32[16,768]{1,0:T(8,128)S(1)}, u32[]{:S(2)}, u32[]{:S(2)}) %collective-permute-start.33) | collective-permute-done | bytes 49184 | tf_op jit(solution)/shard_map/ppermute | solution.py:21
  114.7 3.1 %collective-permute-start.36 = (f32[16,448]{1,0:T(8,128)S(1)}, f32[16,448]{1,0:T(8,128)S(1)}, u32[]{:S(2)}, u32[]{:S(2)}) collective-permute-start(f32[16,448]{1,0:T(8,128)S(1)} %get-tuple-element.106), channel_id=1, source_target_pairs={{0,64},{32,96},{64,0},{96,32},{1,65},{33,97},{65,1},{97,33},{2,66}... | collective-permute-start | bytes 86024 | tf_op jit(solution)/shard_map/ppermute | solution.py:21
  122.2 2.0 %collective-permute-done.40 = f32[16,1088]{1,0:T(8,128)S(1)} collective-permute-done((f32[16,1088]{1,0:T(8,128)S(1)}, f32[16,1088]{1,0:T(8,128)S(1)}, u32[]{:S(2)}, u32[]{:S(2)}) %collective-permute-start.40) | collective-permute-done | bytes 69664 | tf_op jit(solution)/shard_map/ppermute | solution.py:21
  126.3 6.0 %collective-permute-start.41 = (f32[4,16,1088]{2,1,0:T(8,128)S(1)}, f32[4,16,1088]{2,1,0:T(8,128)S(1)}, u32[]{:S(2)}, u32[]{:S(2)}) collective-permute-start(f32[4,16,1088]{2,1,0:T(8,128)S(1)} %pad_maximum_fusion.2.mine), channel_id=1, source_target_pairs={{0,1},{1,0},{2,3},{3,2},{4,5},{5,4},{6,7},{7,6},{8,9},{9,8},{10,11... | collective-permute-start | bytes 835592 | tf_op jit(solution)/shard_map/ppermute | solution.py:25
  133.5 3.2 %third_stage.1 = (f32[128,128]{1,0:T(8,128)S(1)}, f32[2,16,320]{2,1,0:T(8,128)S(1)}, f32[2,16,320]{2,1,0:T(8,128)S(1)}, f32[16,128]{1,0:T(8,128)S(1)}, f32[2,16,64]{2,1,0:T(8,128)S(1)}) custom-call(f32[4,16,1088]{2,1,0:T(8,128)S(1)} %pad_maximum_fusion.2.mine, f32[4,16,1088]{2,1,0:T(8,128)S(1)} %collective-permute-done.41.other, ...), custom_call_target="tpu_custom_call" | custom-call | tf_op jit(solution)/shard_map/third_stage/pallas_call | solution.py:165
  136.8 14.5 %all_to_all.16 = f32[128,1,128]{2,1,0:T(1,128)S(1)} all-to-all(f32[128,1,128]{2,1,0:T(1,128)S(1)} %bitcast.49), channel_id=1, replica_groups=mesh['day_0'=4,'day_1'=4,'blk_0'=4,'blk_1'=2] {'day_0','day_1','blk_0','..., dimensions={0} | all-to-all | bytes 131072 | tf_op jit(solution)/shard_map/all_to_all | solution.py:689
  (105 shorter events, 48.9 us)
Async XLA Ops:
  3.5 15.2 %all-to-all-start = ((f32[16,4,320]{2,1,0:T(4,128)}), f32[16,4,320]{2,1,0:T(4,128)S(1)}, u32[]{:S(2)}, u32[]{:S(2)}) async-start(f32[16,4,320]{2,1,0:T(4,128)} %broadcast_in_dim.15), calls=%async_computation | async-start | bytes 196608 | tf_op jit(solution)/shard_map/all_to_all | solution.py:654
  24.7 6.5 %collective-permute-start.3 = (f32[2,320]{1,0:T(2,128)S(1)}, f32[2,320]{1,0:T(2,128)S(1)}, u32[]{:S(2)}, u32[]{:S(2)}) collective-permute-start(f32[2,320]{1,0:T(2,128)S(1)} %get-tuple-element.130), channel_id=1, source_target_pairs={{0,6},{2,0},{4,2},{6,4},{1,7},{3,1},{5,3},{7,5},{8,14},{10,8},{12,... | collective-permute-start | bytes 7688 | tf_op jit(solution)/shard_map/ppermute | solution.py:21
  27.5 4.0 %collective-permute-start.2 = (f32[2,320]{1,0:T(2,128)S(1)}, f32[2,320]{1,0:T(2,128)S(1)}, u32[]{:S(2)}, u32[]{:S(2)}) collective-permute-start(f32[2,320]{1,0:T(2,128)S(1)} %get-tuple-element.131), channel_id=1, source_target_pairs={{0,4},{2,6},{4,0},{6,2},{1,5},{3,7},{5,1},{7,3},{8,12},{10,14},{12... | collective-permute-start | bytes 7688 | tf_op jit(solution)/shard_map/ppermute | solution.py:21
  31.6 4.7 %collective-permute-start.6 = (f32[16,768]{1,0:T(8,128)S(1)}, f32[16,768]{1,0:T(8,128)S(1)}, u32[]{:S(2)}, u32[]{:S(2)}) collective-permute-start(f32[16,768]{1,0:T(8,128)S(1)} %get-tuple-element.65.m0), channel_id=1, source_target_pairs={{0,24},{8,0},{16,8},{24,16},{1,25},{9,1},{17,9},{25,17},{2,26},{10... | collective-permute-start | bytes 147464 | tf_op jit(solution)/shard_map/ppermute | solution.py:21
  32.4 4.4 %collective-permute-start.5 = (f32[16,768]{1,0:T(8,128)S(1)}, f32[16,768]{1,0:T(8,128)S(1)}, u32[]{:S(2)}, u32[]{:S(2)}) collective-permute-start(f32[16,768]{1,0:T(8,128)S(1)} %get-tuple-element.65.m0), channel_id=1, source_target_pairs={{0,16},{8,24},{16,0},{24,8},{1,17},{9,25},{17,1},{25,9},{2,18},{10... | collective-permute-start | bytes 147464 | tf_op jit(solution)/shard_map/ppermute | solution.py:21
  33.7 4.2 %collective-permute-start.4 = (f32[16,768]{1,0:T(8,128)S(1)}, f32[16,768]{1,0:T(8,128)S(1)}, u32[]{:S(2)}, u32[]{:S(2)}) collective-permute-start(f32[16,768]{1,0:T(8,128)S(1)} %get-tuple-element.65.m0), channel_id=1, source_target_pairs={{0,8},{8,16},{16,24},{24,0},{1,9},{9,17},{17,25},{25,1},{2,10},{10... | collective-permute-start | bytes 147464 | tf_op jit(solution)/shard_map/ppermute | solution.py:21
  38.0 5.5 %collective-permute-start.7 = (f32[16,448]{1,0:T(8,128)S(1)}, f32[16,448]{1,0:T(8,128)S(1)}, u32[]{:S(2)}, u32[]{:S(2)}) collective-permute-start(f32[16,448]{1,0:T(8,128)S(1)} %get-tuple-element.66), channel_id=1, source_target_pairs={{0,32},{32,64},{64,96},{96,0},{1,33},{33,65},{65,97},{97,1},{2,34}... | collective-permute-start | bytes 86024 | tf_op jit(solution)/shard_map/ppermute | solution.py:21
  38.2 5.4 %collective-permute-start.8 = (f32[16,448]{1,0:T(8,128)S(1)}, f32[16,448]{1,0:T(8,128)S(1)}, u32[]{:S(2)}, u32[]{:S(2)}) collective-permute-start(f32[16,448]{1,0:T(8,128)S(1)} %get-tuple-element.67), channel_id=1, source_target_pairs={{0,64},{32,96},{64,0},{96,32},{1,65},{33,97},{65,1},{97,33},{2,66}... | collective-permute-start | bytes 86024 | tf_op jit(solution)/shard_map/ppermute | solution.py:21
  43.7 8.0 %collective-permute-start.12 = (f32[16,1088]{1,0:T(8,128)S(1)}, f32[16,1088]{1,0:T(8,128)S(1)}, u32[]{:S(2)}, u32[]{:S(2)}) collective-permute-start(f32[16,1088]{1,0:T(8,128)S(1)} %get-tuple-element.71), channel_id=1, source_target_pairs={{0,6},{2,0},{4,2},{6,4},{1,7},{3,1},{5,3},{7,5},{8,14},{10,8},{12,... | collective-permute-start | bytes 208904 | tf_op jit(solution)/shard_map/ppermute | solution.py:21
  45.4 6.3 %collective-permute-start.11 = (f32[16,1088]{1,0:T(8,128)S(1)}, f32[16,1088]{1,0:T(8,128)S(1)}, u32[]{:S(2)}, u32[]{:S(2)}) collective-permute-start(f32[16,1088]{1,0:T(8,128)S(1)} %get-tuple-element.71), channel_id=1, source_target_pairs={{0,4},{2,6},{4,0},{6,2},{1,5},{3,7},{5,1},{7,3},{8,12},{10,14},{12... | collective-permute-start | bytes 208904 | tf_op jit(solution)/shard_map/ppermute | solution.py:21
  46.8 4.9 %collective-permute-start.10 = (f32[16,1088]{1,0:T(8,128)S(1)}, f32[16,1088]{1,0:T(8,128)S(1)}, u32[]{:S(2)}, u32[]{:S(2)}) collective-permute-start(f32[16,1088]{1,0:T(8,128)S(1)} %get-tuple-element.71), channel_id=1, source_target_pairs={{0,2},{2,4},{4,6},{6,0},{1,3},{3,5},{5,7},{7,1},{8,10},{10,12},{12... | collective-permute-start | bytes 208904 | tf_op jit(solution)/shard_map/ppermute | solution.py:21
  51.8 6.4 %collective-permute-start.13 = (f32[4,16,1088]{2,1,0:T(8,128)S(1)}, f32[4,16,1088]{2,1,0:T(8,128)S(1)}, u32[]{:S(2)}, u32[]{:S(2)}) collective-permute-start(f32[4,16,1088]{2,1,0:T(8,128)S(1)} %pad_maximum_fusion.mine), channel_id=1, source_target_pairs={{0,1},{1,0},{2,3},{3,2},{4,5},{5,4},{6,7},{7,6},{8,9},{9,8},{10,11... | collective-permute-start | bytes 835592 | tf_op jit(solution)/shard_map/ppermute | solution.py:25
  61.6 5.4 %collective-permute-start.17 = (f32[3,16,320]{2,1,0:T(8,128)S(1)}, f32[3,16,320]{2,1,0:T(8,128)S(1)}, u32[]{:S(2)}, u32[]{:S(2)}) collective-permute-start(f32[3,16,320]{2,1,0:T(8,128)S(1)} %get-tuple-element.126), channel_id=1, source_target_pairs={{0,6},{2,0},{4,2},{6,4},{1,7},{3,1},{5,3},{7,5},{8,14},{10,8},{12,... | collective-permute-start | bytes 184328 | tf_op jit(solution)/shard_map/ppermute | solution.py:21
  63.9 4.8 %collective-permute-start.16 = (f32[3,16,320]{2,1,0:T(8,128)S(1)}, f32[3,16,320]{2,1,0:T(8,128)S(1)}, u32[]{:S(2)}, u32[]{:S(2)}) collective-permute-start(f32[3,16,320]{2,1,0:T(8,128)S(1)} %get-tuple-element.127), channel_id=1, source_target_pairs={{0,4},{2,6},{4,0},{6,2},{1,5},{3,7},{5,1},{7,3},{8,12},{10,14},{12... | collective-permute-start | bytes 184328 | tf_op jit(solution)/shard_map/ppermute | solution.py:21
  64.3 6.5 %collective-permute-start.15 = (f32[3,16,320]{2,1,0:T(8,128)S(1)}, f32[3,16,320]{2,1,0:T(8,128)S(1)}, u32[]{:S(2)}, u32[]{:S(2)}) collective-permute-start(f32[3,16,320]{2,1,0:T(8,128)S(1)} %get-tuple-element.128), channel_id=1, source_target_pairs={{0,2},{2,4},{4,6},{6,0},{1,3},{3,5},{5,7},{7,1},{8,10},{10,12},{12... | collective-permute-start | bytes 184328 | tf_op jit(solution)/shard_map/ppermute | solution.py:21
  71.5 4.5 %collective-permute-start.19 = (f32[16,768]{1,0:T(8,128)S(1)}, f32[16,768]{1,0:T(8,128)S(1)}, u32[]{:S(2)}, u32[]{:S(2)}) collective-permute-start(f32[16,768]{1,0:T(8,128)S(1)} %get-tuple-element.85.m0), channel_id=1, source_target_pairs={{0,16},{8,24},{16,0},{24,8},{1,17},{9,25},{17,1},{25,9},{2,18},{10... | collective-permute-start | bytes 147464 | tf_op jit(solution)/shard_map/ppermute | solution.py:21
  72.1 4.3 %collective-permute-start.18 = (f32[16,768]{1,0:T(8,128)S(1)}, f32[16,768]{1,0:T(8,128)S(1)}, u32[]{:S(2)}, u32[]{:S(2)}) collective-permute-start(f32[16,768]{1,0:T(8,128)S(1)} %get-tuple-element.85.m0), channel_id=1, source_target_pairs={{0,8},{8,16},{16,24},{24,0},{1,9},{9,17},{17,25},{25,1},{2,10},{10... | collective-permute-start | bytes 147464 | tf_op jit(solution)/shard_map/ppermute | solution.py:21
  76.6 4.3 %collective-permute-start.21 = (f32[16,448]{1,0:T(8,128)S(1)}, f32[16,448]{1,0:T(8,128)S(1)}, u32[]{:S(2)}, u32[]{:S(2)}) collective-permute-start(f32[16,448]{1,0:T(8,128)S(1)} %get-tuple-element.86), channel_id=1, source_target_pairs={{0,32},{32,64},{64,96},{96,0},{1,33},{33,65},{65,97},{97,1},{2,34}... | collective-permute-start | bytes 86024 | tf_op jit(solution)/shard_map/ppermute | solution.py:21
  78.0 4.3 %collective-permute-start.22 = (f32[16,448]{1,0:T(8,128)S(1)}, f32[16,448]{1,0:T(8,128)S(1)}, u32[]{:S(2)}, u32[]{:S(2)}) collective-permute-start(f32[16,448]{1,0:T(8,128)S(1)} %get-tuple-element.87), channel_id=1, source_target_pairs={{0,64},{32,96},{64,0},{96,32},{1,65},{33,97},{65,1},{97,33},{2,66}... | collective-permute-start | bytes 86024 | tf_op jit(solution)/shard_map/ppermute | solution.py:21
  83.2 4.8 %collective-permute-start.25 = (f32[16,1088]{1,0:T(8,128)S(1)}, f32[16,1088]{1,0:T(8,128)S(1)}, u32[]{:S(2)}, u32[]{:S(2)}) collective-permute-start(f32[16,1088]{1,0:T(8,128)S(1)} %get-tuple-element.91), channel_id=1, source_target_pairs={{0,4},{2,6},{4,0},{6,2},{1,5},{3,7},{5,1},{7,3},{8,12},{10,14},{12... | collective-permute-start | bytes 208904 | tf_op jit(solution)/shard_map/ppermute | solution.py:21
  83.8 4.9 %collective-permute-start.24 = (f32[16,1088]{1,0:T(8,128)S(1)}, f32[16,1088]{1,0:T(8,128)S(1)}, u32[]{:S(2)}, u32[]{:S(2)}) collective-permute-start(f32[16,1088]{1,0:T(8,128)S(1)} %get-tuple-element.91), channel_id=1, source_target_pairs={{0,2},{2,4},{4,6},{6,0},{1,3},{3,5},{5,7},{7,1},{8,10},{10,12},{12... | collective-permute-start | bytes 208904 | tf_op jit(solution)/shard_map/ppermute | solution.py:21
  88.8 7.1 %collective-permute-start.27 = (f32[4,16,1088]{2,1,0:T(8,128)S(1)}, f32[4,16,1088]{2,1,0:T(8,128)S(1)}, u32[]{:S(2)}, u32[]{:S(2)}) collective-permute-start(f32[4,16,1088]{2,1,0:T(8,128)S(1)} %pad_maximum_fusion.1.mine), channel_id=1, source_target_pairs={{0,1},{1,0},{2,3},{3,2},{4,5},{5,4},{6,7},{7,6},{8,9},{9,8},{10,11... | collective-permute-start | bytes 835592 | tf_op jit(solution)/shard_map/ppermute | solution.py:25
  99.6 4.5 %collective-permute-start.31 = (f32[3,16,320]{2,1,0:T(8,128)S(1)}, f32[3,16,320]{2,1,0:T(8,128)S(1)}, u32[]{:S(2)}, u32[]{:S(2)}) collective-permute-start(f32[3,16,320]{2,1,0:T(8,128)S(1)} %get-tuple-element.122), channel_id=1, source_target_pairs={{0,6},{2,0},{4,2},{6,4},{1,7},{3,1},{5,3},{7,5},{8,14},{10,8},{12,... | collective-permute-start | bytes 184328 | tf_op jit(solution)/shard_map/ppermute | solution.py:21
  101.4 4.8 %collective-permute-start.30 = (f32[3,16,320]{2,1,0:T(8,128)S(1)}, f32[3,16,320]{2,1,0:T(8,128)S(1)}, u32[]{:S(2)}, u32[]{:S(2)}) collective-permute-start(f32[3,16,320]{2,1,0:T(8,128)S(1)} %get-tuple-element.123), channel_id=1, source_target_pairs={{0,4},{2,6},{4,0},{6,2},{1,5},{3,7},{5,1},{7,3},{8,12},{10,14},{12... | collective-permute-start | bytes 184328 | tf_op jit(solution)/shard_map/ppermute | solution.py:21
  102.1 6.1 %collective-permute-start.29 = (f32[3,16,320]{2,1,0:T(8,128)S(1)}, f32[3,16,320]{2,1,0:T(8,128)S(1)}, u32[]{:S(2)}, u32[]{:S(2)}) collective-permute-start(f32[3,16,320]{2,1,0:T(8,128)S(1)} %get-tuple-element.124), channel_id=1, source_target_pairs={{0,2},{2,4},{4,6},{6,0},{1,3},{3,5},{5,7},{7,1},{8,10},{10,12},{12... | collective-permute-start | bytes 184328 | tf_op jit(solution)/shard_map/ppermute | solution.py:21
  109.5 4.5 %collective-permute-start.33 = (f32[16,768]{1,0:T(8,128)S(1)}, f32[16,768]{1,0:T(8,128)S(1)}, u32[]{:S(2)}, u32[]{:S(2)}) collective-permute-start(f32[16,768]{1,0:T(8,128)S(1)} %get-tuple-element.104.m0), channel_id=1, source_target_pairs={{0,16},{8,24},{16,0},{24,8},{1,17},{9,25},{17,1},{25,9},{2,18},{10... | collective-permute-start | bytes 147464 | tf_op jit(solution)/shard_map/ppermute | solution.py:21
  110.2 4.3 %collective-permute-start.32 = (f32[16,768]{1,0:T(8,128)S(1)}, f32[16,768]{1,0:T(8,128)S(1)}, u32[]{:S(2)}, u32[]{:S(2)}) collective-permute-start(f32[16,768]{1,0:T(8,128)S(1)} %get-tuple-element.104.m0), channel_id=1, source_target_pairs={{0,8},{8,16},{16,24},{24,0},{1,9},{9,17},{17,25},{25,1},{2,10},{10... | collective-permute-start | bytes 147464 | tf_op jit(solution)/shard_map/ppermute | solution.py:21
  114.6 4.0 %collective-permute-start.35 = (f32[16,448]{1,0:T(8,128)S(1)}, f32[16,448]{1,0:T(8,128)S(1)}, u32[]{:S(2)}, u32[]{:S(2)}) collective-permute-start(f32[16,448]{1,0:T(8,128)S(1)} %get-tuple-element.105), channel_id=1, source_target_pairs={{0,32},{32,64},{64,96},{96,0},{1,33},{33,65},{65,97},{97,1},{2,34}... | collective-permute-start | bytes 86024 | tf_op jit(solution)/shard_map/ppermute | solution.py:21
  114.7 4.7 %collective-permute-start.36 = (f32[16,448]{1,0:T(8,128)S(1)}, f32[16,448]{1,0:T(8,128)S(1)}, u32[]{:S(2)}, u32[]{:S(2)}) collective-permute-start(f32[16,448]{1,0:T(8,128)S(1)} %get-tuple-element.106), channel_id=1, source_target_pairs={{0,64},{32,96},{64,0},{96,32},{1,65},{33,97},{65,1},{97,33},{2,66}... | collective-permute-start | bytes 86024 | tf_op jit(solution)/shard_map/ppermute | solution.py:21
  120.7 4.8 %collective-permute-start.39 = (f32[16,1088]{1,0:T(8,128)S(1)}, f32[16,1088]{1,0:T(8,128)S(1)}, u32[]{:S(2)}, u32[]{:S(2)}) collective-permute-start(f32[16,1088]{1,0:T(8,128)S(1)} %get-tuple-element.110), channel_id=1, source_target_pairs={{0,4},{2,6},{4,0},{6,2},{1,5},{3,7},{5,1},{7,3},{8,12},{10,14},{12... | collective-permute-start | bytes 208904 | tf_op jit(solution)/shard_map/ppermute | solution.py:21
  121.2 5.1 %collective-permute-start.38 = (f32[16,1088]{1,0:T(8,128)S(1)}, f32[16,1088]{1,0:T(8,128)S(1)}, u32[]{:S(2)}, u32[]{:S(2)}) collective-permute-start(f32[16,1088]{1,0:T(8,128)S(1)} %get-tuple-element.110), channel_id=1, source_target_pairs={{0,2},{2,4},{4,6},{6,0},{1,3},{3,5},{5,7},{7,1},{8,10},{10,12},{12... | collective-permute-start | bytes 208904 | tf_op jit(solution)/shard_map/ppermute | solution.py:21
  126.3 7.2 %collective-permute-start.41 = (f32[4,16,1088]{2,1,0:T(8,128)S(1)}, f32[4,16,1088]{2,1,0:T(8,128)S(1)}, u32[]{:S(2)}, u32[]{:S(2)}) collective-permute-start(f32[4,16,1088]{2,1,0:T(8,128)S(1)} %pad_maximum_fusion.2.mine), channel_id=1, source_target_pairs={{0,1},{1,0},{2,3},{3,2},{4,5},{5,4},{6,7},{7,6},{8,9},{9,8},{10,11... | collective-permute-start | bytes 835592 | tf_op jit(solution)/shard_map/ppermute | solution.py:25
  (15 other events, 72.9 us)

commit v2 on v1

--- a/solution.py
+++ b/solution.py
@@ -84,7 +84,6 @@
 
 def last_body(r1, r2, r3, local, w, co, v, message):
     group = lax.axis_index("day_0")
-    g0, g1, gg, d1, dg = co[0:1], co[1:2], co[2:3], co[4:5], co[5:6]
     far_f, far_b = jnp.zeros((16, 320), F32), jnp.zeros((16, 320), F32)
     packs = [local[2, :, :128]]
     for k, r in ((1, r1), (2, r2), (3, r3)):
@@ -94,6 +93,11 @@
         far_b = far_b + jnp.where(group >= k, 0.0, value)
     come_f = local[0] + co[23:24] * far_f
     come_b = local[1] + co[24:25] * far_b
+    raise_days(come_f, come_b, w, co, v, message, ring_sum(packs))
+
+
+def raise_days(come_f, come_b, w, co, v, message, pack):
+    g0, g1, gg, d1, dg = co[0:1], co[1:2], co[2:3], co[4:5], co[5:6]
     l0 = w[0] + come_f
     l1 = w[1] + d1 * l0
     u1 = dg * (come_b + gg * w[2])
@@ -102,7 +106,7 @@
     for day, value in enumerate(days):
         v[day] = value
         message[:, day * 320 : day * 320 + 320] = value
-    message[:, 960:] = ring_sum(packs)
+    message[:, 960:] = pack
 
 
 def precondition(w, message, co, early=(), late=()):
@@ -207,25 +211,97 @@
     )
 
 
-def chain_kernel(every, co, gains, decs, steps):
+def pick(values, index):
+    out = jnp.zeros_like(values[0])
+    for place, value in enumerate(values):
+        out = jnp.where(index == place, value, out)
+    return out
+
+
+def put_rows(message, values):
+    for r, value in enumerate(values):
+        for c, width in enumerate((128, 128, 64)):
+            row = 1 + 3 * r + c
+            message[row : row + 1, 640 : 640 + width] = value[:, 128 * c : 128 * c + width]
+
+
+def get_rows(pack):
+    return [
+        jnp.concatenate(
+            [pack[1 + 3 * r : 2 + 3 * r], pack[2 + 3 * r : 3 + 3 * r], pack[3 + 3 * r : 4 + 3 * r, :64]], axis=1
+        )
+        for r in range(4)
+    ]
+
+
+def only_first_row(value):
+    return jnp.where(lax.broadcasted_iota(jnp.int32, value.shape, 0) == 0, value, 0.0)
+
+
+def ordered(kept, messages, place):
+    for k, message in enumerate(messages):
+        kept[k] = message[...]
+    return [kept[lax.rem(place + (4 - j), 4)] for j in range(4)]
+
+
+def first_middle_kernel(m0, m1, m2, m3, *refs):
+    out, ordered_out, kept = refs[-3:]
+    messages = ordered(kept, (m0, m1, m2, m3), lax.axis_index("day_1"))
+    for j, message in enumerate(messages):
+        ordered_out[j] = message
+    pack = ring_sum([m[:, 640:] for m in (m0, m1, m2, m3)])
+    out[:, 640:] = only_first_row(pack)
+    chain = [get_rows(m[:, 640:]) for m in messages]
+    alpha, beta = jnp.zeros((1, 320), F32), jnp.ones((1, 320), F32)
+    alphas = [None] * 4
+    for j in (3, 2, 1, 0):
+        dec0, dec1, dom0, dom1 = chain[j]
+        alphas[j] = alpha
+        const = 1.0 / dom0 + dec1 * dec1 * (1.0 / dom1 + alpha)
+        slope = dec1 * dec1 * beta
+        alpha, beta = dec0 * dec0 * const, dec0 * dec0 * slope
+    moved = jnp.ones((1, 320), F32)
+    total_f = total_p = jnp.zeros((16, 320), F32)
+    for j in range(4):
+        dec0, dec1 = chain[j][:2]
+        f, p = messages[j][:, :320], messages[j][:, 320:640]
+        if j:
+            moved = moved * dec0
+        total_f = f + dec0 * dec1 * total_f
+        total_p = total_p + moved * (p + alphas[j] * dec1 * f)
+        moved = moved * dec1
+    out[:, :320] = total_f
+    out[:, 320:640] = total_p
+    put_rows(out, (moved, const, slope, chain[0][0]))
+
+
+def first_last_kernel(z0, z1, z2, z3, near, bx, *refs):
+    co, w, v, message, kept = refs[-5:]
     group, place = lax.axis_index("day_0"), lax.axis_index("day_1")
-    me = 4 * group + place
     zero, one = jnp.zeros((1, 320), F32), jnp.ones((1, 320), F32)
-    follow = [every[day // 2, day % 2 : day % 2 + 1, :] for day in range(32)] + [zero]
-    gain = zero
-    for day in range(32, -1, -1):
-        if day < 32:
-            inverse = 1.0 / every[day // 2, 2 + day % 2 : 3 + day % 2, :]
-            gain = inverse + follow[day + 1] * follow[day + 1] * gain
-        gains[day : day + 1] = gain
-        decs[day : day + 1] = follow[day]
-    for device in range(16):
-        steps[device : device + 1] = follow[2 * device + 1] * follow[2 * device + 2]
-    mine = [steps[pl.ds(4 * group + device, 1), :] for device in range(4)]
-    whole = []
-    for other in range(4):
-        rows = [steps[4 * other + device : 4 * other + device + 1] for device in range(4)]
-        whole.append(rows[0] * rows[1] * rows[2] * rows[3])
+    groups = ordered(kept, (z0, z1, z2, z3), group)
+    chain = [get_rows(near[j, :, 640:]) for j in range(4)]
+    whole_chain = [get_rows(m[:, 640:]) for m in groups]
+    moved = [c[0] for c in whole_chain]
+    first_decay = [c[3] for c in whole_chain] + [zero]
+    exits, entry = [zero] * 4, [zero] * 5
+    for g in (3, 2, 1, 0):
+        entry[g] = whole_chain[g][1] + whole_chain[g][2] * exits[g]
+        if g:
+            exits[g - 1] = first_decay[g] * first_decay[g] * entry[g]
+    dec0 = [c[0] for c in chain]
+    dec1 = [c[1] for c in chain]
+    after_decay = dec0[1:] + [pick(first_decay[1:], group)]
+    gain0, gain1, after_gain = [None] * 4, [None] * 4, [None] * 4
+    beyond = pick(exits, group)
+    for j in (3, 2, 1, 0):
+        after_gain[j] = beyond
+        gain1[j] = 1.0 / chain[j][3] + beyond
+        gain0[j] = 1.0 / chain[j][2] + dec1[j] * dec1[j] * gain1[j]
+        beyond = dec0[j] * dec0[j] * gain0[j]
+    next_gain = gain0[1:] + [pick(entry[1:], group)]
+    mine = [dec1[j] * after_decay[j] for j in range(4)]
+    whole = [moved[g] * first_decay[g + 1] for g in range(4)]
 
     def product(factors, low, high):
         kept = [
@@ -234,8 +310,7 @@
         ]
         return kept[0] * kept[1] * kept[2] * kept[3]
 
-    rows = [gains[pl.ds(2 * me + day, 1), :] for day in range(3)]
-    rows += [decs[pl.ds(2 * me + day, 1), :] for day in range(3)]
+    rows = [pick(values, place) for values in (gain0, gain1, next_gain, dec0, dec1, after_decay)]
     local_f, local_b, total_f, total_b, far = [], [], [], [], []
     for k in range(4):
         source = lax.rem(place + (4 - k), 4)
@@ -246,20 +321,46 @@
             local_b.append(jnp.where(source > place, product(mine, place + 1, source), zero))
             origin = lax.rem(group + (4 - k), 4)
             far.append(product(whole, jnp.minimum(origin, group) + 1, jnp.maximum(origin, group)))
-    rows += local_f + local_b + total_f + total_b + far
-    rows += [product(mine, 0, place), product(mine, place + 1, 4)]
+    before, after = product(mine, 0, place), product(mine, place + 1, 4)
+    rows += local_f + local_b + total_f + total_b + far + [before, after]
     for index, row in enumerate(rows):
         co[index : index + 1] = row
 
-
-def chain_coefficients(every):
-    return call(
-        chain_kernel,
-        "chain",
-        shaped(25, 320),
-        [VMEM_BLOCK],
-        every,
-        scratch=[pltpu.VMEM((40, 320), F32), pltpu.VMEM((40, 320), F32), pltpu.VMEM((16, 320), F32)],
+    come_f = come_b = far_f = far_b = jnp.zeros((16, 320), F32)
+    for j in range(4):
+        f, p = near[j, :, :320], near[j, :, 320:640]
+        ahead = after_decay[j] * f
+        behind = p + after_gain[j] * dec1[j] * f
+        come_f = come_f + jnp.where(j < place, product(mine, j + 1, place) * ahead, 0.0)
+        come_b = come_b + jnp.where(j > place, product(mine, place + 1, j) * behind, 0.0)
+        f, p = groups[j][:, :320], groups[j][:, 320:640]
+        ahead = first_decay[j + 1] * f
+        behind = p + exits[j] * moved[j] * f
+        far_f = far_f + jnp.where(j < group, product(whole, j + 1, group) * ahead, 0.0)
+        far_b = far_b + jnp.where(j > group, product(whole, group + 1, j) * behind, 0.0)
+    w[0], w[1], w[2] = bx[0], bx[1], jnp.zeros((16, 320), F32)
+    pack = only_first_row(ring_sum([z[:, 640:] for z in (z0, z1, z2, z3)]))
+    raise_days(come_f + before * far_f, come_b + after * far_b, w, co, v, message, pack)
+
+
+def first_precondition(bx, message, early, late):
+    pieces = ring_gather(message, "day_1")
+    out, near = call(
+        first_middle_kernel,
+        "first_middle",
+        (shaped(16, 768), shaped(4, 16, 768)),
+        [VMEM_BLOCK] * 4 + [ANY_BLOCK],
+        *pieces, early,
+        scratch=[pltpu.VMEM((4, 16, 768), F32)],
+    )
+    field = shaped(3, 16, 320)
+    return call(
+        first_last_kernel,
+        "first_last",
+        (shaped(25, 320), field, field, shaped(16, 1088)),
+        [VMEM_BLOCK] * 6 + [ANY_BLOCK],
+        *ring_gather(out, "day_0"), near, bx, late,
+        scratch=[pltpu.VMEM((4, 16, 768), F32)],
     )
 
 
@@ -322,26 +423,26 @@
     )
 
 
-def start_kernel(p0, p1, p2, p3, probes, grad_cov, co, *refs):
-    bx, w, message = refs[-3:]
+def start_kernel(p0, p1, p2, p3, probes, grad_cov, own_chain, *refs):
+    bx, message = refs[-2:]
     grad = ring_sum([p0[...], p1[...], p2[...], p3[...]])
     for day in range(2):
         bx[day, 0:1] = grad[day : day + 1]
         bx[day, 1:16] = probes[:, day, :]
-        w[day] = bx[day]
-    w[2] = jnp.zeros((16, 320), F32)
-    ahead, behind = ring_message(w, co)
+    dec1 = own_chain[1:2]
+    ahead = bx[1] + dec1 * bx[0]
     message[:, :320] = ahead
-    message[:, 320:640] = behind
+    message[:, 320:640] = bx[0] / own_chain[2:3] + dec1 * ahead / own_chain[3:4]
     message[:, 640:] = jnp.zeros((16, 128), F32)
     message[0:1, 640:704] = grad_cov[...]
+    put_rows(message, [own_chain[r : r + 1] for r in range(4)])
 
 
 def start_stage(*operands):
     return call(
         start_kernel,
         "start_stage",
-        (shaped(2, 16, 320), shaped(3, 16, 320), shaped(16, 768)),
+        (shaped(2, 16, 320), shaped(16, 768)),
         [VMEM_BLOCK] * 7 + [ANY_BLOCK] * (len(operands) - 7),
         *operands,
     )
@@ -585,7 +686,7 @@
     )
 
 
-def setup_kernel(count, vertices, bary, prec, value, covs, after, spread, weight, kept, sent, grad_cov, covariates):
+def setup_kernel(count, vertices, bary, prec, value, covs, spread, weight, kept, sent, grad_cov, covariates):
     core = lax.axis_index("blk_1")
     slot_start = (lax.axis_index("blk_0") * 2 + core) * 128
     cov_sum = jnp.zeros((1, 64), F32)
@@ -622,10 +723,9 @@
             pltpu.VMEM((2, 2560, 256), BF16), shaped(2, 128), shaped(4, 2, 320), shaped(4, 2, 320),
             shaped(1, 64), pltpu.VMEM((2, 128, 128), BF16),
         ),
-        [SMEM_BLOCK] + [whole_block(o) for o in operands[1:-1]] + [ANY_BLOCK],
+        [SMEM_BLOCK] + [whole_block(o) for o in operands[1:]],
         operands[0],
-        *(pltpu.with_memory_space_constraint(o, pltpu.HBM) for o in operands[1:-1]),
-        operands[-1],
+        *(pltpu.with_memory_space_constraint(o, pltpu.HBM) for o in operands[1:]),
         grid=(1,),
     )
 
@@ -651,21 +751,19 @@
     columns = lax.broadcasted_iota(jnp.int32, (2, 320, 320), 2)
     dominant = jnp.sum(jnp.where(rows == columns, square, 0.0), axis=1)
     both = jnp.concatenate([1.0 - leakage, dominant])
-    every = lax.all_to_all(jnp.broadcast_to(both, (16, 4, 320)), DAY, 0, 0, tiled=True)
-    co = chain_coefficients(every)
 
     vertices = triangles[:, obs_triangle]
     spread, weight, kept, sent, grad_cov, covs = setup_stage(
-        obs_count, vertices, obs_bary, obs_prec, obs_value, covariates, co
+        obs_count, vertices, obs_bary, obs_prec, obs_value, covariates
     )
     off_pair = [split_blocks(off_blocks, "split_off", day) for day in range(2)]
     diag_pair = [split_blocks(diag_blocks, "split_diag", day) for day in range(2)]
-    bx, w0, message = start_stage(*scattered_pieces(kept, sent), probes, grad_cov, co, off_pair[0])
+    bx, message = start_stage(*scattered_pieces(kept, sent), probes, grad_cov, both, off_pair[0])
     prior = prior_prec[None]
     padded_cov = jnp.pad(probes_cov, ((1, 0), (0, 0)))
 
     pairs = (*diag_pair, *off_pair)
-    v1, message = precondition(w0, message, co, (off_pair[1],), (diag_pair[0],))
+    co, _, v1, message = first_precondition(bx, message, off_pair[1], diag_pair[0])
     nodes, behind1 = gather_nodes(message, own_terms(pairs, v1))
     kept, sent, cov1, whole1, c0 = first_stage(
         *nodes, padded_cov, spread, covs, weight, behind1

time: 153 us -> 144 us (0.941)
  starting transfers between devices: 60.8 us -> 54.9 us
  waiting for transfers between devices: 38.2 us -> 34.8 us
    all_to_all x1 -> x0, starting transfers between devices: 8.43 us -> none  [on_device(): lax.all_to_all(jnp.broadcast_to(both, (16, 4, 320)), DAY, 0, 0, tiled=True)]
    ppermute x36, starting transfers between devices: 32.2 us -> 35.7 us  [shift(): lax.ppermute(value, axis, [(i, (i + distance) % size) for i in range(size)])]
    all_to_all x1 -> x0, waiting for transfers between devices: 2.97 us -> none  [on_device(): lax.all_to_all(jnp.broadcast_to(both, (16, 4, 320)), DAY, 0, 0, tiled=True)]
    pallas_call x23 -> x22, Pallas kernels: 31.1 us -> 32 us  [call(): pl.pallas_call(kernel, grid=grid, out_shape=outs, in_specs=in_specs, out_...]
  transfers between devices with their start and end apart: 43 -> 42, of which waited for: 31 -> 32; matrix products, arithmetic and copies ran while one was open for 2% -> 2% of each run, Pallas kernels for 12% -> 13%
where the time goes in v2:
time: 144 us
  starting transfers between devices  54.9 us (38%)
  waiting for transfers between devices  34.8 us (24%)
  Pallas kernels  32 us (22%)
  blocking collectives  14.3 us (10%)
  local copies, waits for them, and re-layouts  3.81 us (3%)
  other arithmetic  3.02 us (2%)
    ppermute x36, starting transfers between devices, shift(): lax.ppermute(value, axis, [(i, (i + distance) % size) for i in range(size)])  35.7 us
    pallas_call x22, Pallas kernels, call(): pl.pallas_call(kernel, grid=grid, out_shape=outs, in_specs=in_specs, out_...  32 us
    ppermute x36, waiting for transfers between devices, shift(): lax.ppermute(value, axis, [(i, (i + distance) % size) for i in range(size)])  28.8 us
    ppermute x6, starting transfers between devices, swapped(): return lax.ppermute(value, 'blk_1', [(0, 1), (1, 0)])  19.2 us
    all_to_all x1, blocking collectives, on_device(): sums = lax.all_to_all(sums, DAY + BLK, 0, 0, tiled=True)  14.3 us
    ppermute x6, waiting for transfers between devices, swapped(): return lax.ppermute(value, 'blk_1', [(0, 1), (1, 0)])  6.04 us
  transfers between devices with their start and end apart: 42, of which 32 were waited for; matrix products, arithmetic and copies ran while one was open for 2% of the time, Pallas kernels for 13%

profile of v2, /device:TPU:1, one launch (start us, length us, event | category | flops | bytes accessed | tf_op | source)
XLA Modules:
  0.0 143.8 jit_solution(11948591546545785235)
XLA Ops:
  1.3 1.7 %copy.17 = s32[3,5116]{0,1:T(8,128)S(1)} copy(s32[3,5116]{1,0:T(4,128)} %param.22) | data formatting | bytes 122784 | tf_op args[9]
  5.0 2.9 %setup_stage.1 = (bf16[2,2560,256]{2,1,0:T(8,128)(2,1)S(1)}, f32[2,128]{1,0:T(2,128)S(1)}, f32[4,2,320]{2,1,0:T(2,128)S(1)}, f32[4,2,320]{2,1,0:T(2,128)S(1)}, f...) custom-call(s32[2]{0:T(128)S(1)} %copy-done.2, s32[3,2,128]{2,1,0:T(2,128)} %bitcast.62, f32[3,2,128]{2,1,0:T(2,128)} %bary.1, ...), custom_call_target="tpu_custom_call" | custom-call | tf_op jit(solution)/shard_map/setup_stage/pallas_call | solution.py:169
  11.7 2.8 %collective-permute-start.3 = (f32[2,320]{1,0:T(2,128)S(1)}, f32[2,320]{1,0:T(2,128)S(1)}, u32[]{:S(2)}, u32[]{:S(2)}) collective-permute-start(f32[2,320]{1,0:T(2,128)S(1)} %get-tuple-element.126), channel_id=1, source_target_pairs={{0,6},{2,0},{4,2},{6,4},{1,7},{3,1},{5,3},{7,5},{8,14},{10,8},{12,... | collective-permute-start | bytes 7688 | tf_op jit(solution)/shard_map/ppermute | solution.py:21
  15.7 2.6 %split_off0.1.refs_0_.o0 = bf16[640,2560]{1,0:T(8,128)(2,1)S(1)} custom-call(f32[2,320,2560]{2,1,0:T(8,128)} %source.5), custom_call_target="tpu_custom_call" | custom-call | tf_op jit(solution)/shard_map/split_off0/pallas_call | solution.py:169
  18.7 2.5 %collective-permute-start.6 = (f32[16,768]{1,0:T(8,128)S(1)}, f32[16,768]{1,0:T(8,128)S(1)}, u32[]{:S(2)}, u32[]{:S(2)}) collective-permute-start(f32[16,768]{1,0:T(8,128)S(1)} %get-tuple-element.63.m0), channel_id=1, source_target_pairs={{0,24},{8,0},{16,8},{24,16},{1,25},{9,1},{17,9},{25,17},{2,26},{10... | collective-permute-start | bytes 147464 | tf_op jit(solution)/shard_map/ppermute | solution.py:21
  22.3 2.6 %split_off1.1.refs_0_.o1 = bf16[640,2560]{1,0:T(8,128)(2,1)S(1)} custom-call(f32[2,320,2560]{2,1,0:T(8,128)} %source.5), custom_call_target="tpu_custom_call" | custom-call | tf_op jit(solution)/shard_map/split_off1/pallas_call | solution.py:169
  26.5 3.8 %collective-permute-start.9 = (f32[16,768]{1,0:T(8,128)S(1)}, f32[16,768]{1,0:T(8,128)S(1)}, u32[]{:S(2)}, u32[]{:S(2)}) collective-permute-start(f32[16,768]{1,0:T(8,128)S(1)} %get-tuple-element.64.z0), channel_id=1, source_target_pairs={{0,96},{32,0},{64,32},{96,64},{1,97},{33,1},{65,33},{97,65},{2,98}... | collective-permute-start | bytes 147464 | tf_op jit(solution)/shard_map/ppermute | solution.py:21
  31.0 2.6 %split_diag0.1.refs_0_.a0 = bf16[640,2560]{1,0:T(8,128)(2,1)S(1)} custom-call(f32[2,320,2560]{2,1,0:T(8,128)} %source.7), custom_call_target="tpu_custom_call" | custom-call | tf_op jit(solution)/shard_map/split_diag0/pallas_call | solution.py:169
  36.0 1.7 %collective-permute-start.12 = (f32[16,1088]{1,0:T(8,128)S(1)}, f32[16,1088]{1,0:T(8,128)S(1)}, u32[]{:S(2)}, u32[]{:S(2)}) collective-permute-start(f32[16,1088]{1,0:T(8,128)S(1)} %get-tuple-element.67), channel_id=1, source_target_pairs={{0,6},{2,0},{4,2},{6,4},{1,7},{3,1},{5,3},{7,5},{8,14},{10,8},{12,... | collective-permute-start | bytes 208904 | tf_op jit(solution)/shard_map/ppermute | solution.py:21
  39.0 2.6 %split_diag1.1.a1 = bf16[640,2560]{1,0:T(8,128)(2,1)S(1)} custom-call(f32[2,320,2560]{2,1,0:T(8,128)} %source.7), custom_call_target="tpu_custom_call" | custom-call | tf_op jit(solution)/shard_map/split_diag1/pallas_call | solution.py:169
  41.6 2.2 %own_terms.2.behind.behind1 = f32[3,16,2560]{2,1,0:T(8,128)S(1)} custom-call(bf16[640,2560]{1,0:T(8,128)(2,1)S(1)} %split_diag0.1.refs_0_.a0, bf16[640,2560]{1,0:T(8,128)(2,1)S(1)} %split_diag1.1.a1, bf16[640,2560]{1,0:T(8,128)(2,1)S(1)} %split_off0.1.refs_0_.o0, bf16[640,2560]{1,0:T(8,128)(2,1)S(1)} %split_off1.1.refs_0_.o1, ...), custom_call_target="tpu_custom_call" | custom-call | tf_op jit(solution)/shard_map/own_terms/pallas_call | solution.py:169
  44.0 5.3 %collective-permute-start.13 = (f32[4,16,1088]{2,1,0:T(8,128)S(1)}, f32[4,16,1088]{2,1,0:T(8,128)S(1)}, u32[]{:S(2)}, u32[]{:S(2)}) collective-permute-start(f32[4,16,1088]{2,1,0:T(8,128)S(1)} %pad_maximum_fusion.mine), channel_id=1, source_target_pairs={{0,1},{1,0},{2,3},{3,2},{4,5},{5,4},{6,7},{7,6},{8,9},{9,8},{10,11... | collective-permute-start | bytes 835592 | tf_op jit(solution)/shard_map/ppermute | solution.py:25
  53.9 2.4 %collective-permute-start.17 = (f32[3,16,320]{2,1,0:T(8,128)S(1)}, f32[3,16,320]{2,1,0:T(8,128)S(1)}, u32[]{:S(2)}, u32[]{:S(2)}) collective-permute-start(f32[3,16,320]{2,1,0:T(8,128)S(1)} %get-tuple-element.122), channel_id=1, source_target_pairs={{0,6},{2,0},{4,2},{6,4},{1,7},{3,1},{5,3},{7,5},{8,14},{10,8},{12,... | collective-permute-start | bytes 184328 | tf_op jit(solution)/shard_map/ppermute | solution.py:21
  57.2 2.0 %first_rows.1 = (f32[2,16,320]{2,1,0:T(8,128)S(1)}, f32[16,64]{1,0:T(8,128)S(1)}) custom-call(bf16[640,2560]{1,0:T(8,128)(2,1)S(1)} %split_off0.1.refs_0_.o0, bf16[640,2560]{1,0:T(8,128)(2,1)S(1)} %split_off1.1.refs_0_.o1, f32[3,16,2560]{2,1,0:T(8,128)S(1)} %get-tuple-element.76.whole.whole1, f32[2,16,320]{2,1,0:T(8,128)S(1)} %get-tuple-element.66.bx, ...), custom_call_target="tpu_custom_call" | custom-call | tf_op jit(solution)/shard_map/first_rows/pallas_call | solution.py:169
  59.3 1.8 %collective-permute-done.16.p2 = f32[3,16,320]{2,1,0:T(8,128)S(1)} collective-permute-done((f32[3,16,320]{2,1,0:T(8,128)S(1)}, f32[3,16,320]{2,1,0:T(8,128)S(1)}, u32[]{:S(2)}, u32[]{:S(2)}) %collective-permute-start.16) | collective-permute-done | bytes 61472 | tf_op jit(solution)/shard_map/ppermute | solution.py:21
  61.0 2.0 %collective-permute-done.15.p1 = f32[3,16,320]{2,1,0:T(8,128)S(1)} collective-permute-done((f32[3,16,320]{2,1,0:T(8,128)S(1)}, f32[3,16,320]{2,1,0:T(8,128)S(1)}, u32[]{:S(2)}, u32[]{:S(2)}) %collective-permute-start.15) | collective-permute-done | bytes 61472 | tf_op jit(solution)/shard_map/ppermute | solution.py:21
  66.2 1.8 %collective-permute-done.19.m2 = f32[16,768]{1,0:T(8,128)S(1)} collective-permute-done((f32[16,768]{1,0:T(8,128)S(1)}, f32[16,768]{1,0:T(8,128)S(1)}, u32[]{:S(2)}, u32[]{:S(2)}) %collective-permute-start.19) | collective-permute-done | bytes 49184 | tf_op jit(solution)/shard_map/ppermute | solution.py:21
  69.1 1.7 %collective-permute-start.22 = (f32[16,448]{1,0:T(8,128)S(1)}, f32[16,448]{1,0:T(8,128)S(1)}, u32[]{:S(2)}, u32[]{:S(2)}) collective-permute-start(f32[16,448]{1,0:T(8,128)S(1)} %get-tuple-element.83), channel_id=1, source_target_pairs={{0,64},{32,96},{64,0},{96,32},{1,65},{33,97},{65,1},{97,33},{2,66}... | collective-permute-start | bytes 86024 | tf_op jit(solution)/shard_map/ppermute | solution.py:21
  70.8 1.8 %collective-permute-start.23 = (f32[16,448]{1,0:T(8,128)S(1)}, f32[16,448]{1,0:T(8,128)S(1)}, u32[]{:S(2)}, u32[]{:S(2)}) collective-permute-start(f32[16,448]{1,0:T(8,128)S(1)} %get-tuple-element.84), channel_id=1, source_target_pairs={{0,96},{32,0},{64,32},{96,64},{1,97},{33,1},{65,33},{97,65},{2,98}... | collective-permute-start | bytes 86024 | tf_op jit(solution)/shard_map/ppermute | solution.py:21
  75.6 2.3 %own_terms.3.behind2 = f32[3,16,2560]{2,1,0:T(8,128)S(1)} custom-call(bf16[640,2560]{1,0:T(8,128)(2,1)S(1)} %split_diag0.1.refs_0_.a0, bf16[640,2560]{1,0:T(8,128)(2,1)S(1)} %split_diag1.1.a1, bf16[640,2560]{1,0:T(8,128)(2,1)S(1)} %split_off0.1.refs_0_.o0, bf16[640,2560]{1,0:T(8,128)(2,1)S(1)} %split_off1.1.refs_0_.o1, ...), custom_call_target="tpu_custom_call" | custom-call | tf_op jit(solution)/shard_map/own_terms/pallas_call | solution.py:169
  79.8 5.8 %collective-permute-start.27 = (f32[4,16,1088]{2,1,0:T(8,128)S(1)}, f32[4,16,1088]{2,1,0:T(8,128)S(1)}, u32[]{:S(2)}, u32[]{:S(2)}) collective-permute-start(f32[4,16,1088]{2,1,0:T(8,128)S(1)} %pad_maximum_fusion.1.mine), channel_id=1, source_target_pairs={{0,1},{1,0},{2,3},{3,2},{4,5},{5,4},{6,7},{7,6},{8,9},{9,8},{10,11... | collective-permute-start | bytes 835592 | tf_op jit(solution)/shard_map/ppermute | solution.py:25
  86.8 2.0 %second_stage.1 = (f32[4,3,16,320]{3,2,1,0:T(8,128)S(1)}, f32[4,3,16,320]{3,2,1,0:T(8,128)S(1)}, f32[16,64]{1,0:T(8,128)S(1)}, f32[3,16,2560]{2,1,0:T(8,128)S(1)...) custom-call(f32[4,16,1088]{2,1,0:T(8,128)S(1)} %pad_maximum_fusion.1.mine, ...), custom_call_target="tpu_custom_call" | custom-call | tf_op jit(solution)/shard_map/second_stage/pallas_call | solution.py:169
  90.5 1.6 %collective-permute-start.31 = (f32[3,16,320]{2,1,0:T(8,128)S(1)}, f32[3,16,320]{2,1,0:T(8,128)S(1)}, u32[]{:S(2)}, u32[]{:S(2)}) collective-permute-start(f32[3,16,320]{2,1,0:T(8,128)S(1)} %get-tuple-element.118), channel_id=1, source_target_pairs={{0,6},{2,0},{4,2},{6,4},{1,7},{3,1},{5,3},{7,5},{8,14},{10,8},{12,... | collective-permute-start | bytes 184328 | tf_op jit(solution)/shard_map/ppermute | solution.py:21
  92.8 2.0 %second_rows.1 = (f32[2,16,320]{2,1,0:T(8,128)S(1)}, f32[16,64]{1,0:T(8,128)S(1)}, f32[3,16,320]{2,1,0:T(8,128)S(1)}, f32[3,16,320]{2,1,0:T(8,128)S(1)}) custom-call(bf16[640,2560]{1,0:T(8,128)(2,1)S(1)} %split_off0.1.refs_0_.o0, bf16[640,2560]{1,0:T(8,128)(2,1)S(1)} %split_off1.1.refs_0_.o1, f32[3,16,2560]{2,1,0:T(8,128)S(1)} %get-tuple-element.94.whole.z1whole, ...), custom_call_target="tpu_custom_call" | custom-call | tf_op jit(solution)/shard_map/second_rows/pallas_call | solution.py:169
  94.9 2.0 %collective-permute-done.30.p2 = f32[3,16,320]{2,1,0:T(8,128)S(1)} collective-permute-done((f32[3,16,320]{2,1,0:T(8,128)S(1)}, f32[3,16,320]{2,1,0:T(8,128)S(1)}, u32[]{:S(2)}, u32[]{:S(2)}) %collective-permute-start.30) | collective-permute-done | bytes 61472 | tf_op jit(solution)/shard_map/ppermute | solution.py:21
  96.9 1.9 %collective-permute-done.29.p1 = f32[3,16,320]{2,1,0:T(8,128)S(1)} collective-permute-done((f32[3,16,320]{2,1,0:T(8,128)S(1)}, f32[3,16,320]{2,1,0:T(8,128)S(1)}, u32[]{:S(2)}, u32[]{:S(2)}) %collective-permute-start.29) | collective-permute-done | bytes 61472 | tf_op jit(solution)/shard_map/ppermute | solution.py:21
  102.0 2.6 %collective-permute-done.33.m2 = f32[16,768]{1,0:T(8,128)S(1)} collective-permute-done((f32[16,768]{1,0:T(8,128)S(1)}, f32[16,768]{1,0:T(8,128)S(1)}, u32[]{:S(2)}, u32[]{:S(2)}) %collective-permute-start.33) | collective-permute-done | bytes 49184 | tf_op jit(solution)/shard_map/ppermute | solution.py:21
  106.7 2.7 %collective-permute-start.36 = (f32[16,448]{1,0:T(8,128)S(1)}, f32[16,448]{1,0:T(8,128)S(1)}, u32[]{:S(2)}, u32[]{:S(2)}) collective-permute-start(f32[16,448]{1,0:T(8,128)S(1)} %get-tuple-element.102), channel_id=1, source_target_pairs={{0,64},{32,96},{64,0},{96,32},{1,65},{33,97},{65,1},{97,33},{2,66}... | collective-permute-start | bytes 86024 | tf_op jit(solution)/shard_map/ppermute | solution.py:21
  114.1 2.0 %collective-permute-done.40 = f32[16,1088]{1,0:T(8,128)S(1)} collective-permute-done((f32[16,1088]{1,0:T(8,128)S(1)}, f32[16,1088]{1,0:T(8,128)S(1)}, u32[]{:S(2)}, u32[]{:S(2)}) %collective-permute-start.40) | collective-permute-done | bytes 69664 | tf_op jit(solution)/shard_map/ppermute | solution.py:21
  118.3 5.7 %collective-permute-start.41 = (f32[4,16,1088]{2,1,0:T(8,128)S(1)}, f32[4,16,1088]{2,1,0:T(8,128)S(1)}, u32[]{:S(2)}, u32[]{:S(2)}) collective-permute-start(f32[4,16,1088]{2,1,0:T(8,128)S(1)} %pad_maximum_fusion.2.mine), channel_id=1, source_target_pairs={{0,1},{1,0},{2,3},{3,2},{4,5},{5,4},{6,7},{7,6},{8,9},{9,8},{10,11... | collective-permute-start | bytes 835592 | tf_op jit(solution)/shard_map/ppermute | solution.py:25
  125.2 3.2 %third_stage.1 = (f32[128,128]{1,0:T(8,128)S(1)}, f32[2,16,320]{2,1,0:T(8,128)S(1)}, f32[2,16,320]{2,1,0:T(8,128)S(1)}, f32[16,128]{1,0:T(8,128)S(1)}, f32[2,16,64]{2,1,0:T(8,128)S(1)}) custom-call(f32[4,16,1088]{2,1,0:T(8,128)S(1)} %pad_maximum_fusion.2.mine, f32[4,16,1088]{2,1,0:T(8,128)S(1)} %collective-permute-done.41.other, ...), custom_call_target="tpu_custom_call" | custom-call | tf_op jit(solution)/shard_map/third_stage/pallas_call | solution.py:169
  128.4 14.3 %all_to_all.11 = f32[128,1,128]{2,1,0:T(1,128)S(1)} all-to-all(f32[128,1,128]{2,1,0:T(1,128)S(1)} %bitcast.49), channel_id=1, replica_groups=mesh['day_0'=4,'day_1'=4,'blk_0'=4,'blk_1'=2] {'day_0','day_1','blk_0','..., dimensions={0} | all-to-all | bytes 131072 | tf_op jit(solution)/shard_map/all_to_all | solution.py:787
  (101 shorter events, 47.8 us)
Async XLA Ops:
  11.7 6.6 %collective-permute-start.3 = (f32[2,320]{1,0:T(2,128)S(1)}, f32[2,320]{1,0:T(2,128)S(1)}, u32[]{:S(2)}, u32[]{:S(2)}) collective-permute-start(f32[2,320]{1,0:T(2,128)S(1)} %get-tuple-element.126), channel_id=1, source_target_pairs={{0,6},{2,0},{4,2},{6,4},{1,7},{3,1},{5,3},{7,5},{8,14},{10,8},{12,... | collective-permute-start | bytes 7688 | tf_op jit(solution)/shard_map/ppermute | solution.py:21
  14.5 4.0 %collective-permute-start.2 = (f32[2,320]{1,0:T(2,128)S(1)}, f32[2,320]{1,0:T(2,128)S(1)}, u32[]{:S(2)}, u32[]{:S(2)}) collective-permute-start(f32[2,320]{1,0:T(2,128)S(1)} %get-tuple-element.127), channel_id=1, source_target_pairs={{0,4},{2,6},{4,0},{6,2},{1,5},{3,7},{5,1},{7,3},{8,12},{10,14},{12... | collective-permute-start | bytes 7688 | tf_op jit(solution)/shard_map/ppermute | solution.py:21
  18.7 6.2 %collective-permute-start.6 = (f32[16,768]{1,0:T(8,128)S(1)}, f32[16,768]{1,0:T(8,128)S(1)}, u32[]{:S(2)}, u32[]{:S(2)}) collective-permute-start(f32[16,768]{1,0:T(8,128)S(1)} %get-tuple-element.63.m0), channel_id=1, source_target_pairs={{0,24},{8,0},{16,8},{24,16},{1,25},{9,1},{17,9},{25,17},{2,26},{10... | collective-permute-start | bytes 147464 | tf_op jit(solution)/shard_map/ppermute | solution.py:21
  21.2 4.5 %collective-permute-start.5 = (f32[16,768]{1,0:T(8,128)S(1)}, f32[16,768]{1,0:T(8,128)S(1)}, u32[]{:S(2)}, u32[]{:S(2)}) collective-permute-start(f32[16,768]{1,0:T(8,128)S(1)} %get-tuple-element.63.m0), channel_id=1, source_target_pairs={{0,16},{8,24},{16,0},{24,8},{1,17},{9,25},{17,1},{25,9},{2,18},{10... | collective-permute-start | bytes 147464 | tf_op jit(solution)/shard_map/ppermute | solution.py:21
  21.7 4.5 %collective-permute-start.4 = (f32[16,768]{1,0:T(8,128)S(1)}, f32[16,768]{1,0:T(8,128)S(1)}, u32[]{:S(2)}, u32[]{:S(2)}) collective-permute-start(f32[16,768]{1,0:T(8,128)S(1)} %get-tuple-element.63.m0), channel_id=1, source_target_pairs={{0,8},{8,16},{16,24},{24,0},{1,9},{9,17},{17,25},{25,1},{2,10},{10... | collective-permute-start | bytes 147464 | tf_op jit(solution)/shard_map/ppermute | solution.py:21
  26.5 7.1 %collective-permute-start.9 = (f32[16,768]{1,0:T(8,128)S(1)}, f32[16,768]{1,0:T(8,128)S(1)}, u32[]{:S(2)}, u32[]{:S(2)}) collective-permute-start(f32[16,768]{1,0:T(8,128)S(1)} %get-tuple-element.64.z0), channel_id=1, source_target_pairs={{0,96},{32,0},{64,32},{96,64},{1,97},{33,1},{65,33},{97,65},{2,98}... | collective-permute-start | bytes 147464 | tf_op jit(solution)/shard_map/ppermute | solution.py:21
  30.3 4.5 %collective-permute-start.8 = (f32[16,768]{1,0:T(8,128)S(1)}, f32[16,768]{1,0:T(8,128)S(1)}, u32[]{:S(2)}, u32[]{:S(2)}) collective-permute-start(f32[16,768]{1,0:T(8,128)S(1)} %get-tuple-element.64.z0), channel_id=1, source_target_pairs={{0,64},{32,96},{64,0},{96,32},{1,65},{33,97},{65,1},{97,33},{2,66}... | collective-permute-start | bytes 147464 | tf_op jit(solution)/shard_map/ppermute | solution.py:21
  30.3 4.7 %collective-permute-start.7 = (f32[16,768]{1,0:T(8,128)S(1)}, f32[16,768]{1,0:T(8,128)S(1)}, u32[]{:S(2)}, u32[]{:S(2)}) collective-permute-start(f32[16,768]{1,0:T(8,128)S(1)} %get-tuple-element.64.z0), channel_id=1, source_target_pairs={{0,32},{32,64},{64,96},{96,0},{1,33},{33,65},{65,97},{97,1},{2,34}... | collective-permute-start | bytes 147464 | tf_op jit(solution)/shard_map/ppermute | solution.py:21
  36.0 7.9 %collective-permute-start.12 = (f32[16,1088]{1,0:T(8,128)S(1)}, f32[16,1088]{1,0:T(8,128)S(1)}, u32[]{:S(2)}, u32[]{:S(2)}) collective-permute-start(f32[16,1088]{1,0:T(8,128)S(1)} %get-tuple-element.67), channel_id=1, source_target_pairs={{0,6},{2,0},{4,2},{6,4},{1,7},{3,1},{5,3},{7,5},{8,14},{10,8},{12,... | collective-permute-start | bytes 208904 | tf_op jit(solution)/shard_map/ppermute | solution.py:21
  37.7 6.2 %collective-permute-start.11 = (f32[16,1088]{1,0:T(8,128)S(1)}, f32[16,1088]{1,0:T(8,128)S(1)}, u32[]{:S(2)}, u32[]{:S(2)}) collective-permute-start(f32[16,1088]{1,0:T(8,128)S(1)} %get-tuple-element.67), channel_id=1, source_target_pairs={{0,4},{2,6},{4,0},{6,2},{1,5},{3,7},{5,1},{7,3},{8,12},{10,14},{12... | collective-permute-start | bytes 208904 | tf_op jit(solution)/shard_map/ppermute | solution.py:21
  39.0 4.9 %collective-permute-start.10 = (f32[16,1088]{1,0:T(8,128)S(1)}, f32[16,1088]{1,0:T(8,128)S(1)}, u32[]{:S(2)}, u32[]{:S(2)}) collective-permute-start(f32[16,1088]{1,0:T(8,128)S(1)} %get-tuple-element.67), channel_id=1, source_target_pairs={{0,2},{2,4},{4,6},{6,0},{1,3},{3,5},{5,7},{7,1},{8,10},{10,12},{12... | collective-permute-start | bytes 208904 | tf_op jit(solution)/shard_map/ppermute | solution.py:21
  44.0 6.5 %collective-permute-start.13 = (f32[4,16,1088]{2,1,0:T(8,128)S(1)}, f32[4,16,1088]{2,1,0:T(8,128)S(1)}, u32[]{:S(2)}, u32[]{:S(2)}) collective-permute-start(f32[4,16,1088]{2,1,0:T(8,128)S(1)} %pad_maximum_fusion.mine), channel_id=1, source_target_pairs={{0,1},{1,0},{2,3},{3,2},{4,5},{5,4},{6,7},{7,6},{8,9},{9,8},{10,11... | collective-permute-start | bytes 835592 | tf_op jit(solution)/shard_map/ppermute | solution.py:25
  53.9 5.4 %collective-permute-start.17 = (f32[3,16,320]{2,1,0:T(8,128)S(1)}, f32[3,16,320]{2,1,0:T(8,128)S(1)}, u32[]{:S(2)}, u32[]{:S(2)}) collective-permute-start(f32[3,16,320]{2,1,0:T(8,128)S(1)} %get-tuple-element.122), channel_id=1, source_target_pairs={{0,6},{2,0},{4,2},{6,4},{1,7},{3,1},{5,3},{7,5},{8,14},{10,8},{12,... | collective-permute-start | bytes 184328 | tf_op jit(solution)/shard_map/ppermute | solution.py:21
  56.2 4.8 %collective-permute-start.16 = (f32[3,16,320]{2,1,0:T(8,128)S(1)}, f32[3,16,320]{2,1,0:T(8,128)S(1)}, u32[]{:S(2)}, u32[]{:S(2)}) collective-permute-start(f32[3,16,320]{2,1,0:T(8,128)S(1)} %get-tuple-element.123), channel_id=1, source_target_pairs={{0,4},{2,6},{4,0},{6,2},{1,5},{3,7},{5,1},{7,3},{8,12},{10,14},{12... | collective-permute-start | bytes 184328 | tf_op jit(solution)/shard_map/ppermute | solution.py:21
  56.6 6.5 %collective-permute-start.15 = (f32[3,16,320]{2,1,0:T(8,128)S(1)}, f32[3,16,320]{2,1,0:T(8,128)S(1)}, u32[]{:S(2)}, u32[]{:S(2)}) collective-permute-start(f32[3,16,320]{2,1,0:T(8,128)S(1)} %get-tuple-element.124), channel_id=1, source_target_pairs={{0,2},{2,4},{4,6},{6,0},{1,3},{3,5},{5,7},{7,1},{8,10},{10,12},{12... | collective-permute-start | bytes 184328 | tf_op jit(solution)/shard_map/ppermute | solution.py:21
  63.5 4.4 %collective-permute-start.19 = (f32[16,768]{1,0:T(8,128)S(1)}, f32[16,768]{1,0:T(8,128)S(1)}, u32[]{:S(2)}, u32[]{:S(2)}) collective-permute-start(f32[16,768]{1,0:T(8,128)S(1)} %get-tuple-element.81.m0), channel_id=1, source_target_pairs={{0,16},{8,24},{16,0},{24,8},{1,17},{9,25},{17,1},{25,9},{2,18},{10... | collective-permute-start | bytes 147464 | tf_op jit(solution)/shard_map/ppermute | solution.py:21
  64.8 4.2 %collective-permute-start.18 = (f32[16,768]{1,0:T(8,128)S(1)}, f32[16,768]{1,0:T(8,128)S(1)}, u32[]{:S(2)}, u32[]{:S(2)}) collective-permute-start(f32[16,768]{1,0:T(8,128)S(1)} %get-tuple-element.81.m0), channel_id=1, source_target_pairs={{0,8},{8,16},{16,24},{24,0},{1,9},{9,17},{17,25},{25,1},{2,10},{10... | collective-permute-start | bytes 147464 | tf_op jit(solution)/shard_map/ppermute | solution.py:21
  69.0 4.0 %collective-permute-start.21 = (f32[16,448]{1,0:T(8,128)S(1)}, f32[16,448]{1,0:T(8,128)S(1)}, u32[]{:S(2)}, u32[]{:S(2)}) collective-permute-start(f32[16,448]{1,0:T(8,128)S(1)} %get-tuple-element.82), channel_id=1, source_target_pairs={{0,32},{32,64},{64,96},{96,0},{1,33},{33,65},{65,97},{97,1},{2,34}... | collective-permute-start | bytes 86024 | tf_op jit(solution)/shard_map/ppermute | solution.py:21
  69.1 4.3 %collective-permute-start.22 = (f32[16,448]{1,0:T(8,128)S(1)}, f32[16,448]{1,0:T(8,128)S(1)}, u32[]{:S(2)}, u32[]{:S(2)}) collective-permute-start(f32[16,448]{1,0:T(8,128)S(1)} %get-tuple-element.83), channel_id=1, source_target_pairs={{0,64},{32,96},{64,0},{96,32},{1,65},{33,97},{65,1},{97,33},{2,66}... | collective-permute-start | bytes 86024 | tf_op jit(solution)/shard_map/ppermute | solution.py:21
  74.2 4.8 %collective-permute-start.25 = (f32[16,1088]{1,0:T(8,128)S(1)}, f32[16,1088]{1,0:T(8,128)S(1)}, u32[]{:S(2)}, u32[]{:S(2)}) collective-permute-start(f32[16,1088]{1,0:T(8,128)S(1)} %get-tuple-element.87), channel_id=1, source_target_pairs={{0,4},{2,6},{4,0},{6,2},{1,5},{3,7},{5,1},{7,3},{8,12},{10,14},{12... | collective-permute-start | bytes 208904 | tf_op jit(solution)/shard_map/ppermute | solution.py:21
  74.8 4.9 %collective-permute-start.24 = (f32[16,1088]{1,0:T(8,128)S(1)}, f32[16,1088]{1,0:T(8,128)S(1)}, u32[]{:S(2)}, u32[]{:S(2)}) collective-permute-start(f32[16,1088]{1,0:T(8,128)S(1)} %get-tuple-element.87), channel_id=1, source_target_pairs={{0,2},{2,4},{4,6},{6,0},{1,3},{3,5},{5,7},{7,1},{8,10},{10,12},{12... | collective-permute-start | bytes 208904 | tf_op jit(solution)/shard_map/ppermute | solution.py:21
  79.8 7.0 %collective-permute-start.27 = (f32[4,16,1088]{2,1,0:T(8,128)S(1)}, f32[4,16,1088]{2,1,0:T(8,128)S(1)}, u32[]{:S(2)}, u32[]{:S(2)}) collective-permute-start(f32[4,16,1088]{2,1,0:T(8,128)S(1)} %pad_maximum_fusion.1.mine), channel_id=1, source_target_pairs={{0,1},{1,0},{2,3},{3,2},{4,5},{5,4},{6,7},{7,6},{8,9},{9,8},{10,11... | collective-permute-start | bytes 835592 | tf_op jit(solution)/shard_map/ppermute | solution.py:25
  90.5 4.4 %collective-permute-start.31 = (f32[3,16,320]{2,1,0:T(8,128)S(1)}, f32[3,16,320]{2,1,0:T(8,128)S(1)}, u32[]{:S(2)}, u32[]{:S(2)}) collective-permute-start(f32[3,16,320]{2,1,0:T(8,128)S(1)} %get-tuple-element.118), channel_id=1, source_target_pairs={{0,6},{2,0},{4,2},{6,4},{1,7},{3,1},{5,3},{7,5},{8,14},{10,8},{12,... | collective-permute-start | bytes 184328 | tf_op jit(solution)/shard_map/ppermute | solution.py:21
  92.1 4.8 %collective-permute-start.30 = (f32[3,16,320]{2,1,0:T(8,128)S(1)}, f32[3,16,320]{2,1,0:T(8,128)S(1)}, u32[]{:S(2)}, u32[]{:S(2)}) collective-permute-start(f32[3,16,320]{2,1,0:T(8,128)S(1)} %get-tuple-element.119), channel_id=1, source_target_pairs={{0,4},{2,6},{4,0},{6,2},{1,5},{3,7},{5,1},{7,3},{8,12},{10,14},{12... | collective-permute-start | bytes 184328 | tf_op jit(solution)/shard_map/ppermute | solution.py:21
  92.8 6.1 %collective-permute-start.29 = (f32[3,16,320]{2,1,0:T(8,128)S(1)}, f32[3,16,320]{2,1,0:T(8,128)S(1)}, u32[]{:S(2)}, u32[]{:S(2)}) collective-permute-start(f32[3,16,320]{2,1,0:T(8,128)S(1)} %get-tuple-element.120), channel_id=1, source_target_pairs={{0,2},{2,4},{4,6},{6,0},{1,3},{3,5},{5,7},{7,1},{8,10},{10,12},{12... | collective-permute-start | bytes 184328 | tf_op jit(solution)/shard_map/ppermute | solution.py:21
  100.1 4.5 %collective-permute-start.33 = (f32[16,768]{1,0:T(8,128)S(1)}, f32[16,768]{1,0:T(8,128)S(1)}, u32[]{:S(2)}, u32[]{:S(2)}) collective-permute-start(f32[16,768]{1,0:T(8,128)S(1)} %get-tuple-element.100.m0), channel_id=1, source_target_pairs={{0,16},{8,24},{16,0},{24,8},{1,17},{9,25},{17,1},{25,9},{2,18},{10... | collective-permute-start | bytes 147464 | tf_op jit(solution)/shard_map/ppermute | solution.py:21
  100.8 4.3 %collective-permute-start.32 = (f32[16,768]{1,0:T(8,128)S(1)}, f32[16,768]{1,0:T(8,128)S(1)}, u32[]{:S(2)}, u32[]{:S(2)}) collective-permute-start(f32[16,768]{1,0:T(8,128)S(1)} %get-tuple-element.100.m0), channel_id=1, source_target_pairs={{0,8},{8,16},{16,24},{24,0},{1,9},{9,17},{17,25},{25,1},{2,10},{10... | collective-permute-start | bytes 147464 | tf_op jit(solution)/shard_map/ppermute | solution.py:21
  105.2 4.3 %collective-permute-start.35 = (f32[16,448]{1,0:T(8,128)S(1)}, f32[16,448]{1,0:T(8,128)S(1)}, u32[]{:S(2)}, u32[]{:S(2)}) collective-permute-start(f32[16,448]{1,0:T(8,128)S(1)} %get-tuple-element.101), channel_id=1, source_target_pairs={{0,32},{32,64},{64,96},{96,0},{1,33},{33,65},{65,97},{97,1},{2,34}... | collective-permute-start | bytes 86024 | tf_op jit(solution)/shard_map/ppermute | solution.py:21
  106.7 4.4 %collective-permute-start.36 = (f32[16,448]{1,0:T(8,128)S(1)}, f32[16,448]{1,0:T(8,128)S(1)}, u32[]{:S(2)}, u32[]{:S(2)}) collective-permute-start(f32[16,448]{1,0:T(8,128)S(1)} %get-tuple-element.102), channel_id=1, source_target_pairs={{0,64},{32,96},{64,0},{96,32},{1,65},{33,97},{65,1},{97,33},{2,66}... | collective-permute-start | bytes 86024 | tf_op jit(solution)/shard_map/ppermute | solution.py:21
  112.7 4.8 %collective-permute-start.39 = (f32[16,1088]{1,0:T(8,128)S(1)}, f32[16,1088]{1,0:T(8,128)S(1)}, u32[]{:S(2)}, u32[]{:S(2)}) collective-permute-start(f32[16,1088]{1,0:T(8,128)S(1)} %get-tuple-element.106), channel_id=1, source_target_pairs={{0,4},{2,6},{4,0},{6,2},{1,5},{3,7},{5,1},{7,3},{8,12},{10,14},{12... | collective-permute-start | bytes 208904 | tf_op jit(solution)/shard_map/ppermute | solution.py:21
  113.1 5.1 %collective-permute-start.38 = (f32[16,1088]{1,0:T(8,128)S(1)}, f32[16,1088]{1,0:T(8,128)S(1)}, u32[]{:S(2)}, u32[]{:S(2)}) collective-permute-start(f32[16,1088]{1,0:T(8,128)S(1)} %get-tuple-element.106), channel_id=1, source_target_pairs={{0,2},{2,4},{4,6},{6,0},{1,3},{3,5},{5,7},{7,1},{8,10},{10,12},{12... | collective-permute-start | bytes 208904 | tf_op jit(solution)/shard_map/ppermute | solution.py:21
  118.3 6.9 %collective-permute-start.41 = (f32[4,16,1088]{2,1,0:T(8,128)S(1)}, f32[4,16,1088]{2,1,0:T(8,128)S(1)}, u32[]{:S(2)}, u32[]{:S(2)}) collective-permute-start(f32[4,16,1088]{2,1,0:T(8,128)S(1)} %pad_maximum_fusion.2.mine), channel_id=1, source_target_pairs={{0,1},{1,0},{2,3},{3,2},{4,5},{5,4},{6,7},{7,6},{8,9},{9,8},{10,11... | collective-permute-start | bytes 835592 | tf_op jit(solution)/shard_map/ppermute | solution.py:25
  (14 other events, 52.5 us)

commit v3 on v2

--- a/solution.py
+++ b/solution.py
@@ -186,16 +186,13 @@
 
     def fetch(index):
         day, row = jobs[index]
-        slot = index % 3
-        return pltpu.make_async_copy(source.at[day, pl.ds(row, CHUNK)], buffer.at[slot], sem.at[slot])
-
-    fetch(0).start()
-    fetch(1).start()
+        return pltpu.make_async_copy(source.at[day, pl.ds(row, CHUNK)], buffer.at[index], sem.at[index])
+
+    for index in range(len(jobs)):
+        fetch(index).start()
     for index, (day, row) in enumerate(jobs):
-        if index + 2 < len(jobs):
-            fetch(index + 2).start()
         fetch(index).wait()
-        high, low = halves(buffer[index % 3])
+        high, low = halves(buffer[index])
         target[pl.ds(row, CHUNK)] = high
         target[pl.ds(320 + row, CHUNK)] = low
 
@@ -207,7 +204,7 @@
         pltpu.VMEM((640, 2560), BF16),
         [HBM_BLOCK],
         pltpu.with_memory_space_constraint(blocks, pltpu.HBM),
-        scratch=[pltpu.VMEM((3, CHUNK, 2560), F32), pltpu.SemaphoreType.DMA((3,))],
+        scratch=[pltpu.VMEM((4, CHUNK, 2560), F32), pltpu.SemaphoreType.DMA((4,))],
     )
 
 
@@ -686,17 +683,23 @@
     )
 
 
-def setup_kernel(count, vertices, bary, prec, value, covs, spread, weight, kept, sent, grad_cov, covariates):
+def setup_kernel(count, triangles, cells, bary, prec, value, covs, spread, weight, kept, sent, grad_cov, covariates, table):
     core = lax.axis_index("blk_1")
     slot_start = (lax.axis_index("blk_0") * 2 + core) * 128
     cov_sum = jnp.zeros((1, 64), F32)
+    table[...] = jnp.zeros((8, 5120), F32)
+    table[0:3, 0:5116] = triangles[...].astype(F32)
+    parts = stacked_halves(table[...])
     for day in range(2):
+        cell = lax.broadcasted_iota(jnp.int32, (5120, 128), 0) == cells[day : day + 1, :]
+        found = matmul(parts, jnp.where(cell, 1.0, 0.0).astype(BF16), NN)
+        corners = (found[:8] + found[8:]).astype(jnp.int32)
         shares = [bary[k, day : day + 1, :] for k in range(3)]
         total = shares[0] + shares[1] + shares[2]
         nodes = lax.broadcasted_iota(jnp.int32, (2560, 128), 0)
         dense = jnp.zeros((2560, 128), F32)
         for k in range(3):
-            dense = dense + jnp.where(nodes == vertices[k, day : day + 1, :], shares[k] / total, 0.0)
+            dense = dense + jnp.where(nodes == corners[k : k + 1, :], shares[k] / total, 0.0)
         high, low = halves(dense)
         spread[day, :, :128] = high
         spread[day, :, 128:] = low
@@ -727,6 +730,7 @@
         operands[0],
         *(pltpu.with_memory_space_constraint(o, pltpu.HBM) for o in operands[1:]),
         grid=(1,),
+        scratch=[pltpu.VMEM((8, 5120), F32)],
     )
 
 
@@ -752,9 +756,8 @@
     dominant = jnp.sum(jnp.where(rows == columns, square, 0.0), axis=1)
     both = jnp.concatenate([1.0 - leakage, dominant])
 
-    vertices = triangles[:, obs_triangle]
     spread, weight, kept, sent, grad_cov, covs = setup_stage(
-        obs_count, vertices, obs_bary, obs_prec, obs_value, covariates
+        obs_count, triangles, obs_triangle, obs_bary, obs_prec, obs_value, covariates
     )
     off_pair = [split_blocks(off_blocks, "split_off", day) for day in range(2)]
     diag_pair = [split_blocks(diag_blocks, "split_diag", day) for day in range(2)]

time: 144 us -> 140 us (0.972)
  local copies, waits for them, and re-layouts: 3.81 us -> 0.76 us
    unnamed x9 -> x8, local copies, waits for them, and re-layouts: 2.32 us -> 0.66 us
    pallas_call x22, Pallas kernels: 32 us -> 30.6 us  [call(): pl.pallas_call(kernel, grid=grid, out_shape=outs, in_specs=in_specs, out_...]
  transfers between devices with their start and end apart: 42 -> 42, of which waited for: 32 -> 33; matrix products, arithmetic and copies ran while one was open for 2% -> 2% of each run, Pallas kernels for 13% -> 12%
where the time goes in v3:
time: 140 us
  starting transfers between devices  55 us (39%)
  waiting for transfers between devices  35.8 us (26%)
  Pallas kernels  30.6 us (22%)
  blocking collectives  14.3 us (10%)
  other arithmetic  2.33 us (2%)
    ppermute x36, starting transfers between devices, shift(): lax.ppermute(value, axis, [(i, (i + distance) % size) for i in range(size)])  35.5 us
    pallas_call x22, Pallas kernels, call(): pl.pallas_call(kernel, grid=grid, out_shape=outs, in_specs=in_specs, out_...  30.6 us
    ppermute x36, waiting for transfers between devices, shift(): lax.ppermute(value, axis, [(i, (i + distance) % size) for i in range(size)])  29.8 us
    ppermute x6, starting transfers between devices, swapped(): return lax.ppermute(value, 'blk_1', [(0, 1), (1, 0)])  19.5 us
    all_to_all x1, blocking collectives, on_device(): sums = lax.all_to_all(sums, DAY + BLK, 0, 0, tiled=True)  14.3 us
    ppermute x6, waiting for transfers between devices, swapped(): return lax.ppermute(value, 'blk_1', [(0, 1), (1, 0)])  6.04 us
  transfers between devices with their start and end apart: 42, of which 33 were waited for; matrix products, arithmetic and copies ran while one was open for 2% of the time, Pallas kernels for 12%

profile of v3, /device:TPU:1, one launch (start us, length us, event | category | flops | bytes accessed | tf_op | source)
XLA Modules:
  0.0 139.7 jit_solution(9628525335773337383)
XLA Ops:
  1.3 3.7 %setup_stage.1 = (bf16[2,2560,256]{2,1,0:T(8,128)(2,1)S(1)}, f32[2,128]{1,0:T(2,128)S(1)}, f32[4,2,320]{2,1,0:T(2,128)S(1)}, f32[4,2,320]{2,1,0:T(2,128)S(1)}, f...) custom-call(s32[2]{0:T(128)S(1)} %copy-done.2, s32[3,5116]{1,0:T(4,128)} %triangles.1, s32[2,128]{1,0:T(2,128)} %cells.1, ...), custom_call_target="tpu_custom_call" | custom-call | tf_op jit(solution)/shard_map/setup_stage/pallas_call | solution.py:169
  8.7 2.8 %collective-permute-start.3 = (f32[2,320]{1,0:T(2,128)S(1)}, f32[2,320]{1,0:T(2,128)S(1)}, u32[]{:S(2)}, u32[]{:S(2)}) collective-permute-start(f32[2,320]{1,0:T(2,128)S(1)} %get-tuple-element.126), channel_id=1, source_target_pairs={{0,6},{2,0},{4,2},{6,4},{1,7},{3,1},{5,3},{7,5},{8,14},{10,8},{12,... | collective-permute-start | bytes 7688 | tf_op jit(solution)/shard_map/ppermute | solution.py:21
  12.7 2.0 %split_off0.1.refs_0_.o0 = bf16[640,2560]{1,0:T(8,128)(2,1)S(1)} custom-call(f32[2,320,2560]{2,1,0:T(8,128)} %source.5), custom_call_target="tpu_custom_call" | custom-call | tf_op jit(solution)/shard_map/split_off0/pallas_call | solution.py:169
  15.7 2.5 %collective-permute-start.6 = (f32[16,768]{1,0:T(8,128)S(1)}, f32[16,768]{1,0:T(8,128)S(1)}, u32[]{:S(2)}, u32[]{:S(2)}) collective-permute-start(f32[16,768]{1,0:T(8,128)S(1)} %get-tuple-element.63.m0), channel_id=1, source_target_pairs={{0,24},{8,0},{16,8},{24,16},{1,25},{9,1},{17,9},{25,17},{2,26},{10... | collective-permute-start | bytes 147464 | tf_op jit(solution)/shard_map/ppermute | solution.py:21
  19.3 2.0 %split_off1.1.refs_0_.o1 = bf16[640,2560]{1,0:T(8,128)(2,1)S(1)} custom-call(f32[2,320,2560]{2,1,0:T(8,128)} %source.5), custom_call_target="tpu_custom_call" | custom-call | tf_op jit(solution)/shard_map/split_off1/pallas_call | solution.py:169
  23.5 3.8 %collective-permute-start.9 = (f32[16,768]{1,0:T(8,128)S(1)}, f32[16,768]{1,0:T(8,128)S(1)}, u32[]{:S(2)}, u32[]{:S(2)}) collective-permute-start(f32[16,768]{1,0:T(8,128)S(1)} %get-tuple-element.64.z0), channel_id=1, source_target_pairs={{0,96},{32,0},{64,32},{96,64},{1,97},{33,1},{65,33},{97,65},{2,98}... | collective-permute-start | bytes 147464 | tf_op jit(solution)/shard_map/ppermute | solution.py:21
  28.0 2.0 %split_diag0.1.refs_0_.a0 = bf16[640,2560]{1,0:T(8,128)(2,1)S(1)} custom-call(f32[2,320,2560]{2,1,0:T(8,128)} %source.7), custom_call_target="tpu_custom_call" | custom-call | tf_op jit(solution)/shard_map/split_diag0/pallas_call | solution.py:169
  30.0 1.8 %collective-permute-done.8.z2 = f32[16,768]{1,0:T(8,128)S(1)} collective-permute-done((f32[16,768]{1,0:T(8,128)S(1)}, f32[16,768]{1,0:T(8,128)S(1)}, u32[]{:S(2)}, u32[]{:S(2)}) %collective-permute-start.8) | collective-permute-done | bytes 49184 | tf_op jit(solution)/shard_map/ppermute | solution.py:21
  35.4 2.0 %split_diag1.1.a1 = bf16[640,2560]{1,0:T(8,128)(2,1)S(1)} custom-call(f32[2,320,2560]{2,1,0:T(8,128)} %source.7), custom_call_target="tpu_custom_call" | custom-call | tf_op jit(solution)/shard_map/split_diag1/pallas_call | solution.py:169
  37.5 2.3 %own_terms.2.behind.behind1 = f32[3,16,2560]{2,1,0:T(8,128)S(1)} custom-call(bf16[640,2560]{1,0:T(8,128)(2,1)S(1)} %split_diag0.1.refs_0_.a0, bf16[640,2560]{1,0:T(8,128)(2,1)S(1)} %split_diag1.1.a1, bf16[640,2560]{1,0:T(8,128)(2,1)S(1)} %split_off0.1.refs_0_.o0, bf16[640,2560]{1,0:T(8,128)(2,1)S(1)} %split_off1.1.refs_0_.o1, ...), custom_call_target="tpu_custom_call" | custom-call | tf_op jit(solution)/shard_map/own_terms/pallas_call | solution.py:169
  39.9 5.8 %collective-permute-start.13 = (f32[4,16,1088]{2,1,0:T(8,128)S(1)}, f32[4,16,1088]{2,1,0:T(8,128)S(1)}, u32[]{:S(2)}, u32[]{:S(2)}) collective-permute-start(f32[4,16,1088]{2,1,0:T(8,128)S(1)} %pad_maximum_fusion.mine), channel_id=1, source_target_pairs={{0,1},{1,0},{2,3},{3,2},{4,5},{5,4},{6,7},{7,6},{8,9},{9,8},{10,11... | collective-permute-start | bytes 835592 | tf_op jit(solution)/shard_map/ppermute | solution.py:25
  46.9 1.6 %first_stage.1 = (f32[4,3,16,320]{3,2,1,0:T(8,128)S(1)}, f32[4,3,16,320]{3,2,1,0:T(8,128)S(1)}, f32[16,64]{1,0:T(8,128)S(1)}, f32[3,16,2560]{2,1,0:T(8,128)S(1)}, f32[16,64]{1,0:T(8,128)S(1)}) custom-call(f32[4,16,1088]{2,1,0:T(8,128)S(1)} %pad_maximum_fusion.mine, f32[4,16,1088]{2,1,0:T(8,128)S(1)} %collective-permute-done.13.other, ...), custom_call_target="tpu_custom_call" | custom-call | tf_op jit(solution)/shard_map/first_stage/pallas_call | solution.py:169
  50.3 1.8 %collective-permute-start.17 = (f32[3,16,320]{2,1,0:T(8,128)S(1)}, f32[3,16,320]{2,1,0:T(8,128)S(1)}, u32[]{:S(2)}, u32[]{:S(2)}) collective-permute-start(f32[3,16,320]{2,1,0:T(8,128)S(1)} %get-tuple-element.122), channel_id=1, source_target_pairs={{0,6},{2,0},{4,2},{6,4},{1,7},{3,1},{5,3},{7,5},{8,14},{10,8},{12,... | collective-permute-start | bytes 184328 | tf_op jit(solution)/shard_map/ppermute | solution.py:21
  53.6 2.0 %first_rows.1 = (f32[2,16,320]{2,1,0:T(8,128)S(1)}, f32[16,64]{1,0:T(8,128)S(1)}) custom-call(bf16[640,2560]{1,0:T(8,128)(2,1)S(1)} %split_off0.1.refs_0_.o0, bf16[640,2560]{1,0:T(8,128)(2,1)S(1)} %split_off1.1.refs_0_.o1, f32[3,16,2560]{2,1,0:T(8,128)S(1)} %get-tuple-element.76.whole.whole1, f32[2,16,320]{2,1,0:T(8,128)S(1)} %get-tuple-element.66.bx, ...), custom_call_target="tpu_custom_call" | custom-call | tf_op jit(solution)/shard_map/first_rows/pallas_call | solution.py:169
  56.8 2.1 %collective-permute-done.15.p1 = f32[3,16,320]{2,1,0:T(8,128)S(1)} collective-permute-done((f32[3,16,320]{2,1,0:T(8,128)S(1)}, f32[3,16,320]{2,1,0:T(8,128)S(1)}, u32[]{:S(2)}, u32[]{:S(2)}) %collective-permute-start.15) | collective-permute-done | bytes 61472 | tf_op jit(solution)/shard_map/ppermute | solution.py:21
  62.0 1.8 %collective-permute-done.19.m2 = f32[16,768]{1,0:T(8,128)S(1)} collective-permute-done((f32[16,768]{1,0:T(8,128)S(1)}, f32[16,768]{1,0:T(8,128)S(1)}, u32[]{:S(2)}, u32[]{:S(2)}) %collective-permute-start.19) | collective-permute-done | bytes 49184 | tf_op jit(solution)/shard_map/ppermute | solution.py:21
  64.7 1.7 %collective-permute-start.22 = (f32[16,448]{1,0:T(8,128)S(1)}, f32[16,448]{1,0:T(8,128)S(1)}, u32[]{:S(2)}, u32[]{:S(2)}) collective-permute-start(f32[16,448]{1,0:T(8,128)S(1)} %get-tuple-element.83), channel_id=1, source_target_pairs={{0,64},{32,96},{64,0},{96,32},{1,65},{33,97},{65,1},{97,33},{2,66}... | collective-permute-start | bytes 86024 | tf_op jit(solution)/shard_map/ppermute | solution.py:21
  66.5 1.8 %collective-permute-start.23 = (f32[16,448]{1,0:T(8,128)S(1)}, f32[16,448]{1,0:T(8,128)S(1)}, u32[]{:S(2)}, u32[]{:S(2)}) collective-permute-start(f32[16,448]{1,0:T(8,128)S(1)} %get-tuple-element.84), channel_id=1, source_target_pairs={{0,96},{32,0},{64,32},{96,64},{1,97},{33,1},{65,33},{97,65},{2,98}... | collective-permute-start | bytes 86024 | tf_op jit(solution)/shard_map/ppermute | solution.py:21
  71.3 2.3 %own_terms.3.behind2 = f32[3,16,2560]{2,1,0:T(8,128)S(1)} custom-call(bf16[640,2560]{1,0:T(8,128)(2,1)S(1)} %split_diag0.1.refs_0_.a0, bf16[640,2560]{1,0:T(8,128)(2,1)S(1)} %split_diag1.1.a1, bf16[640,2560]{1,0:T(8,128)(2,1)S(1)} %split_off0.1.refs_0_.o0, bf16[640,2560]{1,0:T(8,128)(2,1)S(1)} %split_off1.1.refs_0_.o1, ...), custom_call_target="tpu_custom_call" | custom-call | tf_op jit(solution)/shard_map/own_terms/pallas_call | solution.py:169
  75.4 5.6 %collective-permute-start.27 = (f32[4,16,1088]{2,1,0:T(8,128)S(1)}, f32[4,16,1088]{2,1,0:T(8,128)S(1)}, u32[]{:S(2)}, u32[]{:S(2)}) collective-permute-start(f32[4,16,1088]{2,1,0:T(8,128)S(1)} %pad_maximum_fusion.1.mine), channel_id=1, source_target_pairs={{0,1},{1,0},{2,3},{3,2},{4,5},{5,4},{6,7},{7,6},{8,9},{9,8},{10,11... | collective-permute-start | bytes 835592 | tf_op jit(solution)/shard_map/ppermute | solution.py:25
  82.3 2.0 %second_stage.1 = (f32[4,3,16,320]{3,2,1,0:T(8,128)S(1)}, f32[4,3,16,320]{3,2,1,0:T(8,128)S(1)}, f32[16,64]{1,0:T(8,128)S(1)}, f32[3,16,2560]{2,1,0:T(8,128)S(1)...) custom-call(f32[4,16,1088]{2,1,0:T(8,128)S(1)} %pad_maximum_fusion.1.mine, ...), custom_call_target="tpu_custom_call" | custom-call | tf_op jit(solution)/shard_map/second_stage/pallas_call | solution.py:169
  86.0 1.7 %collective-permute-start.31 = (f32[3,16,320]{2,1,0:T(8,128)S(1)}, f32[3,16,320]{2,1,0:T(8,128)S(1)}, u32[]{:S(2)}, u32[]{:S(2)}) collective-permute-start(f32[3,16,320]{2,1,0:T(8,128)S(1)} %get-tuple-element.118), channel_id=1, source_target_pairs={{0,6},{2,0},{4,2},{6,4},{1,7},{3,1},{5,3},{7,5},{8,14},{10,8},{12,... | collective-permute-start | bytes 184328 | tf_op jit(solution)/shard_map/ppermute | solution.py:21
  88.4 2.0 %second_rows.1 = (f32[2,16,320]{2,1,0:T(8,128)S(1)}, f32[16,64]{1,0:T(8,128)S(1)}, f32[3,16,320]{2,1,0:T(8,128)S(1)}, f32[3,16,320]{2,1,0:T(8,128)S(1)}) custom-call(bf16[640,2560]{1,0:T(8,128)(2,1)S(1)} %split_off0.1.refs_0_.o0, bf16[640,2560]{1,0:T(8,128)(2,1)S(1)} %split_off1.1.refs_0_.o1, f32[3,16,2560]{2,1,0:T(8,128)S(1)} %get-tuple-element.94.whole.z1whole, ...), custom_call_target="tpu_custom_call" | custom-call | tf_op jit(solution)/shard_map/second_rows/pallas_call | solution.py:169
  90.4 2.0 %collective-permute-done.30.p2 = f32[3,16,320]{2,1,0:T(8,128)S(1)} collective-permute-done((f32[3,16,320]{2,1,0:T(8,128)S(1)}, f32[3,16,320]{2,1,0:T(8,128)S(1)}, u32[]{:S(2)}, u32[]{:S(2)}) %collective-permute-start.30) | collective-permute-done | bytes 61472 | tf_op jit(solution)/shard_map/ppermute | solution.py:21
  92.4 1.9 %collective-permute-done.29.p1 = f32[3,16,320]{2,1,0:T(8,128)S(1)} collective-permute-done((f32[3,16,320]{2,1,0:T(8,128)S(1)}, f32[3,16,320]{2,1,0:T(8,128)S(1)}, u32[]{:S(2)}, u32[]{:S(2)}) %collective-permute-start.29) | collective-permute-done | bytes 61472 | tf_op jit(solution)/shard_map/ppermute | solution.py:21
  97.5 3.0 %collective-permute-done.33.m2 = f32[16,768]{1,0:T(8,128)S(1)} collective-permute-done((f32[16,768]{1,0:T(8,128)S(1)}, f32[16,768]{1,0:T(8,128)S(1)}, u32[]{:S(2)}, u32[]{:S(2)}) %collective-permute-start.33) | collective-permute-done | bytes 49184 | tf_op jit(solution)/shard_map/ppermute | solution.py:21
  102.6 2.7 %collective-permute-start.36 = (f32[16,448]{1,0:T(8,128)S(1)}, f32[16,448]{1,0:T(8,128)S(1)}, u32[]{:S(2)}, u32[]{:S(2)}) collective-permute-start(f32[16,448]{1,0:T(8,128)S(1)} %get-tuple-element.102), channel_id=1, source_target_pairs={{0,64},{32,96},{64,0},{96,32},{1,65},{33,97},{65,1},{97,33},{2,66}... | collective-permute-start | bytes 86024 | tf_op jit(solution)/shard_map/ppermute | solution.py:21
  105.4 1.5 %collective-permute-done.36.r2 = f32[16,448]{1,0:T(8,128)S(1)} collective-permute-done((f32[16,448]{1,0:T(8,128)S(1)}, f32[16,448]{1,0:T(8,128)S(1)}, u32[]{:S(2)}, u32[]{:S(2)}) %collective-permute-start.36) | collective-permute-done | bytes 28704 | tf_op jit(solution)/shard_map/ppermute | solution.py:21
  110.0 2.0 %collective-permute-done.40 = f32[16,1088]{1,0:T(8,128)S(1)} collective-permute-done((f32[16,1088]{1,0:T(8,128)S(1)}, f32[16,1088]{1,0:T(8,128)S(1)}, u32[]{:S(2)}, u32[]{:S(2)}) %collective-permute-start.40) | collective-permute-done | bytes 69664 | tf_op jit(solution)/shard_map/ppermute | solution.py:21
  114.1 5.7 %collective-permute-start.41 = (f32[4,16,1088]{2,1,0:T(8,128)S(1)}, f32[4,16,1088]{2,1,0:T(8,128)S(1)}, u32[]{:S(2)}, u32[]{:S(2)}) collective-permute-start(f32[4,16,1088]{2,1,0:T(8,128)S(1)} %pad_maximum_fusion.2.mine), channel_id=1, source_target_pairs={{0,1},{1,0},{2,3},{3,2},{4,5},{5,4},{6,7},{7,6},{8,9},{9,8},{10,11... | collective-permute-start | bytes 835592 | tf_op jit(solution)/shard_map/ppermute | solution.py:25
  121.0 3.2 %third_stage.1 = (f32[128,128]{1,0:T(8,128)S(1)}, f32[2,16,320]{2,1,0:T(8,128)S(1)}, f32[2,16,320]{2,1,0:T(8,128)S(1)}, f32[16,128]{1,0:T(8,128)S(1)}, f32[2,16,64]{2,1,0:T(8,128)S(1)}) custom-call(f32[4,16,1088]{2,1,0:T(8,128)S(1)} %pad_maximum_fusion.2.mine, f32[4,16,1088]{2,1,0:T(8,128)S(1)} %collective-permute-done.41.other, ...), custom_call_target="tpu_custom_call" | custom-call | tf_op jit(solution)/shard_map/third_stage/pallas_call | solution.py:169
  124.3 14.3 %all_to_all.11 = f32[128,1,128]{2,1,0:T(1,128)S(1)} all-to-all(f32[128,1,128]{2,1,0:T(1,128)S(1)} %bitcast.45), channel_id=1, replica_groups=mesh['day_0'=4,'day_1'=4,'blk_0'=4,'blk_1'=2] {'day_0','day_1','blk_0','..., dimensions={0} | all-to-all | bytes 131072 | tf_op jit(solution)/shard_map/all_to_all | solution.py:790
  (96 shorter events, 45.1 us)
Async XLA Ops:
  8.7 6.0 %collective-permute-start.3 = (f32[2,320]{1,0:T(2,128)S(1)}, f32[2,320]{1,0:T(2,128)S(1)}, u32[]{:S(2)}, u32[]{:S(2)}) collective-permute-start(f32[2,320]{1,0:T(2,128)S(1)} %get-tuple-element.126), channel_id=1, source_target_pairs={{0,6},{2,0},{4,2},{6,4},{1,7},{3,1},{5,3},{7,5},{8,14},{10,8},{12,... | collective-permute-start | bytes 7688 | tf_op jit(solution)/shard_map/ppermute | solution.py:21
  11.5 4.0 %collective-permute-start.2 = (f32[2,320]{1,0:T(2,128)S(1)}, f32[2,320]{1,0:T(2,128)S(1)}, u32[]{:S(2)}, u32[]{:S(2)}) collective-permute-start(f32[2,320]{1,0:T(2,128)S(1)} %get-tuple-element.127), channel_id=1, source_target_pairs={{0,4},{2,6},{4,0},{6,2},{1,5},{3,7},{5,1},{7,3},{8,12},{10,14},{12... | collective-permute-start | bytes 7688 | tf_op jit(solution)/shard_map/ppermute | solution.py:21
  15.7 5.7 %collective-permute-start.6 = (f32[16,768]{1,0:T(8,128)S(1)}, f32[16,768]{1,0:T(8,128)S(1)}, u32[]{:S(2)}, u32[]{:S(2)}) collective-permute-start(f32[16,768]{1,0:T(8,128)S(1)} %get-tuple-element.63.m0), channel_id=1, source_target_pairs={{0,24},{8,0},{16,8},{24,16},{1,25},{9,1},{17,9},{25,17},{2,26},{10... | collective-permute-start | bytes 147464 | tf_op jit(solution)/shard_map/ppermute | solution.py:21
  18.2 4.5 %collective-permute-start.5 = (f32[16,768]{1,0:T(8,128)S(1)}, f32[16,768]{1,0:T(8,128)S(1)}, u32[]{:S(2)}, u32[]{:S(2)}) collective-permute-start(f32[16,768]{1,0:T(8,128)S(1)} %get-tuple-element.63.m0), channel_id=1, source_target_pairs={{0,16},{8,24},{16,0},{24,8},{1,17},{9,25},{17,1},{25,9},{2,18},{10... | collective-permute-start | bytes 147464 | tf_op jit(solution)/shard_map/ppermute | solution.py:21
  18.7 4.5 %collective-permute-start.4 = (f32[16,768]{1,0:T(8,128)S(1)}, f32[16,768]{1,0:T(8,128)S(1)}, u32[]{:S(2)}, u32[]{:S(2)}) collective-permute-start(f32[16,768]{1,0:T(8,128)S(1)} %get-tuple-element.63.m0), channel_id=1, source_target_pairs={{0,8},{8,16},{16,24},{24,0},{1,9},{9,17},{17,25},{25,1},{2,10},{10... | collective-permute-start | bytes 147464 | tf_op jit(solution)/shard_map/ppermute | solution.py:21
  23.5 6.6 %collective-permute-start.9 = (f32[16,768]{1,0:T(8,128)S(1)}, f32[16,768]{1,0:T(8,128)S(1)}, u32[]{:S(2)}, u32[]{:S(2)}) collective-permute-start(f32[16,768]{1,0:T(8,128)S(1)} %get-tuple-element.64.z0), channel_id=1, source_target_pairs={{0,96},{32,0},{64,32},{96,64},{1,97},{33,1},{65,33},{97,65},{2,98}... | collective-permute-start | bytes 147464 | tf_op jit(solution)/shard_map/ppermute | solution.py:21
  27.3 4.5 %collective-permute-start.8 = (f32[16,768]{1,0:T(8,128)S(1)}, f32[16,768]{1,0:T(8,128)S(1)}, u32[]{:S(2)}, u32[]{:S(2)}) collective-permute-start(f32[16,768]{1,0:T(8,128)S(1)} %get-tuple-element.64.z0), channel_id=1, source_target_pairs={{0,64},{32,96},{64,0},{96,32},{1,65},{33,97},{65,1},{97,33},{2,66}... | collective-permute-start | bytes 147464 | tf_op jit(solution)/shard_map/ppermute | solution.py:21
  27.3 4.7 %collective-permute-start.7 = (f32[16,768]{1,0:T(8,128)S(1)}, f32[16,768]{1,0:T(8,128)S(1)}, u32[]{:S(2)}, u32[]{:S(2)}) collective-permute-start(f32[16,768]{1,0:T(8,128)S(1)} %get-tuple-element.64.z0), channel_id=1, source_target_pairs={{0,32},{32,64},{64,96},{96,0},{1,33},{33,65},{65,97},{97,1},{2,34}... | collective-permute-start | bytes 147464 | tf_op jit(solution)/shard_map/ppermute | solution.py:21
  33.0 6.7 %collective-permute-start.12 = (f32[16,1088]{1,0:T(8,128)S(1)}, f32[16,1088]{1,0:T(8,128)S(1)}, u32[]{:S(2)}, u32[]{:S(2)}) collective-permute-start(f32[16,1088]{1,0:T(8,128)S(1)} %get-tuple-element.67), channel_id=1, source_target_pairs={{0,6},{2,0},{4,2},{6,4},{1,7},{3,1},{5,3},{7,5},{8,14},{10,8},{12,... | collective-permute-start | bytes 208904 | tf_op jit(solution)/shard_map/ppermute | solution.py:21
  34.1 5.6 %collective-permute-start.11 = (f32[16,1088]{1,0:T(8,128)S(1)}, f32[16,1088]{1,0:T(8,128)S(1)}, u32[]{:S(2)}, u32[]{:S(2)}) collective-permute-start(f32[16,1088]{1,0:T(8,128)S(1)} %get-tuple-element.67), channel_id=1, source_target_pairs={{0,4},{2,6},{4,0},{6,2},{1,5},{3,7},{5,1},{7,3},{8,12},{10,14},{12... | collective-permute-start | bytes 208904 | tf_op jit(solution)/shard_map/ppermute | solution.py:21
  35.4 4.4 %collective-permute-start.10 = (f32[16,1088]{1,0:T(8,128)S(1)}, f32[16,1088]{1,0:T(8,128)S(1)}, u32[]{:S(2)}, u32[]{:S(2)}) collective-permute-start(f32[16,1088]{1,0:T(8,128)S(1)} %get-tuple-element.67), channel_id=1, source_target_pairs={{0,2},{2,4},{4,6},{6,0},{1,3},{3,5},{5,7},{7,1},{8,10},{10,12},{12... | collective-permute-start | bytes 208904 | tf_op jit(solution)/shard_map/ppermute | solution.py:21
  39.9 7.0 %collective-permute-start.13 = (f32[4,16,1088]{2,1,0:T(8,128)S(1)}, f32[4,16,1088]{2,1,0:T(8,128)S(1)}, u32[]{:S(2)}, u32[]{:S(2)}) collective-permute-start(f32[4,16,1088]{2,1,0:T(8,128)S(1)} %pad_maximum_fusion.mine), channel_id=1, source_target_pairs={{0,1},{1,0},{2,3},{3,2},{4,5},{5,4},{6,7},{7,6},{8,9},{9,8},{10,11... | collective-permute-start | bytes 835592 | tf_op jit(solution)/shard_map/ppermute | solution.py:25
  50.3 5.4 %collective-permute-start.17 = (f32[3,16,320]{2,1,0:T(8,128)S(1)}, f32[3,16,320]{2,1,0:T(8,128)S(1)}, u32[]{:S(2)}, u32[]{:S(2)}) collective-permute-start(f32[3,16,320]{2,1,0:T(8,128)S(1)} %get-tuple-element.122), channel_id=1, source_target_pairs={{0,6},{2,0},{4,2},{6,4},{1,7},{3,1},{5,3},{7,5},{8,14},{10,8},{12,... | collective-permute-start | bytes 184328 | tf_op jit(solution)/shard_map/ppermute | solution.py:21
  52.1 4.7 %collective-permute-start.16 = (f32[3,16,320]{2,1,0:T(8,128)S(1)}, f32[3,16,320]{2,1,0:T(8,128)S(1)}, u32[]{:S(2)}, u32[]{:S(2)}) collective-permute-start(f32[3,16,320]{2,1,0:T(8,128)S(1)} %get-tuple-element.123), channel_id=1, source_target_pairs={{0,4},{2,6},{4,0},{6,2},{1,5},{3,7},{5,1},{7,3},{8,12},{10,14},{12... | collective-permute-start | bytes 184328 | tf_op jit(solution)/shard_map/ppermute | solution.py:21
  52.9 6.0 %collective-permute-start.15 = (f32[3,16,320]{2,1,0:T(8,128)S(1)}, f32[3,16,320]{2,1,0:T(8,128)S(1)}, u32[]{:S(2)}, u32[]{:S(2)}) collective-permute-start(f32[3,16,320]{2,1,0:T(8,128)S(1)} %get-tuple-element.124), channel_id=1, source_target_pairs={{0,2},{2,4},{4,6},{6,0},{1,3},{3,5},{5,7},{7,1},{8,10},{10,12},{12... | collective-permute-start | bytes 184328 | tf_op jit(solution)/shard_map/ppermute | solution.py:21
  59.3 4.4 %collective-permute-start.19 = (f32[16,768]{1,0:T(8,128)S(1)}, f32[16,768]{1,0:T(8,128)S(1)}, u32[]{:S(2)}, u32[]{:S(2)}) collective-permute-start(f32[16,768]{1,0:T(8,128)S(1)} %get-tuple-element.81.m0), channel_id=1, source_target_pairs={{0,16},{8,24},{16,0},{24,8},{1,17},{9,25},{17,1},{25,9},{2,18},{10... | collective-permute-start | bytes 147464 | tf_op jit(solution)/shard_map/ppermute | solution.py:21
  60.4 4.2 %collective-permute-start.18 = (f32[16,768]{1,0:T(8,128)S(1)}, f32[16,768]{1,0:T(8,128)S(1)}, u32[]{:S(2)}, u32[]{:S(2)}) collective-permute-start(f32[16,768]{1,0:T(8,128)S(1)} %get-tuple-element.81.m0), channel_id=1, source_target_pairs={{0,8},{8,16},{16,24},{24,0},{1,9},{9,17},{17,25},{25,1},{2,10},{10... | collective-permute-start | bytes 147464 | tf_op jit(solution)/shard_map/ppermute | solution.py:21
  64.6 4.0 %collective-permute-start.21 = (f32[16,448]{1,0:T(8,128)S(1)}, f32[16,448]{1,0:T(8,128)S(1)}, u32[]{:S(2)}, u32[]{:S(2)}) collective-permute-start(f32[16,448]{1,0:T(8,128)S(1)} %get-tuple-element.82), channel_id=1, source_target_pairs={{0,32},{32,64},{64,96},{96,0},{1,33},{33,65},{65,97},{97,1},{2,34}... | collective-permute-start | bytes 86024 | tf_op jit(solution)/shard_map/ppermute | solution.py:21
  64.7 4.3 %collective-permute-start.22 = (f32[16,448]{1,0:T(8,128)S(1)}, f32[16,448]{1,0:T(8,128)S(1)}, u32[]{:S(2)}, u32[]{:S(2)}) collective-permute-start(f32[16,448]{1,0:T(8,128)S(1)} %get-tuple-element.83), channel_id=1, source_target_pairs={{0,64},{32,96},{64,0},{96,32},{1,65},{33,97},{65,1},{97,33},{2,66}... | collective-permute-start | bytes 86024 | tf_op jit(solution)/shard_map/ppermute | solution.py:21
  69.8 4.8 %collective-permute-start.25 = (f32[16,1088]{1,0:T(8,128)S(1)}, f32[16,1088]{1,0:T(8,128)S(1)}, u32[]{:S(2)}, u32[]{:S(2)}) collective-permute-start(f32[16,1088]{1,0:T(8,128)S(1)} %get-tuple-element.87), channel_id=1, source_target_pairs={{0,4},{2,6},{4,0},{6,2},{1,5},{3,7},{5,1},{7,3},{8,12},{10,14},{12... | collective-permute-start | bytes 208904 | tf_op jit(solution)/shard_map/ppermute | solution.py:21
  70.6 4.8 %collective-permute-start.24 = (f32[16,1088]{1,0:T(8,128)S(1)}, f32[16,1088]{1,0:T(8,128)S(1)}, u32[]{:S(2)}, u32[]{:S(2)}) collective-permute-start(f32[16,1088]{1,0:T(8,128)S(1)} %get-tuple-element.87), channel_id=1, source_target_pairs={{0,2},{2,4},{4,6},{6,0},{1,3},{3,5},{5,7},{7,1},{8,10},{10,12},{12... | collective-permute-start | bytes 208904 | tf_op jit(solution)/shard_map/ppermute | solution.py:21
  75.4 6.9 %collective-permute-start.27 = (f32[4,16,1088]{2,1,0:T(8,128)S(1)}, f32[4,16,1088]{2,1,0:T(8,128)S(1)}, u32[]{:S(2)}, u32[]{:S(2)}) collective-permute-start(f32[4,16,1088]{2,1,0:T(8,128)S(1)} %pad_maximum_fusion.1.mine), channel_id=1, source_target_pairs={{0,1},{1,0},{2,3},{3,2},{4,5},{5,4},{6,7},{7,6},{8,9},{9,8},{10,11... | collective-permute-start | bytes 835592 | tf_op jit(solution)/shard_map/ppermute | solution.py:25
  86.0 4.4 %collective-permute-start.31 = (f32[3,16,320]{2,1,0:T(8,128)S(1)}, f32[3,16,320]{2,1,0:T(8,128)S(1)}, u32[]{:S(2)}, u32[]{:S(2)}) collective-permute-start(f32[3,16,320]{2,1,0:T(8,128)S(1)} %get-tuple-element.118), channel_id=1, source_target_pairs={{0,6},{2,0},{4,2},{6,4},{1,7},{3,1},{5,3},{7,5},{8,14},{10,8},{12,... | collective-permute-start | bytes 184328 | tf_op jit(solution)/shard_map/ppermute | solution.py:21
  87.7 4.8 %collective-permute-start.30 = (f32[3,16,320]{2,1,0:T(8,128)S(1)}, f32[3,16,320]{2,1,0:T(8,128)S(1)}, u32[]{:S(2)}, u32[]{:S(2)}) collective-permute-start(f32[3,16,320]{2,1,0:T(8,128)S(1)} %get-tuple-element.119), channel_id=1, source_target_pairs={{0,4},{2,6},{4,0},{6,2},{1,5},{3,7},{5,1},{7,3},{8,12},{10,14},{12... | collective-permute-start | bytes 184328 | tf_op jit(solution)/shard_map/ppermute | solution.py:21
  88.3 6.1 %collective-permute-start.29 = (f32[3,16,320]{2,1,0:T(8,128)S(1)}, f32[3,16,320]{2,1,0:T(8,128)S(1)}, u32[]{:S(2)}, u32[]{:S(2)}) collective-permute-start(f32[3,16,320]{2,1,0:T(8,128)S(1)} %get-tuple-element.120), channel_id=1, source_target_pairs={{0,2},{2,4},{4,6},{6,0},{1,3},{3,5},{5,7},{7,1},{8,10},{10,12},{12... | collective-permute-start | bytes 184328 | tf_op jit(solution)/shard_map/ppermute | solution.py:21
  96.0 4.5 %collective-permute-start.33 = (f32[16,768]{1,0:T(8,128)S(1)}, f32[16,768]{1,0:T(8,128)S(1)}, u32[]{:S(2)}, u32[]{:S(2)}) collective-permute-start(f32[16,768]{1,0:T(8,128)S(1)} %get-tuple-element.100.m0), channel_id=1, source_target_pairs={{0,16},{8,24},{16,0},{24,8},{1,17},{9,25},{17,1},{25,9},{2,18},{10... | collective-permute-start | bytes 147464 | tf_op jit(solution)/shard_map/ppermute | solution.py:21
  96.6 4.3 %collective-permute-start.32 = (f32[16,768]{1,0:T(8,128)S(1)}, f32[16,768]{1,0:T(8,128)S(1)}, u32[]{:S(2)}, u32[]{:S(2)}) collective-permute-start(f32[16,768]{1,0:T(8,128)S(1)} %get-tuple-element.100.m0), channel_id=1, source_target_pairs={{0,8},{8,16},{16,24},{24,0},{1,9},{9,17},{17,25},{25,1},{2,10},{10... | collective-permute-start | bytes 147464 | tf_op jit(solution)/shard_map/ppermute | solution.py:21
  101.1 4.3 %collective-permute-start.35 = (f32[16,448]{1,0:T(8,128)S(1)}, f32[16,448]{1,0:T(8,128)S(1)}, u32[]{:S(2)}, u32[]{:S(2)}) collective-permute-start(f32[16,448]{1,0:T(8,128)S(1)} %get-tuple-element.101), channel_id=1, source_target_pairs={{0,32},{32,64},{64,96},{96,0},{1,33},{33,65},{65,97},{97,1},{2,34}... | collective-permute-start | bytes 86024 | tf_op jit(solution)/shard_map/ppermute | solution.py:21
  102.6 4.4 %collective-permute-start.36 = (f32[16,448]{1,0:T(8,128)S(1)}, f32[16,448]{1,0:T(8,128)S(1)}, u32[]{:S(2)}, u32[]{:S(2)}) collective-permute-start(f32[16,448]{1,0:T(8,128)S(1)} %get-tuple-element.102), channel_id=1, source_target_pairs={{0,64},{32,96},{64,0},{96,32},{1,65},{33,97},{65,1},{97,33},{2,66}... | collective-permute-start | bytes 86024 | tf_op jit(solution)/shard_map/ppermute | solution.py:21
  108.5 4.8 %collective-permute-start.39 = (f32[16,1088]{1,0:T(8,128)S(1)}, f32[16,1088]{1,0:T(8,128)S(1)}, u32[]{:S(2)}, u32[]{:S(2)}) collective-permute-start(f32[16,1088]{1,0:T(8,128)S(1)} %get-tuple-element.106), channel_id=1, source_target_pairs={{0,4},{2,6},{4,0},{6,2},{1,5},{3,7},{5,1},{7,3},{8,12},{10,14},{12... | collective-permute-start | bytes 208904 | tf_op jit(solution)/shard_map/ppermute | solution.py:21
  109.0 5.1 %collective-permute-start.38 = (f32[16,1088]{1,0:T(8,128)S(1)}, f32[16,1088]{1,0:T(8,128)S(1)}, u32[]{:S(2)}, u32[]{:S(2)}) collective-permute-start(f32[16,1088]{1,0:T(8,128)S(1)} %get-tuple-element.106), channel_id=1, source_target_pairs={{0,2},{2,4},{4,6},{6,0},{1,3},{3,5},{5,7},{7,1},{8,10},{10,12},{12... | collective-permute-start | bytes 208904 | tf_op jit(solution)/shard_map/ppermute | solution.py:21
  114.1 6.9 %collective-permute-start.41 = (f32[4,16,1088]{2,1,0:T(8,128)S(1)}, f32[4,16,1088]{2,1,0:T(8,128)S(1)}, u32[]{:S(2)}, u32[]{:S(2)}) collective-permute-start(f32[4,16,1088]{2,1,0:T(8,128)S(1)} %pad_maximum_fusion.2.mine), channel_id=1, source_target_pairs={{0,1},{1,0},{2,3},{3,2},{4,5},{5,4},{6,7},{7,6},{8,9},{9,8},{10,11... | collective-permute-start | bytes 835592 | tf_op jit(solution)/shard_map/ppermute | solution.py:25
  (14 other events, 52.9 us)

commit v4 on v3

--- a/solution.py
+++ b/solution.py
@@ -18,7 +18,7 @@
 
 def shift(value, axis, distance):
     size = lax.axis_size(axis)
-    return lax.ppermute(value, axis, [(i, (i + distance) % size) for i in range(size)])
+    return lax.ppermute(value, axis, [(i, i ^ distance) for i in range(size)])
 
 
 def swapped(value):
@@ -36,7 +36,7 @@
 def scattered_pieces(kept, sent):
     row = lax.axis_index("blk_0")
     half = kept + swapped(sent)
-    pieces = [lax.dynamic_index_in_dim(half, (row + k) % 4, 0, False) for k in range(4)]
+    pieces = [lax.dynamic_index_in_dim(half, row ^ k, 0, False) for k in range(4)]
     return [pieces[0]] + [shift(pieces[k], "blk_0", k) for k in (1, 2, 3)]
 
 
@@ -74,7 +74,7 @@
     total_b = weighted(co, 16, bs)
     group = lax.axis_index("day_0")
     for k, out in ((1, out1), (2, out2), (3, out3)):
-        out[:, :320] = jnp.where(group + k < 4, total_f, total_b)
+        out[:, :320] = jnp.where((group ^ k) > group, total_f, total_b)
         out[:, 320:] = pack
 
 
@@ -89,8 +89,9 @@
     for k, r in ((1, r1), (2, r2), (3, r3)):
         packs.append(r[:, 320:])
         value = co[19 + k : 20 + k] * r[:, :320]
-        far_f = far_f + jnp.where(group >= k, value, 0.0)
-        far_b = far_b + jnp.where(group >= k, 0.0, value)
+        earlier = (group ^ k) < group
+        far_f = far_f + jnp.where(earlier, value, 0.0)
+        far_b = far_b + jnp.where(earlier, 0.0, value)
     come_f = local[0] + co[23:24] * far_f
     come_b = local[1] + co[24:25] * far_b
     raise_days(come_f, come_b, w, co, v, message, ring_sum(packs))
@@ -152,7 +153,6 @@
 
 
 VMEM_BLOCK = pl.BlockSpec(memory_space=pltpu.VMEM)
-SMEM_BLOCK = pl.BlockSpec(memory_space=pltpu.SMEM)
 ANY_BLOCK = pl.BlockSpec(memory_space=pl.ANY)
 HBM_BLOCK = pl.BlockSpec(memory_space=pltpu.HBM)
 
@@ -238,7 +238,7 @@
 def ordered(kept, messages, place):
     for k, message in enumerate(messages):
         kept[k] = message[...]
-    return [kept[lax.rem(place + (4 - j), 4)] for j in range(4)]
+    return [kept[place ^ j] for j in range(4)]
 
 
 def first_middle_kernel(m0, m1, m2, m3, *refs):
@@ -310,13 +310,13 @@
     rows = [pick(values, place) for values in (gain0, gain1, next_gain, dec0, dec1, after_decay)]
     local_f, local_b, total_f, total_b, far = [], [], [], [], []
     for k in range(4):
-        source = lax.rem(place + (4 - k), 4)
+        source = place ^ k
         total_f.append(product(mine, source + 1, 4))
         total_b.append(product(mine, 0, source))
         if k:
             local_f.append(jnp.where(source < place, product(mine, source + 1, place), zero))
             local_b.append(jnp.where(source > place, product(mine, place + 1, source), zero))
-            origin = lax.rem(group + (4 - k), 4)
+            origin = group ^ k
             far.append(product(whole, jnp.minimum(origin, group) + 1, jnp.maximum(origin, group)))
     before, after = product(mine, 0, place), product(mine, place + 1, 4)
     rows += local_f + local_b + total_f + total_b + far + [before, after]
@@ -475,7 +475,7 @@
     row, core = lax.axis_index("blk_0"), lax.axis_index("blk_1")
     packs = []
     for k in range(4):
-        at = pl.multiple_of(lax.rem(row + (4 - k), 4) * 640, 128)
+        at = pl.multiple_of((row ^ k) * 640, 128)
         for day in range(3):
             a = mine[k, :, day * 320 : day * 320 + 320]
             b = other[k, :, day * 320 : day * 320 + 320]
@@ -705,7 +705,7 @@
         spread[day, :, 128:] = low
         covariates[day] = stacked_halves(covs[:, day, :])
         slot = lax.broadcasted_iota(jnp.int32, (1, 128), 1) + slot_start
-        slot_weight = jnp.where(slot < count[day], prec[day : day + 1], 0.0)
+        slot_weight = jnp.where(slot < count[0:1, day : day + 1], prec[day : day + 1], 0.0)
         weight[day : day + 1] = slot_weight
         weighted_value = jnp.broadcast_to(slot_weight * value[day : day + 1], (16, 128))
         grad = spread_out(weighted_value, spread[day])[:1]
@@ -726,9 +726,8 @@
             pltpu.VMEM((2, 2560, 256), BF16), shaped(2, 128), shaped(4, 2, 320), shaped(4, 2, 320),
             shaped(1, 64), pltpu.VMEM((2, 128, 128), BF16),
         ),
-        [SMEM_BLOCK] + [whole_block(o) for o in operands[1:]],
-        operands[0],
-        *(pltpu.with_memory_space_constraint(o, pltpu.HBM) for o in operands[1:]),
+        [whole_block(o) for o in operands],
+        *(pltpu.with_memory_space_constraint(o, pltpu.HBM) for o in operands),
         grid=(1,),
         scratch=[pltpu.VMEM((8, 5120), F32)],
     )
@@ -757,7 +756,7 @@
     both = jnp.concatenate([1.0 - leakage, dominant])
 
     spread, weight, kept, sent, grad_cov, covs = setup_stage(
-        obs_count, triangles, obs_triangle, obs_bary, obs_prec, obs_value, covariates
+        obs_count.reshape(1, 2), triangles, obs_triangle, obs_bary, obs_prec, obs_value, covariates
     )
     off_pair = [split_blocks(off_blocks, "split_off", day) for day in range(2)]
     diag_pair = [split_blocks(diag_blocks, "split_diag", day) for day in range(2)]

time: 140 us -> 138 us (0.986)
  waiting for transfers between devices: 35.8 us -> 26.4 us
  starting transfers between devices: 55 us -> 63.3 us
    ppermute x36, waiting for transfers between devices: 29.8 us -> 20.4 us  [shift(): return lax.ppermute(value, axis, [(i, i ^ distance) for i in range(size)])]
    ppermute x36, starting transfers between devices: 35.5 us -> 42.2 us  [shift(): return lax.ppermute(value, axis, [(i, i ^ distance) for i in range(size)])]
    ppermute x6, starting transfers between devices: 19.5 us -> 21.2 us  [swapped(): return lax.ppermute(value, 'blk_1', [(0, 1), (1, 0)])]
  transfers between devices with their start and end apart: 42 -> 42, of which waited for: 33 -> 24; matrix products, arithmetic and copies ran while one was open for 2% -> 2% of each run, Pallas kernels for 12% -> 12%
where the time goes in v4:
time: 138 us
  starting transfers between devices  63.3 us (46%)
  Pallas kernels  30.1 us (22%)
  waiting for transfers between devices  26.4 us (19%)
  blocking collectives  14.7 us (11%)
  other arithmetic  2.33 us (2%)
    ppermute x36, starting transfers between devices, shift(): return lax.ppermute(value, axis, [(i, i ^ distance) for i in range(size)])  42.2 us
    pallas_call x22, Pallas kernels, call(): pl.pallas_call(kernel, grid=grid, out_shape=outs, in_specs=in_specs, out_...  30.1 us
    ppermute x6, starting transfers between devices, swapped(): return lax.ppermute(value, 'blk_1', [(0, 1), (1, 0)])  21.2 us
    ppermute x36, waiting for transfers between devices, shift(): return lax.ppermute(value, axis, [(i, i ^ distance) for i in range(size)])  20.4 us
    all_to_all x1, blocking collectives, on_device(): sums = lax.all_to_all(sums, DAY + BLK, 0, 0, tiled=True)  14.7 us
    ppermute x6, waiting for transfers between devices, swapped(): return lax.ppermute(value, 'blk_1', [(0, 1), (1, 0)])  6.04 us
  transfers between devices with their start and end apart: 42, of which 24 were waited for; matrix products, arithmetic and copies ran while one was open for 2% of the time, Pallas kernels for 12%

profile of v4, /device:TPU:1, one launch (start us, length us, event | category | flops | bytes accessed | tf_op | source)
XLA Modules:
  0.0 137.9 jit_solution(9959620949538702388)
XLA Ops:
  0.6 3.7 %setup_stage.1 = (bf16[2,2560,256]{2,1,0:T(8,128)(2,1)S(1)}, f32[2,128]{1,0:T(2,128)S(1)}, f32[4,2,320]{2,1,0:T(2,128)S(1)}, f32[4,2,320]{2,1,0:T(2,128)S(1)}, f...) custom-call(s32[1,2]{1,0:T(1,128)} %bitcast.58, s32[3,5116]{1,0:T(4,128)} %triangles.1, s32[2,128]{1,0:T(2,128)} %cells.1, ...), custom_call_target="tpu_custom_call" | custom-call | tf_op jit(solution)/shard_map/setup_stage/pallas_call | solution.py:169
  4.3 1.4 %collective-permute-start = (f32[4,2,320]{2,1,0:T(2,128)S(1)}, f32[4,2,320]{2,1,0:T(2,128)S(1)}, u32[]{:S(2)}, u32[]{:S(2)}) collective-permute-start(f32[4,2,320]{2,1,0:T(2,128)S(1)} %get-tuple-element.61), channel_id=1, source_target_pairs={{0,1},{1,0},{2,3},{3,2},{4,5},{5,4},{6,7},{7,6},{8,9},{9,8},{10,11... | collective-permute-start | bytes 30728 | tf_op jit(solution)/shard_map/ppermute | solution.py:25
  6.5 1.5 %select_reduce_fusion = f32[2,320]{1,0:T(2,128)S(1)} fusion(f32[2,320,2560]{2,1,0:T(8,128)} %source.7, s32[]{:T(128)S(6)} %select_n.33), kind=kLoop, calls=%fused_computation | loop fusion | flops 613760 | bytes 821764 | tf_op jit(solution)/shard_map/reduce_sum | solution.py:755
  8.0 2.8 %collective-permute-start.3 = (f32[2,320]{1,0:T(2,128)S(1)}, f32[2,320]{1,0:T(2,128)S(1)}, u32[]{:S(2)}, u32[]{:S(2)}) collective-permute-start(f32[2,320]{1,0:T(2,128)S(1)} %get-tuple-element.126), channel_id=1, source_target_pairs={{0,6},{2,4},{4,2},{6,0},{1,7},{3,5},{5,3},{7,1},{8,14},{10,12},{12... | collective-permute-start | bytes 7688 | tf_op jit(solution)/shard_map/ppermute | solution.py:21
  11.5 2.0 %split_off0.1.refs_0_.o0 = bf16[640,2560]{1,0:T(8,128)(2,1)S(1)} custom-call(f32[2,320,2560]{2,1,0:T(8,128)} %source.5), custom_call_target="tpu_custom_call" | custom-call | tf_op jit(solution)/shard_map/split_off0/pallas_call | solution.py:169
  14.9 2.5 %collective-permute-start.6 = (f32[16,768]{1,0:T(8,128)S(1)}, f32[16,768]{1,0:T(8,128)S(1)}, u32[]{:S(2)}, u32[]{:S(2)}) collective-permute-start(f32[16,768]{1,0:T(8,128)S(1)} %get-tuple-element.63.m0), channel_id=1, source_target_pairs={{0,24},{8,16},{16,8},{24,0},{1,25},{9,17},{17,9},{25,1},{2,26},{10... | collective-permute-start | bytes 147464 | tf_op jit(solution)/shard_map/ppermute | solution.py:21
  18.1 2.0 %split_off1.1.refs_0_.o1 = bf16[640,2560]{1,0:T(8,128)(2,1)S(1)} custom-call(f32[2,320,2560]{2,1,0:T(8,128)} %source.5), custom_call_target="tpu_custom_call" | custom-call | tf_op jit(solution)/shard_map/split_off1/pallas_call | solution.py:169
  20.2 1.6 %collective-permute-done.5.m2 = f32[16,768]{1,0:T(8,128)S(1)} collective-permute-done((f32[16,768]{1,0:T(8,128)S(1)}, f32[16,768]{1,0:T(8,128)S(1)}, u32[]{:S(2)}, u32[]{:S(2)}) %collective-permute-start.5) | collective-permute-done | bytes 49184 | tf_op jit(solution)/shard_map/ppermute | solution.py:21
  22.1 3.8 %collective-permute-start.9 = (f32[16,768]{1,0:T(8,128)S(1)}, f32[16,768]{1,0:T(8,128)S(1)}, u32[]{:S(2)}, u32[]{:S(2)}) collective-permute-start(f32[16,768]{1,0:T(8,128)S(1)} %get-tuple-element.64.z0), channel_id=1, source_target_pairs={{0,96},{32,64},{64,32},{96,0},{1,97},{33,65},{65,33},{97,1},{2,98}... | collective-permute-start | bytes 147464 | tf_op jit(solution)/shard_map/ppermute | solution.py:21
  26.6 2.0 %split_diag0.1.refs_0_.a0 = bf16[640,2560]{1,0:T(8,128)(2,1)S(1)} custom-call(f32[2,320,2560]{2,1,0:T(8,128)} %source.7), custom_call_target="tpu_custom_call" | custom-call | tf_op jit(solution)/shard_map/split_diag0/pallas_call | solution.py:169
  28.6 1.8 %collective-permute-done.8.z2 = f32[16,768]{1,0:T(8,128)S(1)} collective-permute-done((f32[16,768]{1,0:T(8,128)S(1)}, f32[16,768]{1,0:T(8,128)S(1)}, u32[]{:S(2)}, u32[]{:S(2)}) %collective-permute-start.8) | collective-permute-done | bytes 49184 | tf_op jit(solution)/shard_map/ppermute | solution.py:21
  31.5 1.5 %collective-permute-start.12 = (f32[16,1088]{1,0:T(8,128)S(1)}, f32[16,1088]{1,0:T(8,128)S(1)}, u32[]{:S(2)}, u32[]{:S(2)}) collective-permute-start(f32[16,1088]{1,0:T(8,128)S(1)} %get-tuple-element.67), channel_id=1, source_target_pairs={{0,6},{2,4},{4,2},{6,0},{1,7},{3,5},{5,3},{7,1},{8,14},{10,12},{12... | collective-permute-start | bytes 208904 | tf_op jit(solution)/shard_map/ppermute | solution.py:21
  34.7 2.0 %split_diag1.1.a1 = bf16[640,2560]{1,0:T(8,128)(2,1)S(1)} custom-call(f32[2,320,2560]{2,1,0:T(8,128)} %source.7), custom_call_target="tpu_custom_call" | custom-call | tf_op jit(solution)/shard_map/split_diag1/pallas_call | solution.py:169
  36.8 2.3 %own_terms.2.behind.behind1 = f32[3,16,2560]{2,1,0:T(8,128)S(1)} custom-call(bf16[640,2560]{1,0:T(8,128)(2,1)S(1)} %split_diag0.1.refs_0_.a0, bf16[640,2560]{1,0:T(8,128)(2,1)S(1)} %split_diag1.1.a1, bf16[640,2560]{1,0:T(8,128)(2,1)S(1)} %split_off0.1.refs_0_.o0, bf16[640,2560]{1,0:T(8,128)(2,1)S(1)} %split_off1.1.refs_0_.o1, ...), custom_call_target="tpu_custom_call" | custom-call | tf_op jit(solution)/shard_map/own_terms/pallas_call | solution.py:169
  39.1 5.3 %collective-permute-start.13 = (f32[4,16,1088]{2,1,0:T(8,128)S(1)}, f32[4,16,1088]{2,1,0:T(8,128)S(1)}, u32[]{:S(2)}, u32[]{:S(2)}) collective-permute-start(f32[4,16,1088]{2,1,0:T(8,128)S(1)} %pad_maximum_fusion.mine), channel_id=1, source_target_pairs={{0,1},{1,0},{2,3},{3,2},{4,5},{5,4},{6,7},{7,6},{8,9},{9,8},{10,11... | collective-permute-start | bytes 835592 | tf_op jit(solution)/shard_map/ppermute | solution.py:25
  45.6 1.5 %first_stage.1 = (f32[4,3,16,320]{3,2,1,0:T(8,128)S(1)}, f32[4,3,16,320]{3,2,1,0:T(8,128)S(1)}, f32[16,64]{1,0:T(8,128)S(1)}, f32[3,16,2560]{2,1,0:T(8,128)S(1)}, f32[16,64]{1,0:T(8,128)S(1)}) custom-call(f32[4,16,1088]{2,1,0:T(8,128)S(1)} %pad_maximum_fusion.mine, f32[4,16,1088]{2,1,0:T(8,128)S(1)} %collective-permute-done.13.other, ...), custom_call_target="tpu_custom_call" | custom-call | tf_op jit(solution)/shard_map/first_stage/pallas_call | solution.py:169
  52.2 2.0 %first_rows.1 = (f32[2,16,320]{2,1,0:T(8,128)S(1)}, f32[16,64]{1,0:T(8,128)S(1)}) custom-call(bf16[640,2560]{1,0:T(8,128)(2,1)S(1)} %split_off0.1.refs_0_.o0, bf16[640,2560]{1,0:T(8,128)(2,1)S(1)} %split_off1.1.refs_0_.o1, f32[3,16,2560]{2,1,0:T(8,128)S(1)} %get-tuple-element.76.whole.whole1, f32[2,16,320]{2,1,0:T(8,128)S(1)} %get-tuple-element.66.bx, ...), custom_call_target="tpu_custom_call" | custom-call | tf_op jit(solution)/shard_map/first_rows/pallas_call | solution.py:169
  61.5 2.0 %collective-permute-start.22 = (f32[16,448]{1,0:T(8,128)S(1)}, f32[16,448]{1,0:T(8,128)S(1)}, u32[]{:S(2)}, u32[]{:S(2)}) collective-permute-start(f32[16,448]{1,0:T(8,128)S(1)} %get-tuple-element.83), channel_id=1, source_target_pairs={{0,64},{32,96},{64,0},{96,32},{1,65},{33,97},{65,1},{97,33},{2,66}... | collective-permute-start | bytes 86024 | tf_op jit(solution)/shard_map/ppermute | solution.py:21
  63.4 1.9 %collective-permute-start.23 = (f32[16,448]{1,0:T(8,128)S(1)}, f32[16,448]{1,0:T(8,128)S(1)}, u32[]{:S(2)}, u32[]{:S(2)}) collective-permute-start(f32[16,448]{1,0:T(8,128)S(1)} %get-tuple-element.84), channel_id=1, source_target_pairs={{0,96},{32,64},{64,32},{96,0},{1,97},{33,65},{65,33},{97,1},{2,98}... | collective-permute-start | bytes 86024 | tf_op jit(solution)/shard_map/ppermute | solution.py:21
  65.8 1.6 %collective-permute-done.23.r3 = f32[16,448]{1,0:T(8,128)S(1)} collective-permute-done((f32[16,448]{1,0:T(8,128)S(1)}, f32[16,448]{1,0:T(8,128)S(1)}, u32[]{:S(2)}, u32[]{:S(2)}) %collective-permute-start.23) | collective-permute-done | bytes 28704 | tf_op jit(solution)/shard_map/ppermute | solution.py:21
  70.8 2.3 %own_terms.3.behind2 = f32[3,16,2560]{2,1,0:T(8,128)S(1)} custom-call(bf16[640,2560]{1,0:T(8,128)(2,1)S(1)} %split_diag0.1.refs_0_.a0, bf16[640,2560]{1,0:T(8,128)(2,1)S(1)} %split_diag1.1.a1, bf16[640,2560]{1,0:T(8,128)(2,1)S(1)} %split_off0.1.refs_0_.o0, bf16[640,2560]{1,0:T(8,128)(2,1)S(1)} %split_off1.1.refs_0_.o1, ...), custom_call_target="tpu_custom_call" | custom-call | tf_op jit(solution)/shard_map/own_terms/pallas_call | solution.py:169
  73.5 6.6 %collective-permute-start.27 = (f32[4,16,1088]{2,1,0:T(8,128)S(1)}, f32[4,16,1088]{2,1,0:T(8,128)S(1)}, u32[]{:S(2)}, u32[]{:S(2)}) collective-permute-start(f32[4,16,1088]{2,1,0:T(8,128)S(1)} %pad_maximum_fusion.1.mine), channel_id=1, source_target_pairs={{0,1},{1,0},{2,3},{3,2},{4,5},{5,4},{6,7},{7,6},{8,9},{9,8},{10,11... | collective-permute-start | bytes 835592 | tf_op jit(solution)/shard_map/ppermute | solution.py:25
  81.3 1.9 %second_stage.1 = (f32[4,3,16,320]{3,2,1,0:T(8,128)S(1)}, f32[4,3,16,320]{3,2,1,0:T(8,128)S(1)}, f32[16,64]{1,0:T(8,128)S(1)}, f32[3,16,2560]{2,1,0:T(8,128)S(1)...) custom-call(f32[4,16,1088]{2,1,0:T(8,128)S(1)} %pad_maximum_fusion.1.mine, ...), custom_call_target="tpu_custom_call" | custom-call | tf_op jit(solution)/shard_map/second_stage/pallas_call | solution.py:169
  88.3 2.0 %second_rows.1 = (f32[2,16,320]{2,1,0:T(8,128)S(1)}, f32[16,64]{1,0:T(8,128)S(1)}, f32[3,16,320]{2,1,0:T(8,128)S(1)}, f32[3,16,320]{2,1,0:T(8,128)S(1)}) custom-call(bf16[640,2560]{1,0:T(8,128)(2,1)S(1)} %split_off0.1.refs_0_.o0, bf16[640,2560]{1,0:T(8,128)(2,1)S(1)} %split_off1.1.refs_0_.o1, f32[3,16,2560]{2,1,0:T(8,128)S(1)} %get-tuple-element.94.whole.z1whole, ...), custom_call_target="tpu_custom_call" | custom-call | tf_op jit(solution)/shard_map/second_rows/pallas_call | solution.py:169
  91.4 1.6 %collective-permute-start.34 = (f32[16,768]{1,0:T(8,128)S(1)}, f32[16,768]{1,0:T(8,128)S(1)}, u32[]{:S(2)}, u32[]{:S(2)}) collective-permute-start(f32[16,768]{1,0:T(8,128)S(1)} %get-tuple-element.100.m0), channel_id=1, source_target_pairs={{0,24},{8,16},{16,8},{24,0},{1,25},{9,17},{17,9},{25,1},{2,26},{10... | collective-permute-start | bytes 147464 | tf_op jit(solution)/shard_map/ppermute | solution.py:21
  95.6 1.9 %collective-permute-done.33.m2 = f32[16,768]{1,0:T(8,128)S(1)} collective-permute-done((f32[16,768]{1,0:T(8,128)S(1)}, f32[16,768]{1,0:T(8,128)S(1)}, u32[]{:S(2)}, u32[]{:S(2)}) %collective-permute-start.33) | collective-permute-done | bytes 49184 | tf_op jit(solution)/shard_map/ppermute | solution.py:21
  97.7 3.0 %collective-permute-start.36 = (f32[16,448]{1,0:T(8,128)S(1)}, f32[16,448]{1,0:T(8,128)S(1)}, u32[]{:S(2)}, u32[]{:S(2)}) collective-permute-start(f32[16,448]{1,0:T(8,128)S(1)} %get-tuple-element.102), channel_id=1, source_target_pairs={{0,64},{32,96},{64,0},{96,32},{1,65},{33,97},{65,1},{97,33},{2,66}... | collective-permute-start | bytes 86024 | tf_op jit(solution)/shard_map/ppermute | solution.py:21
  102.4 2.3 %collective-permute-done.37.r3 = f32[16,448]{1,0:T(8,128)S(1)} collective-permute-done((f32[16,448]{1,0:T(8,128)S(1)}, f32[16,448]{1,0:T(8,128)S(1)}, u32[]{:S(2)}, u32[]{:S(2)}) %collective-permute-start.37) | collective-permute-done | bytes 28704 | tf_op jit(solution)/shard_map/ppermute | solution.py:21
  106.1 1.7 %collective-permute-start.39 = (f32[16,1088]{1,0:T(8,128)S(1)}, f32[16,1088]{1,0:T(8,128)S(1)}, u32[]{:S(2)}, u32[]{:S(2)}) collective-permute-start(f32[16,1088]{1,0:T(8,128)S(1)} %get-tuple-element.106), channel_id=1, source_target_pairs={{0,4},{2,6},{4,0},{6,2},{1,5},{3,7},{5,1},{7,3},{8,12},{10,14},{12... | collective-permute-start | bytes 208904 | tf_op jit(solution)/shard_map/ppermute | solution.py:21
  111.0 6.9 %collective-permute-start.41 = (f32[4,16,1088]{2,1,0:T(8,128)S(1)}, f32[4,16,1088]{2,1,0:T(8,128)S(1)}, u32[]{:S(2)}, u32[]{:S(2)}) collective-permute-start(f32[4,16,1088]{2,1,0:T(8,128)S(1)} %pad_maximum_fusion.2.mine), channel_id=1, source_target_pairs={{0,1},{1,0},{2,3},{3,2},{4,5},{5,4},{6,7},{7,6},{8,9},{9,8},{10,11... | collective-permute-start | bytes 835592 | tf_op jit(solution)/shard_map/ppermute | solution.py:25
  119.1 3.0 %third_stage.1 = (f32[128,128]{1,0:T(8,128)S(1)}, f32[2,16,320]{2,1,0:T(8,128)S(1)}, f32[2,16,320]{2,1,0:T(8,128)S(1)}, f32[16,128]{1,0:T(8,128)S(1)}, f32[2,16,64]{2,1,0:T(8,128)S(1)}) custom-call(f32[4,16,1088]{2,1,0:T(8,128)S(1)} %pad_maximum_fusion.2.mine, f32[4,16,1088]{2,1,0:T(8,128)S(1)} %collective-permute-done.41.other, ...), custom_call_target="tpu_custom_call" | custom-call | tf_op jit(solution)/shard_map/third_stage/pallas_call | solution.py:169
  122.1 14.7 %all_to_all.11 = f32[128,1,128]{2,1,0:T(1,128)S(1)} all-to-all(f32[128,1,128]{2,1,0:T(1,128)S(1)} %bitcast.46), channel_id=1, replica_groups=mesh['day_0'=4,'day_1'=4,'blk_0'=4,'blk_1'=2] {'day_0','day_1','blk_0','..., dimensions={0} | all-to-all | bytes 131072 | tf_op jit(solution)/shard_map/all_to_all | solution.py:789
  (94 shorter events, 43.9 us)
Async XLA Ops:
  8.0 5.5 %collective-permute-start.3 = (f32[2,320]{1,0:T(2,128)S(1)}, f32[2,320]{1,0:T(2,128)S(1)}, u32[]{:S(2)}, u32[]{:S(2)}) collective-permute-start(f32[2,320]{1,0:T(2,128)S(1)} %get-tuple-element.126), channel_id=1, source_target_pairs={{0,6},{2,4},{4,2},{6,0},{1,7},{3,5},{5,3},{7,1},{8,14},{10,12},{12... | collective-permute-start | bytes 7688 | tf_op jit(solution)/shard_map/ppermute | solution.py:21
  10.8 4.0 %collective-permute-start.2 = (f32[2,320]{1,0:T(2,128)S(1)}, f32[2,320]{1,0:T(2,128)S(1)}, u32[]{:S(2)}, u32[]{:S(2)}) collective-permute-start(f32[2,320]{1,0:T(2,128)S(1)} %get-tuple-element.127), channel_id=1, source_target_pairs={{0,4},{2,6},{4,0},{6,2},{1,5},{3,7},{5,1},{7,3},{8,12},{10,14},{12... | collective-permute-start | bytes 7688 | tf_op jit(solution)/shard_map/ppermute | solution.py:21
  14.9 5.3 %collective-permute-start.6 = (f32[16,768]{1,0:T(8,128)S(1)}, f32[16,768]{1,0:T(8,128)S(1)}, u32[]{:S(2)}, u32[]{:S(2)}) collective-permute-start(f32[16,768]{1,0:T(8,128)S(1)} %get-tuple-element.63.m0), channel_id=1, source_target_pairs={{0,24},{8,16},{16,8},{24,0},{1,25},{9,17},{17,9},{25,1},{2,26},{10... | collective-permute-start | bytes 147464 | tf_op jit(solution)/shard_map/ppermute | solution.py:21
  17.4 4.4 %collective-permute-start.5 = (f32[16,768]{1,0:T(8,128)S(1)}, f32[16,768]{1,0:T(8,128)S(1)}, u32[]{:S(2)}, u32[]{:S(2)}) collective-permute-start(f32[16,768]{1,0:T(8,128)S(1)} %get-tuple-element.63.m0), channel_id=1, source_target_pairs={{0,16},{8,24},{16,0},{24,8},{1,17},{9,25},{17,1},{25,9},{2,18},{10... | collective-permute-start | bytes 147464 | tf_op jit(solution)/shard_map/ppermute | solution.py:21
  22.1 6.5 %collective-permute-start.9 = (f32[16,768]{1,0:T(8,128)S(1)}, f32[16,768]{1,0:T(8,128)S(1)}, u32[]{:S(2)}, u32[]{:S(2)}) collective-permute-start(f32[16,768]{1,0:T(8,128)S(1)} %get-tuple-element.64.z0), channel_id=1, source_target_pairs={{0,96},{32,64},{64,32},{96,0},{1,97},{33,65},{65,33},{97,1},{2,98}... | collective-permute-start | bytes 147464 | tf_op jit(solution)/shard_map/ppermute | solution.py:21
  25.9 4.5 %collective-permute-start.8 = (f32[16,768]{1,0:T(8,128)S(1)}, f32[16,768]{1,0:T(8,128)S(1)}, u32[]{:S(2)}, u32[]{:S(2)}) collective-permute-start(f32[16,768]{1,0:T(8,128)S(1)} %get-tuple-element.64.z0), channel_id=1, source_target_pairs={{0,64},{32,96},{64,0},{96,32},{1,65},{33,97},{65,1},{97,33},{2,66}... | collective-permute-start | bytes 147464 | tf_op jit(solution)/shard_map/ppermute | solution.py:21
  25.9 4.5 %collective-permute-start.7 = (f32[16,768]{1,0:T(8,128)S(1)}, f32[16,768]{1,0:T(8,128)S(1)}, u32[]{:S(2)}, u32[]{:S(2)}) collective-permute-start(f32[16,768]{1,0:T(8,128)S(1)} %get-tuple-element.64.z0), channel_id=1, source_target_pairs={{0,32},{32,0},{64,96},{96,64},{1,33},{33,1},{65,97},{97,65},{2,34}... | collective-permute-start | bytes 147464 | tf_op jit(solution)/shard_map/ppermute | solution.py:21
  31.5 7.6 %collective-permute-start.12 = (f32[16,1088]{1,0:T(8,128)S(1)}, f32[16,1088]{1,0:T(8,128)S(1)}, u32[]{:S(2)}, u32[]{:S(2)}) collective-permute-start(f32[16,1088]{1,0:T(8,128)S(1)} %get-tuple-element.67), channel_id=1, source_target_pairs={{0,6},{2,4},{4,2},{6,0},{1,7},{3,5},{5,3},{7,1},{8,14},{10,12},{12... | collective-permute-start | bytes 208904 | tf_op jit(solution)/shard_map/ppermute | solution.py:21
  33.0 6.1 %collective-permute-start.11 = (f32[16,1088]{1,0:T(8,128)S(1)}, f32[16,1088]{1,0:T(8,128)S(1)}, u32[]{:S(2)}, u32[]{:S(2)}) collective-permute-start(f32[16,1088]{1,0:T(8,128)S(1)} %get-tuple-element.67), channel_id=1, source_target_pairs={{0,4},{2,6},{4,0},{6,2},{1,5},{3,7},{5,1},{7,3},{8,12},{10,14},{12... | collective-permute-start | bytes 208904 | tf_op jit(solution)/shard_map/ppermute | solution.py:21
  33.4 5.6 %collective-permute-start.10 = (f32[16,1088]{1,0:T(8,128)S(1)}, f32[16,1088]{1,0:T(8,128)S(1)}, u32[]{:S(2)}, u32[]{:S(2)}) collective-permute-start(f32[16,1088]{1,0:T(8,128)S(1)} %get-tuple-element.67), channel_id=1, source_target_pairs={{0,2},{2,0},{4,6},{6,4},{1,3},{3,1},{5,7},{7,5},{8,10},{10,8},{12,... | collective-permute-start | bytes 208904 | tf_op jit(solution)/shard_map/ppermute | solution.py:21
  39.1 6.5 %collective-permute-start.13 = (f32[4,16,1088]{2,1,0:T(8,128)S(1)}, f32[4,16,1088]{2,1,0:T(8,128)S(1)}, u32[]{:S(2)}, u32[]{:S(2)}) collective-permute-start(f32[4,16,1088]{2,1,0:T(8,128)S(1)} %pad_maximum_fusion.mine), channel_id=1, source_target_pairs={{0,1},{1,0},{2,3},{3,2},{4,5},{5,4},{6,7},{7,6},{8,9},{9,8},{10,11... | collective-permute-start | bytes 835592 | tf_op jit(solution)/shard_map/ppermute | solution.py:25
  48.9 5.4 %collective-permute-start.17 = (f32[3,16,320]{2,1,0:T(8,128)S(1)}, f32[3,16,320]{2,1,0:T(8,128)S(1)}, u32[]{:S(2)}, u32[]{:S(2)}) collective-permute-start(f32[3,16,320]{2,1,0:T(8,128)S(1)} %get-tuple-element.122), channel_id=1, source_target_pairs={{0,6},{2,4},{4,2},{6,0},{1,7},{3,5},{5,3},{7,1},{8,14},{10,12},{12... | collective-permute-start | bytes 184328 | tf_op jit(solution)/shard_map/ppermute | solution.py:21
  50.0 4.8 %collective-permute-start.16 = (f32[3,16,320]{2,1,0:T(8,128)S(1)}, f32[3,16,320]{2,1,0:T(8,128)S(1)}, u32[]{:S(2)}, u32[]{:S(2)}) collective-permute-start(f32[3,16,320]{2,1,0:T(8,128)S(1)} %get-tuple-element.123), channel_id=1, source_target_pairs={{0,4},{2,6},{4,0},{6,2},{1,5},{3,7},{5,1},{7,3},{8,12},{10,14},{12... | collective-permute-start | bytes 184328 | tf_op jit(solution)/shard_map/ppermute | solution.py:21
  51.0 4.5 %collective-permute-start.15 = (f32[3,16,320]{2,1,0:T(8,128)S(1)}, f32[3,16,320]{2,1,0:T(8,128)S(1)}, u32[]{:S(2)}, u32[]{:S(2)}) collective-permute-start(f32[3,16,320]{2,1,0:T(8,128)S(1)} %get-tuple-element.124), channel_id=1, source_target_pairs={{0,2},{2,0},{4,6},{6,4},{1,3},{3,1},{5,7},{7,5},{8,10},{10,8},{12,... | collective-permute-start | bytes 184328 | tf_op jit(solution)/shard_map/ppermute | solution.py:21
  55.7 4.2 %collective-permute-start.20 = (f32[16,768]{1,0:T(8,128)S(1)}, f32[16,768]{1,0:T(8,128)S(1)}, u32[]{:S(2)}, u32[]{:S(2)}) collective-permute-start(f32[16,768]{1,0:T(8,128)S(1)} %get-tuple-element.81.m0), channel_id=1, source_target_pairs={{0,24},{8,16},{16,8},{24,0},{1,25},{9,17},{17,9},{25,1},{2,26},{10... | collective-permute-start | bytes 147464 | tf_op jit(solution)/shard_map/ppermute | solution.py:21
  56.8 4.4 %collective-permute-start.19 = (f32[16,768]{1,0:T(8,128)S(1)}, f32[16,768]{1,0:T(8,128)S(1)}, u32[]{:S(2)}, u32[]{:S(2)}) collective-permute-start(f32[16,768]{1,0:T(8,128)S(1)} %get-tuple-element.81.m0), channel_id=1, source_target_pairs={{0,16},{8,24},{16,0},{24,8},{1,17},{9,25},{17,1},{25,9},{2,18},{10... | collective-permute-start | bytes 147464 | tf_op jit(solution)/shard_map/ppermute | solution.py:21
  61.4 3.9 %collective-permute-start.21 = (f32[16,448]{1,0:T(8,128)S(1)}, f32[16,448]{1,0:T(8,128)S(1)}, u32[]{:S(2)}, u32[]{:S(2)}) collective-permute-start(f32[16,448]{1,0:T(8,128)S(1)} %get-tuple-element.82), channel_id=1, source_target_pairs={{0,32},{32,0},{64,96},{96,64},{1,33},{33,1},{65,97},{97,65},{2,34}... | collective-permute-start | bytes 86024 | tf_op jit(solution)/shard_map/ppermute | solution.py:21
  61.5 4.3 %collective-permute-start.22 = (f32[16,448]{1,0:T(8,128)S(1)}, f32[16,448]{1,0:T(8,128)S(1)}, u32[]{:S(2)}, u32[]{:S(2)}) collective-permute-start(f32[16,448]{1,0:T(8,128)S(1)} %get-tuple-element.83), channel_id=1, source_target_pairs={{0,64},{32,96},{64,0},{96,32},{1,65},{33,97},{65,1},{97,33},{2,66}... | collective-permute-start | bytes 86024 | tf_op jit(solution)/shard_map/ppermute | solution.py:21
  63.4 4.0 %collective-permute-start.23 = (f32[16,448]{1,0:T(8,128)S(1)}, f32[16,448]{1,0:T(8,128)S(1)}, u32[]{:S(2)}, u32[]{:S(2)}) collective-permute-start(f32[16,448]{1,0:T(8,128)S(1)} %get-tuple-element.84), channel_id=1, source_target_pairs={{0,96},{32,64},{64,32},{96,0},{1,97},{33,65},{65,33},{97,1},{2,98}... | collective-permute-start | bytes 86024 | tf_op jit(solution)/shard_map/ppermute | solution.py:21
  67.5 5.6 %collective-permute-start.26 = (f32[16,1088]{1,0:T(8,128)S(1)}, f32[16,1088]{1,0:T(8,128)S(1)}, u32[]{:S(2)}, u32[]{:S(2)}) collective-permute-start(f32[16,1088]{1,0:T(8,128)S(1)} %get-tuple-element.87), channel_id=1, source_target_pairs={{0,6},{2,4},{4,2},{6,0},{1,7},{3,5},{5,3},{7,1},{8,14},{10,12},{12... | collective-permute-start | bytes 208904 | tf_op jit(solution)/shard_map/ppermute | solution.py:21
  68.8 4.7 %collective-permute-start.25 = (f32[16,1088]{1,0:T(8,128)S(1)}, f32[16,1088]{1,0:T(8,128)S(1)}, u32[]{:S(2)}, u32[]{:S(2)}) collective-permute-start(f32[16,1088]{1,0:T(8,128)S(1)} %get-tuple-element.87), channel_id=1, source_target_pairs={{0,4},{2,6},{4,0},{6,2},{1,5},{3,7},{5,1},{7,3},{8,12},{10,14},{12... | collective-permute-start | bytes 208904 | tf_op jit(solution)/shard_map/ppermute | solution.py:21
  73.5 7.8 %collective-permute-start.27 = (f32[4,16,1088]{2,1,0:T(8,128)S(1)}, f32[4,16,1088]{2,1,0:T(8,128)S(1)}, u32[]{:S(2)}, u32[]{:S(2)}) collective-permute-start(f32[4,16,1088]{2,1,0:T(8,128)S(1)} %pad_maximum_fusion.1.mine), channel_id=1, source_target_pairs={{0,1},{1,0},{2,3},{3,2},{4,5},{5,4},{6,7},{7,6},{8,9},{9,8},{10,11... | collective-permute-start | bytes 835592 | tf_op jit(solution)/shard_map/ppermute | solution.py:25
  84.9 5.4 %collective-permute-start.31 = (f32[3,16,320]{2,1,0:T(8,128)S(1)}, f32[3,16,320]{2,1,0:T(8,128)S(1)}, u32[]{:S(2)}, u32[]{:S(2)}) collective-permute-start(f32[3,16,320]{2,1,0:T(8,128)S(1)} %get-tuple-element.118), channel_id=1, source_target_pairs={{0,6},{2,4},{4,2},{6,0},{1,7},{3,5},{5,3},{7,1},{8,14},{10,12},{12... | collective-permute-start | bytes 184328 | tf_op jit(solution)/shard_map/ppermute | solution.py:21
  86.3 4.8 %collective-permute-start.30 = (f32[3,16,320]{2,1,0:T(8,128)S(1)}, f32[3,16,320]{2,1,0:T(8,128)S(1)}, u32[]{:S(2)}, u32[]{:S(2)}) collective-permute-start(f32[3,16,320]{2,1,0:T(8,128)S(1)} %get-tuple-element.119), channel_id=1, source_target_pairs={{0,4},{2,6},{4,0},{6,2},{1,5},{3,7},{5,1},{7,3},{8,12},{10,14},{12... | collective-permute-start | bytes 184328 | tf_op jit(solution)/shard_map/ppermute | solution.py:21
  91.4 4.2 %collective-permute-start.34 = (f32[16,768]{1,0:T(8,128)S(1)}, f32[16,768]{1,0:T(8,128)S(1)}, u32[]{:S(2)}, u32[]{:S(2)}) collective-permute-start(f32[16,768]{1,0:T(8,128)S(1)} %get-tuple-element.100.m0), channel_id=1, source_target_pairs={{0,24},{8,16},{16,8},{24,0},{1,25},{9,17},{17,9},{25,1},{2,26},{10... | collective-permute-start | bytes 147464 | tf_op jit(solution)/shard_map/ppermute | solution.py:21
  93.0 4.4 %collective-permute-start.33 = (f32[16,768]{1,0:T(8,128)S(1)}, f32[16,768]{1,0:T(8,128)S(1)}, u32[]{:S(2)}, u32[]{:S(2)}) collective-permute-start(f32[16,768]{1,0:T(8,128)S(1)} %get-tuple-element.100.m0), channel_id=1, source_target_pairs={{0,16},{8,24},{16,0},{24,8},{1,17},{9,25},{17,1},{25,9},{2,18},{10... | collective-permute-start | bytes 147464 | tf_op jit(solution)/shard_map/ppermute | solution.py:21
  97.6 3.9 %collective-permute-start.35 = (f32[16,448]{1,0:T(8,128)S(1)}, f32[16,448]{1,0:T(8,128)S(1)}, u32[]{:S(2)}, u32[]{:S(2)}) collective-permute-start(f32[16,448]{1,0:T(8,128)S(1)} %get-tuple-element.101), channel_id=1, source_target_pairs={{0,32},{32,0},{64,96},{96,64},{1,33},{33,1},{65,97},{97,65},{2,34}... | collective-permute-start | bytes 86024 | tf_op jit(solution)/shard_map/ppermute | solution.py:21
  97.7 4.7 %collective-permute-start.36 = (f32[16,448]{1,0:T(8,128)S(1)}, f32[16,448]{1,0:T(8,128)S(1)}, u32[]{:S(2)}, u32[]{:S(2)}) collective-permute-start(f32[16,448]{1,0:T(8,128)S(1)} %get-tuple-element.102), channel_id=1, source_target_pairs={{0,64},{32,96},{64,0},{96,32},{1,65},{33,97},{65,1},{97,33},{2,66}... | collective-permute-start | bytes 86024 | tf_op jit(solution)/shard_map/ppermute | solution.py:21
  100.7 4.0 %collective-permute-start.37 = (f32[16,448]{1,0:T(8,128)S(1)}, f32[16,448]{1,0:T(8,128)S(1)}, u32[]{:S(2)}, u32[]{:S(2)}) collective-permute-start(f32[16,448]{1,0:T(8,128)S(1)} %get-tuple-element.103), channel_id=1, source_target_pairs={{0,96},{32,64},{64,32},{96,0},{1,97},{33,65},{65,33},{97,1},{2,98}... | collective-permute-start | bytes 86024 | tf_op jit(solution)/shard_map/ppermute | solution.py:21
  104.8 4.6 %collective-permute-start.40 = (f32[16,1088]{1,0:T(8,128)S(1)}, f32[16,1088]{1,0:T(8,128)S(1)}, u32[]{:S(2)}, u32[]{:S(2)}) collective-permute-start(f32[16,1088]{1,0:T(8,128)S(1)} %get-tuple-element.106), channel_id=1, source_target_pairs={{0,6},{2,4},{4,2},{6,0},{1,7},{3,5},{5,3},{7,1},{8,14},{10,12},{12... | collective-permute-start | bytes 208904 | tf_op jit(solution)/shard_map/ppermute | solution.py:21
  106.1 4.7 %collective-permute-start.39 = (f32[16,1088]{1,0:T(8,128)S(1)}, f32[16,1088]{1,0:T(8,128)S(1)}, u32[]{:S(2)}, u32[]{:S(2)}) collective-permute-start(f32[16,1088]{1,0:T(8,128)S(1)} %get-tuple-element.106), channel_id=1, source_target_pairs={{0,4},{2,6},{4,0},{6,2},{1,5},{3,7},{5,1},{7,3},{8,12},{10,14},{12... | collective-permute-start | bytes 208904 | tf_op jit(solution)/shard_map/ppermute | solution.py:21
  111.0 8.1 %collective-permute-start.41 = (f32[4,16,1088]{2,1,0:T(8,128)S(1)}, f32[4,16,1088]{2,1,0:T(8,128)S(1)}, u32[]{:S(2)}, u32[]{:S(2)}) collective-permute-start(f32[4,16,1088]{2,1,0:T(8,128)S(1)} %pad_maximum_fusion.2.mine), channel_id=1, source_target_pairs={{0,1},{1,0},{2,3},{3,2},{4,5},{5,4},{6,7},{7,6},{8,9},{9,8},{10,11... | collective-permute-start | bytes 835592 | tf_op jit(solution)/shard_map/ppermute | solution.py:25
  (13 other events, 53.4 us)

commit v5 on v4

--- a/solution.py
+++ b/solution.py
@@ -420,19 +420,20 @@
     )
 
 
-def start_kernel(p0, p1, p2, p3, probes, grad_cov, own_chain, *refs):
+def start_kernel(p0, p1, p2, p3, probes, grad_cov, leakage, dominant, *refs):
     bx, message = refs[-2:]
     grad = ring_sum([p0[...], p1[...], p2[...], p3[...]])
     for day in range(2):
         bx[day, 0:1] = grad[day : day + 1]
         bx[day, 1:16] = probes[:, day, :]
-    dec1 = own_chain[1:2]
+    dec0, dec1 = 1.0 - leakage[0:1], 1.0 - leakage[1:2]
+    dom0, dom1 = dominant[0:1], dominant[1:2]
     ahead = bx[1] + dec1 * bx[0]
     message[:, :320] = ahead
-    message[:, 320:640] = bx[0] / own_chain[2:3] + dec1 * ahead / own_chain[3:4]
+    message[:, 320:640] = bx[0] / dom0 + dec1 * ahead / dom1
     message[:, 640:] = jnp.zeros((16, 128), F32)
     message[0:1, 640:704] = grad_cov[...]
-    put_rows(message, [own_chain[r : r + 1] for r in range(4)])
+    put_rows(message, (dec0, dec1, dom0, dom1))
 
 
 def start_stage(*operands):
@@ -440,7 +441,7 @@
         start_kernel,
         "start_stage",
         (shaped(2, 16, 320), shaped(16, 768)),
-        [VMEM_BLOCK] * 7 + [ANY_BLOCK] * (len(operands) - 7),
+        [VMEM_BLOCK] * 8 + [ANY_BLOCK] * (len(operands) - 8),
         *operands,
     )
 
@@ -753,14 +754,13 @@
     rows = lax.broadcasted_iota(jnp.int32, (2, 320, 320), 1)
     columns = lax.broadcasted_iota(jnp.int32, (2, 320, 320), 2)
     dominant = jnp.sum(jnp.where(rows == columns, square, 0.0), axis=1)
-    both = jnp.concatenate([1.0 - leakage, dominant])
 
     spread, weight, kept, sent, grad_cov, covs = setup_stage(
         obs_count.reshape(1, 2), triangles, obs_triangle, obs_bary, obs_prec, obs_value, covariates
     )
     off_pair = [split_blocks(off_blocks, "split_off", day) for day in range(2)]
     diag_pair = [split_blocks(diag_blocks, "split_diag", day) for day in range(2)]
-    bx, message = start_stage(*scattered_pieces(kept, sent), probes, grad_cov, both, off_pair[0])
+    bx, message = start_stage(*scattered_pieces(kept, sent), probes, grad_cov, leakage, dominant, off_pair[0])
     prior = prior_prec[None]
     padded_cov = jnp.pad(probes_cov, ((1, 0), (0, 0)))
 

time: 138 us -> 138 us (level)
  transfers between devices with their start and end apart: 42 -> 42, of which waited for: 24 -> 22; matrix products, arithmetic and copies ran while one was open for 2% -> 1% of each run, Pallas kernels for 12% -> 12%
where the time goes in v5:
time: 138 us
  starting transfers between devices  62.6 us (45%)
  Pallas kernels  30.1 us (22%)
  waiting for transfers between devices  27.7 us (20%)
  blocking collectives  14.7 us (11%)
  other arithmetic  1.63 us (1%)
    ppermute x36, starting transfers between devices, shift(): return lax.ppermute(value, axis, [(i, i ^ distance) for i in range(size)])  42.3 us
    pallas_call x22, Pallas kernels, call(): pl.pallas_call(kernel, grid=grid, out_shape=outs, in_specs=in_specs, out_...  30.1 us
    ppermute x36, waiting for transfers between devices, shift(): return lax.ppermute(value, axis, [(i, i ^ distance) for i in range(size)])  20.8 us
    ppermute x6, starting transfers between devices, swapped(): return lax.ppermute(value, 'blk_1', [(0, 1), (1, 0)])  20.3 us
    all_to_all x1, blocking collectives, on_device(): sums = lax.all_to_all(sums, DAY + BLK, 0, 0, tiled=True)  14.7 us
    ppermute x6, waiting for transfers between devices, swapped(): return lax.ppermute(value, 'blk_1', [(0, 1), (1, 0)])  6.87 us
  transfers between devices with their start and end apart: 42, of which 22 were waited for; matrix products, arithmetic and copies ran while one was open for 1% of the time, Pallas kernels for 12%

profile of v5, /device:TPU:1, one launch (start us, length us, event | category | flops | bytes accessed | tf_op | source)
XLA Modules:
  0.0 137.7 jit_solution(3681533568713246356)
XLA Ops:
  0.6 3.7 %setup_stage.1 = (bf16[2,2560,256]{2,1,0:T(8,128)(2,1)S(1)}, f32[2,128]{1,0:T(2,128)S(1)}, f32[4,2,320]{2,1,0:T(2,128)S(1)}, f32[4,2,320]{2,1,0:T(2,128)S(1)}, f...) custom-call(s32[1,2]{1,0:T(1,128)} %bitcast.58, s32[3,5116]{1,0:T(4,128)} %triangles.1, s32[2,128]{1,0:T(2,128)} %cells.1, ...), custom_call_target="tpu_custom_call" | custom-call | tf_op jit(solution)/shard_map/setup_stage/pallas_call | solution.py:169
  6.6 2.9 %collective-permute-start.3 = (f32[2,320]{1,0:T(2,128)S(1)}, f32[2,320]{1,0:T(2,128)S(1)}, u32[]{:S(2)}, u32[]{:S(2)}) collective-permute-start(f32[2,320]{1,0:T(2,128)S(1)} %get-tuple-element.126), channel_id=1, source_target_pairs={{0,6},{2,4},{4,2},{6,0},{1,7},{3,5},{5,3},{7,1},{8,14},{10,12},{12... | collective-permute-start | bytes 7688 | tf_op jit(solution)/shard_map/ppermute | solution.py:21
  11.7 2.0 %split_off0.1.refs_0_.o0 = bf16[640,2560]{1,0:T(8,128)(2,1)S(1)} custom-call(f32[2,320,2560]{2,1,0:T(8,128)} %source.5), custom_call_target="tpu_custom_call" | custom-call | tf_op jit(solution)/shard_map/split_off0/pallas_call | solution.py:169
  13.9 2.5 %collective-permute-start.6 = (f32[16,768]{1,0:T(8,128)S(1)}, f32[16,768]{1,0:T(8,128)S(1)}, u32[]{:S(2)}, u32[]{:S(2)}) collective-permute-start(f32[16,768]{1,0:T(8,128)S(1)} %get-tuple-element.63.m0), channel_id=1, source_target_pairs={{0,24},{8,16},{16,8},{24,0},{1,25},{9,17},{17,9},{25,1},{2,26},{10... | collective-permute-start | bytes 147464 | tf_op jit(solution)/shard_map/ppermute | solution.py:21
  17.2 2.0 %split_off1.1.refs_0_.o1 = bf16[640,2560]{1,0:T(8,128)(2,1)S(1)} custom-call(f32[2,320,2560]{2,1,0:T(8,128)} %source.5), custom_call_target="tpu_custom_call" | custom-call | tf_op jit(solution)/shard_map/split_off1/pallas_call | solution.py:169
  19.3 1.6 %collective-permute-done.5.m2 = f32[16,768]{1,0:T(8,128)S(1)} collective-permute-done((f32[16,768]{1,0:T(8,128)S(1)}, f32[16,768]{1,0:T(8,128)S(1)}, u32[]{:S(2)}, u32[]{:S(2)}) %collective-permute-start.5) | collective-permute-done | bytes 49184 | tf_op jit(solution)/shard_map/ppermute | solution.py:21
  21.2 3.8 %collective-permute-start.9 = (f32[16,768]{1,0:T(8,128)S(1)}, f32[16,768]{1,0:T(8,128)S(1)}, u32[]{:S(2)}, u32[]{:S(2)}) collective-permute-start(f32[16,768]{1,0:T(8,128)S(1)} %get-tuple-element.64.z0), channel_id=1, source_target_pairs={{0,96},{32,64},{64,32},{96,0},{1,97},{33,65},{65,33},{97,1},{2,98}... | collective-permute-start | bytes 147464 | tf_op jit(solution)/shard_map/ppermute | solution.py:21
  25.7 2.0 %split_diag0.1.refs_0_.a0 = bf16[640,2560]{1,0:T(8,128)(2,1)S(1)} custom-call(f32[2,320,2560]{2,1,0:T(8,128)} %source.7), custom_call_target="tpu_custom_call" | custom-call | tf_op jit(solution)/shard_map/split_diag0/pallas_call | solution.py:169
  27.7 1.8 %collective-permute-done.8.z2 = f32[16,768]{1,0:T(8,128)S(1)} collective-permute-done((f32[16,768]{1,0:T(8,128)S(1)}, f32[16,768]{1,0:T(8,128)S(1)}, u32[]{:S(2)}, u32[]{:S(2)}) %collective-permute-start.8) | collective-permute-done | bytes 49184 | tf_op jit(solution)/shard_map/ppermute | solution.py:21
  30.5 2.5 %collective-permute-start.12 = (f32[16,1088]{1,0:T(8,128)S(1)}, f32[16,1088]{1,0:T(8,128)S(1)}, u32[]{:S(2)}, u32[]{:S(2)}) collective-permute-start(f32[16,1088]{1,0:T(8,128)S(1)} %get-tuple-element.67), channel_id=1, source_target_pairs={{0,6},{2,4},{4,2},{6,0},{1,7},{3,5},{5,3},{7,1},{8,14},{10,12},{12... | collective-permute-start | bytes 208904 | tf_op jit(solution)/shard_map/ppermute | solution.py:21
  33.8 2.0 %split_diag1.1.a1 = bf16[640,2560]{1,0:T(8,128)(2,1)S(1)} custom-call(f32[2,320,2560]{2,1,0:T(8,128)} %source.7), custom_call_target="tpu_custom_call" | custom-call | tf_op jit(solution)/shard_map/split_diag1/pallas_call | solution.py:169
  35.8 2.2 %own_terms.2.behind.behind1 = f32[3,16,2560]{2,1,0:T(8,128)S(1)} custom-call(bf16[640,2560]{1,0:T(8,128)(2,1)S(1)} %split_diag0.1.refs_0_.a0, bf16[640,2560]{1,0:T(8,128)(2,1)S(1)} %split_diag1.1.a1, bf16[640,2560]{1,0:T(8,128)(2,1)S(1)} %split_off0.1.refs_0_.o0, bf16[640,2560]{1,0:T(8,128)(2,1)S(1)} %split_off1.1.refs_0_.o1, ...), custom_call_target="tpu_custom_call" | custom-call | tf_op jit(solution)/shard_map/own_terms/pallas_call | solution.py:169
  38.2 5.2 %collective-permute-start.13 = (f32[4,16,1088]{2,1,0:T(8,128)S(1)}, f32[4,16,1088]{2,1,0:T(8,128)S(1)}, u32[]{:S(2)}, u32[]{:S(2)}) collective-permute-start(f32[4,16,1088]{2,1,0:T(8,128)S(1)} %pad_maximum_fusion.mine), channel_id=1, source_target_pairs={{0,1},{1,0},{2,3},{3,2},{4,5},{5,4},{6,7},{7,6},{8,9},{9,8},{10,11... | collective-permute-start | bytes 835592 | tf_op jit(solution)/shard_map/ppermute | solution.py:25
  47.8 2.4 %collective-permute-start.17 = (f32[3,16,320]{2,1,0:T(8,128)S(1)}, f32[3,16,320]{2,1,0:T(8,128)S(1)}, u32[]{:S(2)}, u32[]{:S(2)}) collective-permute-start(f32[3,16,320]{2,1,0:T(8,128)S(1)} %get-tuple-element.122), channel_id=1, source_target_pairs={{0,6},{2,4},{4,2},{6,0},{1,7},{3,5},{5,3},{7,1},{8,14},{10,12},{12... | collective-permute-start | bytes 184328 | tf_op jit(solution)/shard_map/ppermute | solution.py:21
  51.2 2.0 %first_rows.1 = (f32[2,16,320]{2,1,0:T(8,128)S(1)}, f32[16,64]{1,0:T(8,128)S(1)}) custom-call(bf16[640,2560]{1,0:T(8,128)(2,1)S(1)} %split_off0.1.refs_0_.o0, bf16[640,2560]{1,0:T(8,128)(2,1)S(1)} %split_off1.1.refs_0_.o1, f32[3,16,2560]{2,1,0:T(8,128)S(1)} %get-tuple-element.76.whole.whole1, f32[2,16,320]{2,1,0:T(8,128)S(1)} %get-tuple-element.66.bx, ...), custom_call_target="tpu_custom_call" | custom-call | tf_op jit(solution)/shard_map/first_rows/pallas_call | solution.py:169
  53.2 1.7 %collective-permute-done.16.p2 = f32[3,16,320]{2,1,0:T(8,128)S(1)} collective-permute-done((f32[3,16,320]{2,1,0:T(8,128)S(1)}, f32[3,16,320]{2,1,0:T(8,128)S(1)}, u32[]{:S(2)}, u32[]{:S(2)}) %collective-permute-start.16) | collective-permute-done | bytes 61472 | tf_op jit(solution)/shard_map/ppermute | solution.py:21
  60.9 2.0 %collective-permute-start.22 = (f32[16,448]{1,0:T(8,128)S(1)}, f32[16,448]{1,0:T(8,128)S(1)}, u32[]{:S(2)}, u32[]{:S(2)}) collective-permute-start(f32[16,448]{1,0:T(8,128)S(1)} %get-tuple-element.83), channel_id=1, source_target_pairs={{0,64},{32,96},{64,0},{96,32},{1,65},{33,97},{65,1},{97,33},{2,66}... | collective-permute-start | bytes 86024 | tf_op jit(solution)/shard_map/ppermute | solution.py:21
  62.9 1.9 %collective-permute-start.23 = (f32[16,448]{1,0:T(8,128)S(1)}, f32[16,448]{1,0:T(8,128)S(1)}, u32[]{:S(2)}, u32[]{:S(2)}) collective-permute-start(f32[16,448]{1,0:T(8,128)S(1)} %get-tuple-element.84), channel_id=1, source_target_pairs={{0,96},{32,64},{64,32},{96,0},{1,97},{33,65},{65,33},{97,1},{2,98}... | collective-permute-start | bytes 86024 | tf_op jit(solution)/shard_map/ppermute | solution.py:21
  67.0 1.9 %collective-permute-start.26 = (f32[16,1088]{1,0:T(8,128)S(1)}, f32[16,1088]{1,0:T(8,128)S(1)}, u32[]{:S(2)}, u32[]{:S(2)}) collective-permute-start(f32[16,1088]{1,0:T(8,128)S(1)} %get-tuple-element.87), channel_id=1, source_target_pairs={{0,6},{2,4},{4,2},{6,0},{1,7},{3,5},{5,3},{7,1},{8,14},{10,12},{12... | collective-permute-start | bytes 208904 | tf_op jit(solution)/shard_map/ppermute | solution.py:21
  70.3 2.3 %own_terms.3.behind2 = f32[3,16,2560]{2,1,0:T(8,128)S(1)} custom-call(bf16[640,2560]{1,0:T(8,128)(2,1)S(1)} %split_diag0.1.refs_0_.a0, bf16[640,2560]{1,0:T(8,128)(2,1)S(1)} %split_diag1.1.a1, bf16[640,2560]{1,0:T(8,128)(2,1)S(1)} %split_off0.1.refs_0_.o0, bf16[640,2560]{1,0:T(8,128)(2,1)S(1)} %split_off1.1.refs_0_.o1, ...), custom_call_target="tpu_custom_call" | custom-call | tf_op jit(solution)/shard_map/own_terms/pallas_call | solution.py:169
  73.6 6.2 %collective-permute-start.27 = (f32[4,16,1088]{2,1,0:T(8,128)S(1)}, f32[4,16,1088]{2,1,0:T(8,128)S(1)}, u32[]{:S(2)}, u32[]{:S(2)}) collective-permute-start(f32[4,16,1088]{2,1,0:T(8,128)S(1)} %pad_maximum_fusion.1.mine), channel_id=1, source_target_pairs={{0,1},{1,0},{2,3},{3,2},{4,5},{5,4},{6,7},{7,6},{8,9},{9,8},{10,11... | collective-permute-start | bytes 835592 | tf_op jit(solution)/shard_map/ppermute | solution.py:25
  81.0 1.9 %second_stage.1 = (f32[4,3,16,320]{3,2,1,0:T(8,128)S(1)}, f32[4,3,16,320]{3,2,1,0:T(8,128)S(1)}, f32[16,64]{1,0:T(8,128)S(1)}, f32[3,16,2560]{2,1,0:T(8,128)S(1)...) custom-call(f32[4,16,1088]{2,1,0:T(8,128)S(1)} %pad_maximum_fusion.1.mine, ...), custom_call_target="tpu_custom_call" | custom-call | tf_op jit(solution)/shard_map/second_stage/pallas_call | solution.py:169
  84.6 1.7 %collective-permute-start.31 = (f32[3,16,320]{2,1,0:T(8,128)S(1)}, f32[3,16,320]{2,1,0:T(8,128)S(1)}, u32[]{:S(2)}, u32[]{:S(2)}) collective-permute-start(f32[3,16,320]{2,1,0:T(8,128)S(1)} %get-tuple-element.118), channel_id=1, source_target_pairs={{0,6},{2,4},{4,2},{6,0},{1,7},{3,5},{5,3},{7,1},{8,14},{10,12},{12... | collective-permute-start | bytes 184328 | tf_op jit(solution)/shard_map/ppermute | solution.py:21
  87.9 2.0 %second_rows.1 = (f32[2,16,320]{2,1,0:T(8,128)S(1)}, f32[16,64]{1,0:T(8,128)S(1)}, f32[3,16,320]{2,1,0:T(8,128)S(1)}, f32[3,16,320]{2,1,0:T(8,128)S(1)}) custom-call(bf16[640,2560]{1,0:T(8,128)(2,1)S(1)} %split_off0.1.refs_0_.o0, bf16[640,2560]{1,0:T(8,128)(2,1)S(1)} %split_off1.1.refs_0_.o1, f32[3,16,2560]{2,1,0:T(8,128)S(1)} %get-tuple-element.94.whole.z1whole, ...), custom_call_target="tpu_custom_call" | custom-call | tf_op jit(solution)/shard_map/second_rows/pallas_call | solution.py:169
  95.6 1.9 %collective-permute-done.33.m2 = f32[16,768]{1,0:T(8,128)S(1)} collective-permute-done((f32[16,768]{1,0:T(8,128)S(1)}, f32[16,768]{1,0:T(8,128)S(1)}, u32[]{:S(2)}, u32[]{:S(2)}) %collective-permute-start.33) | collective-permute-done | bytes 49184 | tf_op jit(solution)/shard_map/ppermute | solution.py:21
  97.7 3.0 %collective-permute-start.36 = (f32[16,448]{1,0:T(8,128)S(1)}, f32[16,448]{1,0:T(8,128)S(1)}, u32[]{:S(2)}, u32[]{:S(2)}) collective-permute-start(f32[16,448]{1,0:T(8,128)S(1)} %get-tuple-element.102), channel_id=1, source_target_pairs={{0,64},{32,96},{64,0},{96,32},{1,65},{33,97},{65,1},{97,33},{2,66}... | collective-permute-start | bytes 86024 | tf_op jit(solution)/shard_map/ppermute | solution.py:21
  102.3 2.3 %collective-permute-done.37.r3 = f32[16,448]{1,0:T(8,128)S(1)} collective-permute-done((f32[16,448]{1,0:T(8,128)S(1)}, f32[16,448]{1,0:T(8,128)S(1)}, u32[]{:S(2)}, u32[]{:S(2)}) %collective-permute-start.37) | collective-permute-done | bytes 28704 | tf_op jit(solution)/shard_map/ppermute | solution.py:21
  104.8 1.6 %collective-permute-start.40 = (f32[16,1088]{1,0:T(8,128)S(1)}, f32[16,1088]{1,0:T(8,128)S(1)}, u32[]{:S(2)}, u32[]{:S(2)}) collective-permute-start(f32[16,1088]{1,0:T(8,128)S(1)} %get-tuple-element.106), channel_id=1, source_target_pairs={{0,6},{2,4},{4,2},{6,0},{1,7},{3,5},{5,3},{7,1},{8,14},{10,12},{12... | collective-permute-start | bytes 208904 | tf_op jit(solution)/shard_map/ppermute | solution.py:21
  109.4 1.7 %collective-permute-done.39 = f32[16,1088]{1,0:T(8,128)S(1)} collective-permute-done((f32[16,1088]{1,0:T(8,128)S(1)}, f32[16,1088]{1,0:T(8,128)S(1)}, u32[]{:S(2)}, u32[]{:S(2)}) %collective-permute-start.39) | collective-permute-done | bytes 69664 | tf_op jit(solution)/shard_map/ppermute | solution.py:21
  111.2 6.5 %collective-permute-start.41 = (f32[4,16,1088]{2,1,0:T(8,128)S(1)}, f32[4,16,1088]{2,1,0:T(8,128)S(1)}, u32[]{:S(2)}, u32[]{:S(2)}) collective-permute-start(f32[4,16,1088]{2,1,0:T(8,128)S(1)} %pad_maximum_fusion.2.mine), channel_id=1, source_target_pairs={{0,1},{1,0},{2,3},{3,2},{4,5},{5,4},{6,7},{7,6},{8,9},{9,8},{10,11... | collective-permute-start | bytes 835592 | tf_op jit(solution)/shard_map/ppermute | solution.py:25
  118.9 3.0 %third_stage.1 = (f32[128,128]{1,0:T(8,128)S(1)}, f32[2,16,320]{2,1,0:T(8,128)S(1)}, f32[2,16,320]{2,1,0:T(8,128)S(1)}, f32[16,128]{1,0:T(8,128)S(1)}, f32[2,16,64]{2,1,0:T(8,128)S(1)}) custom-call(f32[4,16,1088]{2,1,0:T(8,128)S(1)} %pad_maximum_fusion.2.mine, f32[4,16,1088]{2,1,0:T(8,128)S(1)} %collective-permute-done.41.other, ...), custom_call_target="tpu_custom_call" | custom-call | tf_op jit(solution)/shard_map/third_stage/pallas_call | solution.py:169
  121.9 14.7 %all_to_all.11 = f32[128,1,128]{2,1,0:T(1,128)S(1)} all-to-all(f32[128,1,128]{2,1,0:T(1,128)S(1)} %bitcast.46), channel_id=1, replica_groups=mesh['day_0'=4,'day_1'=4,'blk_0'=4,'blk_1'=2] {'day_0','day_1','blk_0','..., dimensions={0} | all-to-all | bytes 131072 | tf_op jit(solution)/shard_map/all_to_all | solution.py:789
  (94 shorter events, 41.8 us)
Async XLA Ops:
  6.6 7.1 %collective-permute-start.3 = (f32[2,320]{1,0:T(2,128)S(1)}, f32[2,320]{1,0:T(2,128)S(1)}, u32[]{:S(2)}, u32[]{:S(2)}) collective-permute-start(f32[2,320]{1,0:T(2,128)S(1)} %get-tuple-element.126), channel_id=1, source_target_pairs={{0,6},{2,4},{4,2},{6,0},{1,7},{3,5},{5,3},{7,1},{8,14},{10,12},{12... | collective-permute-start | bytes 7688 | tf_op jit(solution)/shard_map/ppermute | solution.py:21
  9.5 4.2 %collective-permute-start.2 = (f32[2,320]{1,0:T(2,128)S(1)}, f32[2,320]{1,0:T(2,128)S(1)}, u32[]{:S(2)}, u32[]{:S(2)}) collective-permute-start(f32[2,320]{1,0:T(2,128)S(1)} %get-tuple-element.127), channel_id=1, source_target_pairs={{0,4},{2,6},{4,0},{6,2},{1,5},{3,7},{5,1},{7,3},{8,12},{10,14},{12... | collective-permute-start | bytes 7688 | tf_op jit(solution)/shard_map/ppermute | solution.py:21
  13.9 5.3 %collective-permute-start.6 = (f32[16,768]{1,0:T(8,128)S(1)}, f32[16,768]{1,0:T(8,128)S(1)}, u32[]{:S(2)}, u32[]{:S(2)}) collective-permute-start(f32[16,768]{1,0:T(8,128)S(1)} %get-tuple-element.63.m0), channel_id=1, source_target_pairs={{0,24},{8,16},{16,8},{24,0},{1,25},{9,17},{17,9},{25,1},{2,26},{10... | collective-permute-start | bytes 147464 | tf_op jit(solution)/shard_map/ppermute | solution.py:21
  16.4 4.4 %collective-permute-start.5 = (f32[16,768]{1,0:T(8,128)S(1)}, f32[16,768]{1,0:T(8,128)S(1)}, u32[]{:S(2)}, u32[]{:S(2)}) collective-permute-start(f32[16,768]{1,0:T(8,128)S(1)} %get-tuple-element.63.m0), channel_id=1, source_target_pairs={{0,16},{8,24},{16,0},{24,8},{1,17},{9,25},{17,1},{25,9},{2,18},{10... | collective-permute-start | bytes 147464 | tf_op jit(solution)/shard_map/ppermute | solution.py:21
  21.2 6.5 %collective-permute-start.9 = (f32[16,768]{1,0:T(8,128)S(1)}, f32[16,768]{1,0:T(8,128)S(1)}, u32[]{:S(2)}, u32[]{:S(2)}) collective-permute-start(f32[16,768]{1,0:T(8,128)S(1)} %get-tuple-element.64.z0), channel_id=1, source_target_pairs={{0,96},{32,64},{64,32},{96,0},{1,97},{33,65},{65,33},{97,1},{2,98}... | collective-permute-start | bytes 147464 | tf_op jit(solution)/shard_map/ppermute | solution.py:21
  25.0 4.5 %collective-permute-start.8 = (f32[16,768]{1,0:T(8,128)S(1)}, f32[16,768]{1,0:T(8,128)S(1)}, u32[]{:S(2)}, u32[]{:S(2)}) collective-permute-start(f32[16,768]{1,0:T(8,128)S(1)} %get-tuple-element.64.z0), channel_id=1, source_target_pairs={{0,64},{32,96},{64,0},{96,32},{1,65},{33,97},{65,1},{97,33},{2,66}... | collective-permute-start | bytes 147464 | tf_op jit(solution)/shard_map/ppermute | solution.py:21
  25.0 4.5 %collective-permute-start.7 = (f32[16,768]{1,0:T(8,128)S(1)}, f32[16,768]{1,0:T(8,128)S(1)}, u32[]{:S(2)}, u32[]{:S(2)}) collective-permute-start(f32[16,768]{1,0:T(8,128)S(1)} %get-tuple-element.64.z0), channel_id=1, source_target_pairs={{0,32},{32,0},{64,96},{96,64},{1,33},{33,1},{65,97},{97,65},{2,34}... | collective-permute-start | bytes 147464 | tf_op jit(solution)/shard_map/ppermute | solution.py:21
  30.5 7.6 %collective-permute-start.12 = (f32[16,1088]{1,0:T(8,128)S(1)}, f32[16,1088]{1,0:T(8,128)S(1)}, u32[]{:S(2)}, u32[]{:S(2)}) collective-permute-start(f32[16,1088]{1,0:T(8,128)S(1)} %get-tuple-element.67), channel_id=1, source_target_pairs={{0,6},{2,4},{4,2},{6,0},{1,7},{3,5},{5,3},{7,1},{8,14},{10,12},{12... | collective-permute-start | bytes 208904 | tf_op jit(solution)/shard_map/ppermute | solution.py:21
  33.1 5.0 %collective-permute-start.11 = (f32[16,1088]{1,0:T(8,128)S(1)}, f32[16,1088]{1,0:T(8,128)S(1)}, u32[]{:S(2)}, u32[]{:S(2)}) collective-permute-start(f32[16,1088]{1,0:T(8,128)S(1)} %get-tuple-element.67), channel_id=1, source_target_pairs={{0,4},{2,6},{4,0},{6,2},{1,5},{3,7},{5,1},{7,3},{8,12},{10,14},{12... | collective-permute-start | bytes 208904 | tf_op jit(solution)/shard_map/ppermute | solution.py:21
  33.5 4.6 %collective-permute-start.10 = (f32[16,1088]{1,0:T(8,128)S(1)}, f32[16,1088]{1,0:T(8,128)S(1)}, u32[]{:S(2)}, u32[]{:S(2)}) collective-permute-start(f32[16,1088]{1,0:T(8,128)S(1)} %get-tuple-element.67), channel_id=1, source_target_pairs={{0,2},{2,0},{4,6},{6,4},{1,3},{3,1},{5,7},{7,5},{8,10},{10,8},{12,... | collective-permute-start | bytes 208904 | tf_op jit(solution)/shard_map/ppermute | solution.py:21
  38.2 6.4 %collective-permute-start.13 = (f32[4,16,1088]{2,1,0:T(8,128)S(1)}, f32[4,16,1088]{2,1,0:T(8,128)S(1)}, u32[]{:S(2)}, u32[]{:S(2)}) collective-permute-start(f32[4,16,1088]{2,1,0:T(8,128)S(1)} %pad_maximum_fusion.mine), channel_id=1, source_target_pairs={{0,1},{1,0},{2,3},{3,2},{4,5},{5,4},{6,7},{7,6},{8,9},{9,8},{10,11... | collective-permute-start | bytes 835592 | tf_op jit(solution)/shard_map/ppermute | solution.py:25
  47.8 5.4 %collective-permute-start.17 = (f32[3,16,320]{2,1,0:T(8,128)S(1)}, f32[3,16,320]{2,1,0:T(8,128)S(1)}, u32[]{:S(2)}, u32[]{:S(2)}) collective-permute-start(f32[3,16,320]{2,1,0:T(8,128)S(1)} %get-tuple-element.122), channel_id=1, source_target_pairs={{0,6},{2,4},{4,2},{6,0},{1,7},{3,5},{5,3},{7,1},{8,14},{10,12},{12... | collective-permute-start | bytes 184328 | tf_op jit(solution)/shard_map/ppermute | solution.py:21
  50.2 4.7 %collective-permute-start.16 = (f32[3,16,320]{2,1,0:T(8,128)S(1)}, f32[3,16,320]{2,1,0:T(8,128)S(1)}, u32[]{:S(2)}, u32[]{:S(2)}) collective-permute-start(f32[3,16,320]{2,1,0:T(8,128)S(1)} %get-tuple-element.123), channel_id=1, source_target_pairs={{0,4},{2,6},{4,0},{6,2},{1,5},{3,7},{5,1},{7,3},{8,12},{10,14},{12... | collective-permute-start | bytes 184328 | tf_op jit(solution)/shard_map/ppermute | solution.py:21
  50.7 4.3 %collective-permute-start.15 = (f32[3,16,320]{2,1,0:T(8,128)S(1)}, f32[3,16,320]{2,1,0:T(8,128)S(1)}, u32[]{:S(2)}, u32[]{:S(2)}) collective-permute-start(f32[3,16,320]{2,1,0:T(8,128)S(1)} %get-tuple-element.124), channel_id=1, source_target_pairs={{0,2},{2,0},{4,6},{6,4},{1,3},{3,1},{5,7},{7,5},{8,10},{10,8},{12,... | collective-permute-start | bytes 184328 | tf_op jit(solution)/shard_map/ppermute | solution.py:21
  55.1 4.2 %collective-permute-start.20 = (f32[16,768]{1,0:T(8,128)S(1)}, f32[16,768]{1,0:T(8,128)S(1)}, u32[]{:S(2)}, u32[]{:S(2)}) collective-permute-start(f32[16,768]{1,0:T(8,128)S(1)} %get-tuple-element.81.m0), channel_id=1, source_target_pairs={{0,24},{8,16},{16,8},{24,0},{1,25},{9,17},{17,9},{25,1},{2,26},{10... | collective-permute-start | bytes 147464 | tf_op jit(solution)/shard_map/ppermute | solution.py:21
  56.2 4.4 %collective-permute-start.19 = (f32[16,768]{1,0:T(8,128)S(1)}, f32[16,768]{1,0:T(8,128)S(1)}, u32[]{:S(2)}, u32[]{:S(2)}) collective-permute-start(f32[16,768]{1,0:T(8,128)S(1)} %get-tuple-element.81.m0), channel_id=1, source_target_pairs={{0,16},{8,24},{16,0},{24,8},{1,17},{9,25},{17,1},{25,9},{2,18},{10... | collective-permute-start | bytes 147464 | tf_op jit(solution)/shard_map/ppermute | solution.py:21
  60.9 4.3 %collective-permute-start.22 = (f32[16,448]{1,0:T(8,128)S(1)}, f32[16,448]{1,0:T(8,128)S(1)}, u32[]{:S(2)}, u32[]{:S(2)}) collective-permute-start(f32[16,448]{1,0:T(8,128)S(1)} %get-tuple-element.83), channel_id=1, source_target_pairs={{0,64},{32,96},{64,0},{96,32},{1,65},{33,97},{65,1},{97,33},{2,66}... | collective-permute-start | bytes 86024 | tf_op jit(solution)/shard_map/ppermute | solution.py:21
  62.9 4.0 %collective-permute-start.23 = (f32[16,448]{1,0:T(8,128)S(1)}, f32[16,448]{1,0:T(8,128)S(1)}, u32[]{:S(2)}, u32[]{:S(2)}) collective-permute-start(f32[16,448]{1,0:T(8,128)S(1)} %get-tuple-element.84), channel_id=1, source_target_pairs={{0,96},{32,64},{64,32},{96,0},{1,97},{33,65},{65,33},{97,1},{2,98}... | collective-permute-start | bytes 86024 | tf_op jit(solution)/shard_map/ppermute | solution.py:21
  67.0 5.6 %collective-permute-start.26 = (f32[16,1088]{1,0:T(8,128)S(1)}, f32[16,1088]{1,0:T(8,128)S(1)}, u32[]{:S(2)}, u32[]{:S(2)}) collective-permute-start(f32[16,1088]{1,0:T(8,128)S(1)} %get-tuple-element.87), channel_id=1, source_target_pairs={{0,6},{2,4},{4,2},{6,0},{1,7},{3,5},{5,3},{7,1},{8,14},{10,12},{12... | collective-permute-start | bytes 208904 | tf_op jit(solution)/shard_map/ppermute | solution.py:21
  68.8 4.7 %collective-permute-start.25 = (f32[16,1088]{1,0:T(8,128)S(1)}, f32[16,1088]{1,0:T(8,128)S(1)}, u32[]{:S(2)}, u32[]{:S(2)}) collective-permute-start(f32[16,1088]{1,0:T(8,128)S(1)} %get-tuple-element.87), channel_id=1, source_target_pairs={{0,4},{2,6},{4,0},{6,2},{1,5},{3,7},{5,1},{7,3},{8,12},{10,14},{12... | collective-permute-start | bytes 208904 | tf_op jit(solution)/shard_map/ppermute | solution.py:21
  69.5 4.1 %collective-permute-start.24 = (f32[16,1088]{1,0:T(8,128)S(1)}, f32[16,1088]{1,0:T(8,128)S(1)}, u32[]{:S(2)}, u32[]{:S(2)}) collective-permute-start(f32[16,1088]{1,0:T(8,128)S(1)} %get-tuple-element.87), channel_id=1, source_target_pairs={{0,2},{2,0},{4,6},{6,4},{1,3},{3,1},{5,7},{7,5},{8,10},{10,8},{12,... | collective-permute-start | bytes 208904 | tf_op jit(solution)/shard_map/ppermute | solution.py:21
  73.6 7.4 %collective-permute-start.27 = (f32[4,16,1088]{2,1,0:T(8,128)S(1)}, f32[4,16,1088]{2,1,0:T(8,128)S(1)}, u32[]{:S(2)}, u32[]{:S(2)}) collective-permute-start(f32[4,16,1088]{2,1,0:T(8,128)S(1)} %pad_maximum_fusion.1.mine), channel_id=1, source_target_pairs={{0,1},{1,0},{2,3},{3,2},{4,5},{5,4},{6,7},{7,6},{8,9},{9,8},{10,11... | collective-permute-start | bytes 835592 | tf_op jit(solution)/shard_map/ppermute | solution.py:25
  84.6 5.4 %collective-permute-start.31 = (f32[3,16,320]{2,1,0:T(8,128)S(1)}, f32[3,16,320]{2,1,0:T(8,128)S(1)}, u32[]{:S(2)}, u32[]{:S(2)}) collective-permute-start(f32[3,16,320]{2,1,0:T(8,128)S(1)} %get-tuple-element.118), channel_id=1, source_target_pairs={{0,6},{2,4},{4,2},{6,0},{1,7},{3,5},{5,3},{7,1},{8,14},{10,12},{12... | collective-permute-start | bytes 184328 | tf_op jit(solution)/shard_map/ppermute | solution.py:21
  86.3 4.7 %collective-permute-start.30 = (f32[3,16,320]{2,1,0:T(8,128)S(1)}, f32[3,16,320]{2,1,0:T(8,128)S(1)}, u32[]{:S(2)}, u32[]{:S(2)}) collective-permute-start(f32[3,16,320]{2,1,0:T(8,128)S(1)} %get-tuple-element.119), channel_id=1, source_target_pairs={{0,4},{2,6},{4,0},{6,2},{1,5},{3,7},{5,1},{7,3},{8,12},{10,14},{12... | collective-permute-start | bytes 184328 | tf_op jit(solution)/shard_map/ppermute | solution.py:21
  91.4 4.2 %collective-permute-start.34 = (f32[16,768]{1,0:T(8,128)S(1)}, f32[16,768]{1,0:T(8,128)S(1)}, u32[]{:S(2)}, u32[]{:S(2)}) collective-permute-start(f32[16,768]{1,0:T(8,128)S(1)} %get-tuple-element.100.m0), channel_id=1, source_target_pairs={{0,24},{8,16},{16,8},{24,0},{1,25},{9,17},{17,9},{25,1},{2,26},{10... | collective-permute-start | bytes 147464 | tf_op jit(solution)/shard_map/ppermute | solution.py:21
  93.0 4.4 %collective-permute-start.33 = (f32[16,768]{1,0:T(8,128)S(1)}, f32[16,768]{1,0:T(8,128)S(1)}, u32[]{:S(2)}, u32[]{:S(2)}) collective-permute-start(f32[16,768]{1,0:T(8,128)S(1)} %get-tuple-element.100.m0), channel_id=1, source_target_pairs={{0,16},{8,24},{16,0},{24,8},{1,17},{9,25},{17,1},{25,9},{2,18},{10... | collective-permute-start | bytes 147464 | tf_op jit(solution)/shard_map/ppermute | solution.py:21
  97.6 3.9 %collective-permute-start.35 = (f32[16,448]{1,0:T(8,128)S(1)}, f32[16,448]{1,0:T(8,128)S(1)}, u32[]{:S(2)}, u32[]{:S(2)}) collective-permute-start(f32[16,448]{1,0:T(8,128)S(1)} %get-tuple-element.101), channel_id=1, source_target_pairs={{0,32},{32,0},{64,96},{96,64},{1,33},{33,1},{65,97},{97,65},{2,34}... | collective-permute-start | bytes 86024 | tf_op jit(solution)/shard_map/ppermute | solution.py:21
  97.7 4.7 %collective-permute-start.36 = (f32[16,448]{1,0:T(8,128)S(1)}, f32[16,448]{1,0:T(8,128)S(1)}, u32[]{:S(2)}, u32[]{:S(2)}) collective-permute-start(f32[16,448]{1,0:T(8,128)S(1)} %get-tuple-element.102), channel_id=1, source_target_pairs={{0,64},{32,96},{64,0},{96,32},{1,65},{33,97},{65,1},{97,33},{2,66}... | collective-permute-start | bytes 86024 | tf_op jit(solution)/shard_map/ppermute | solution.py:21
  100.7 4.0 %collective-permute-start.37 = (f32[16,448]{1,0:T(8,128)S(1)}, f32[16,448]{1,0:T(8,128)S(1)}, u32[]{:S(2)}, u32[]{:S(2)}) collective-permute-start(f32[16,448]{1,0:T(8,128)S(1)} %get-tuple-element.103), channel_id=1, source_target_pairs={{0,96},{32,64},{64,32},{96,0},{1,97},{33,65},{65,33},{97,1},{2,98}... | collective-permute-start | bytes 86024 | tf_op jit(solution)/shard_map/ppermute | solution.py:21
  104.8 4.6 %collective-permute-start.40 = (f32[16,1088]{1,0:T(8,128)S(1)}, f32[16,1088]{1,0:T(8,128)S(1)}, u32[]{:S(2)}, u32[]{:S(2)}) collective-permute-start(f32[16,1088]{1,0:T(8,128)S(1)} %get-tuple-element.106), channel_id=1, source_target_pairs={{0,6},{2,4},{4,2},{6,0},{1,7},{3,5},{5,3},{7,1},{8,14},{10,12},{12... | collective-permute-start | bytes 208904 | tf_op jit(solution)/shard_map/ppermute | solution.py:21
  106.4 4.7 %collective-permute-start.39 = (f32[16,1088]{1,0:T(8,128)S(1)}, f32[16,1088]{1,0:T(8,128)S(1)}, u32[]{:S(2)}, u32[]{:S(2)}) collective-permute-start(f32[16,1088]{1,0:T(8,128)S(1)} %get-tuple-element.106), channel_id=1, source_target_pairs={{0,4},{2,6},{4,0},{6,2},{1,5},{3,7},{5,1},{7,3},{8,12},{10,14},{12... | collective-permute-start | bytes 208904 | tf_op jit(solution)/shard_map/ppermute | solution.py:21
  111.2 7.7 %collective-permute-start.41 = (f32[4,16,1088]{2,1,0:T(8,128)S(1)}, f32[4,16,1088]{2,1,0:T(8,128)S(1)}, u32[]{:S(2)}, u32[]{:S(2)}) collective-permute-start(f32[4,16,1088]{2,1,0:T(8,128)S(1)} %pad_maximum_fusion.2.mine), channel_id=1, source_target_pairs={{0,1},{1,0},{2,3},{3,2},{4,5},{5,4},{6,7},{7,6},{8,9},{9,8},{10,11... | collective-permute-start | bytes 835592 | tf_op jit(solution)/shard_map/ppermute | solution.py:25
  (14 other events, 54.3 us)
